TPU v7x, 256 devices: a whole 4x4x8 slice. The times are simulated.
256 devices in a mesh: src: 2 (over z_hi), gx: 8 (over z_lo, core), gy: 16 (over y, x).
Axes of the slice: x: 4, y: 4, z: 8 (z_hi: 2, z_lo: 4; z = z_hi * 4 + z_lo), core: 2. Of those that a mesh axis runs over, the one named last changes fastest.
Arguments:
- forward_state: float32 [4, 6, 128, 65536], P('src', None, 'gx', 'gy'), may hold values from -6 to 6
- adjoint_state: float32 [4, 6, 128, 65536], P('src', None, 'gx', 'gy'), may hold values from -6 to 6
- permittivity: float32 [128, 65536], P('gx', 'gy'), may hold values from 1 to 3
- waveform: float32 [4, 4], P('src'), may hold values from -8 to 8
- source_cell: int32 [4, 3], P('src'), may hold values from 0 to 1023, as said below
- block_owner: int32 [32, 256], P('gx', 'gy'), may hold values from -1 to 15, as said below
- block_slot: int32 [32, 256], P('gx', 'gy'), may hold values from -1 to 3, as said below
- owner_rows: int32 [128, 64], P(('gx', 'gy')), may hold values from 0 to 63, as said below
Outputs:
- design_gradient: float32 [8192, 1024], P(('gx', 'gy'), 'src')
Inputs may be any that keep to these rules, and one draw needn't show every extreme that they name: `block_owner`: -1 marks a block outside the design region; otherwise the owner lies in the block's own gx row. The design blocks of one device that go to one owner number at most 4, and some device sends exactly 4 to some owner. `block_slot`: -1 exactly where block_owner is -1; the blocks that one device sends to one owner have distinct slots. `owner_rows`: each row is a permutation of 0 to 63. `source_cell`: each row is a cell (x, y, z) of the grid.
All inputs are finite; a program needn't handle non-finite values.
Results may differ from a plain program's by a relative error of at most 0.0003.
Values sent between devices are 32-bit elements; how exact they have to be, the bound alone decides.
No kernel may reach another device: no remote copies, remote signals or barrier semaphores. Data moves between devices by JAX's collectives and lax.ppermute only.
A program may use at most 128 MiB of HBM per device.

v0:
```python
import jax
import jax.numpy as jnp
from jax import lax
from jax.sharding import PartitionSpec as P

NZ = 64
STEPS = 4
BX = 4
BY = 4


courant = 0.55


def passed_along(shard, axis, by):
    count = lax.axis_size(axis)
    pairs = [(i, i + by) for i in range(count) if 0 <= i + by < count]
    return lax.ppermute(shard, axis, pairs)


def upper_z(values, z_cells):
    zindex = lax.broadcasted_iota(jnp.int32, values.shape, values.ndim - 1) % z_cells
    shifted = jnp.concatenate([values[..., 1:], jnp.zeros_like(values[..., :1])], axis=-1)
    return jnp.where(zindex == z_cells - 1, jnp.zeros_like(shifted), shifted)


def lower_z(values, z_cells):
    zindex = lax.broadcasted_iota(jnp.int32, values.shape, values.ndim - 1) % z_cells
    shifted = jnp.concatenate([jnp.zeros_like(values[..., :1]), values[..., :-1]], axis=-1)
    return jnp.where(zindex == 0, jnp.zeros_like(shifted), shifted)


def upper_x(values, ghosts):
    return jnp.concatenate([values[..., 1:, :], ghosts], axis=-2)


def lower_x(values, ghosts):
    return jnp.concatenate([ghosts, values[..., :-1, :]], axis=-2)


def upper_y(values, ghosts, z_cells):
    return jnp.concatenate([values[..., z_cells:], ghosts], axis=-1)


def lower_y(values, ghosts, z_cells):
    return jnp.concatenate([ghosts, values[..., :-z_cells]], axis=-1)


def magnetic_update(electric, magnetic, ghost_x, ghost_y, z_cells):
    new_hx = magnetic[0] - courant * (
        upper_y(electric[2], ghost_y[1], z_cells)
        - electric[2]
        - (upper_z(electric[1], z_cells) - electric[1])
    )
    new_hy = magnetic[1] - courant * (
        upper_z(electric[0], z_cells)
        - electric[0]
        - (upper_x(electric[2], ghost_x[1]) - electric[2])
    )
    new_hz = magnetic[2] - courant * (
        upper_x(electric[1], ghost_x[0])
        - electric[1]
        - (upper_y(electric[0], ghost_y[0], z_cells) - electric[0])
    )
    return (new_hx, new_hy, new_hz)


def electric_update(electric, magnetic, ghost_x, ghost_y, factor, z_cells):
    new_ex = electric[0] + factor * (
        magnetic[2]
        - lower_y(magnetic[2], ghost_y[1], z_cells)
        - (magnetic[1] - lower_z(magnetic[1], z_cells))
    )
    new_ey = electric[1] + factor * (
        magnetic[0]
        - lower_z(magnetic[0], z_cells)
        - (magnetic[2] - lower_x(magnetic[2], ghost_x[1]))
    )
    new_ez = electric[2] + factor * (
        magnetic[1]
        - lower_x(magnetic[1], ghost_x[0])
        - (magnetic[0] - lower_y(magnetic[0], ghost_y[0], z_cells))
    )
    return (new_ex, new_ey, new_ez)


def upper_ghosts(electric, z_cells):
    planes = jnp.stack([electric[1][:, :1, :], electric[2][:, :1, :]], axis=1)
    planes = passed_along(planes, "gx", -1)
    strips = jnp.stack([electric[0][..., :z_cells], electric[2][..., :z_cells]], axis=1)
    flat_strips = passed_along(strips.reshape(strips.shape[0], 2, -1), "gy", -1)
    strips = flat_strips.reshape(strips.shape)
    return ((planes[:, 0], planes[:, 1]), (strips[:, 0], strips[:, 1]))


def lower_ghosts(magnetic, z_cells):
    planes = jnp.stack([magnetic[1][:, -1:, :], magnetic[2][:, -1:, :]], axis=1)
    planes = passed_along(planes, "gx", 1)
    strips = jnp.stack([magnetic[0][..., -z_cells:], magnetic[2][..., -z_cells:]], axis=1)
    flat_strips = passed_along(strips.reshape(strips.shape[0], 2, -1), "gy", 1)
    strips = flat_strips.reshape(strips.shape)
    return ((planes[:, 0], planes[:, 1]), (strips[:, 0], strips[:, 1]))


def advance(electric, magnetic, factor, z_cells):
    ghost_x, ghost_y = upper_ghosts(electric, z_cells)
    magnetic = magnetic_update(electric, magnetic, ghost_x, ghost_y, z_cells)
    ghost_x, ghost_y = lower_ghosts(magnetic, z_cells)
    electric = electric_update(electric, magnetic, ghost_x, ghost_y, factor, z_cells)
    return (electric, magnetic)


def per_device(
    forward_state,
    adjoint_state,
    permittivity,
    waveform,
    source_cell,
    block_owner,
    block_slot,
    owner_rows,
):
    cells_x = permittivity.shape[0]
    cells_yz = permittivity.shape[1]
    cells_y = cells_yz // NZ
    factor = courant / permittivity
    x_index = lax.broadcasted_iota(jnp.int32, (cells_x, cells_yz), 0)
    yz_index = lax.broadcasted_iota(jnp.int32, (cells_x, cells_yz), 1)
    local_x = source_cell[:, 0] - lax.axis_index("gx") * cells_x
    local_yz = (source_cell[:, 1] - lax.axis_index("gy") * cells_y) * NZ + source_cell[:, 2]
    beacon = (
        (x_index[None] == local_x[:, None, None]) & (yz_index[None] == local_yz[:, None, None])
    ).astype(jnp.float32)
    density = jnp.zeros((cells_x, cells_yz), jnp.float32)
    electric = (forward_state[:, 0], forward_state[:, 1], forward_state[:, 2])
    magnetic = (forward_state[:, 3], forward_state[:, 4], forward_state[:, 5])
    increments = []
    for step_index in range(STEPS):
        updated, magnetic = advance(electric, magnetic, factor, NZ)
        updated = (
            updated[0],
            updated[1],
            updated[2] + waveform[:, step_index][:, None, None] * beacon,
        )
        increments.append(
            (updated[0] - electric[0], updated[1] - electric[1], updated[2] - electric[2])
        )
        electric = updated
    electric = (adjoint_state[:, 0], adjoint_state[:, 1], adjoint_state[:, 2])
    magnetic = (adjoint_state[:, 3], adjoint_state[:, 4], adjoint_state[:, 5])
    for step_index in range(STEPS):
        electric, magnetic = advance(electric, magnetic, factor, NZ)
        paired = increments[STEPS - 1 - step_index]
        intersection = electric[0] * paired[0] + electric[1] * paired[1] + electric[2] * paired[2]
        density = density + jnp.sum(intersection, axis=0)
    gradient = -density / permittivity
    blocks = (
        gradient.reshape(cells_x // BX, BX, cells_y // BY, BY, NZ)
        .transpose(0, 2, 1, 3, 4)
        .reshape(-1, BX * BY * NZ)
    )
    owners = block_owner.reshape(-1)
    slots = block_slot.reshape(-1)
    peers = lax.axis_size("gy")
    capacity = max(2, (blocks.shape[0] + peers - 1) // peers)
    rows_owned = peers * capacity
    destination = jnp.where(owners >= 0, owners * capacity + slots, rows_owned)
    outgoing = (
        jnp.zeros((rows_owned, blocks.shape[1]), jnp.float32)
        .at[destination]
        .set(blocks, mode="drop")
    )
    sectioned = outgoing.reshape(peers, capacity, 1, -1)
    arrived = lax.all_to_all(
        lax.all_to_all(sectioned, "src", split_axis=3, concat_axis=2, tiled=True),
        "gy",
        split_axis=0,
        concat_axis=0,
        tiled=True,
    )
    arrived = jnp.sum(arrived, axis=2)
    placed = jnp.zeros((rows_owned, arrived.shape[-1]), jnp.float32)
    return placed.at[owner_rows[0]].set(arrived.reshape(rows_owned, -1))


def solution(mesh):
    in_specs = (
        P("src", None, "gx", "gy"),
        P("src", None, "gx", "gy"),
        P("gx", "gy"),
        P("src", None),
        P("src", None),
        P("gx", "gy"),
        P("gx", "gy"),
        P(("gx", "gy"), None),
    )
    out_specs = P(("gx", "gy"), "src")
    return jax.shard_map(
        per_device, mesh=mesh, in_specs=in_specs, out_specs=out_specs, check_vma=False
    )
```

profile of v0, /device:TPU:32, one launch (start us, length us, event | category | flops | bytes accessed | tf_op | source)
XLA Modules:
  0.0 353.1 jit_solution(7784408515119125524)
XLA Ops:
  0.0 1.5 slice_bitcast_fusion.2
  2.3 1.9 collective-permute-start.3
  5.7 1.5 slice_bitcast_fusion.5
  7.9 3.8 %collective-permute-start = (f32[2,2,1,4096]{3,1,2,0:T(2,128)}, f32[2,2,1,4096]{3,1,2,0:T(2,128)}, u32[]{:S(2)}, u32[]{:S(2)}) collective-permute-start(f32[2,2,1,4096]{3,1,2,0:T(2,128)} %pad_maximum_fusion), channel_id=1, source_target_pairs={{16,0},{32,16},{48,32},{64,48},{80,64},{96,80},{112,96},{17,1},{33... | collective-permute-start | bytes 196616 | tf_op jit(solution)/shard_map/ppermute | solution.py:18
  28.9 1.8 fusion.173
  32.5 1.5 fusion.170
  36.8 5.5 %collective-permute-start.5 = (f32[2,2,1024]{2,0,1:T(2,128)}, f32[2,2,1024]{2,0,1:T(2,128)}, u32[]{:S(2)}, u32[]{:S(2)}) collective-permute-start(f32[2,2,1024]{2,0,1:T(2,128)} %pad_maximum_fusion.19), channel_id=1, source_target_pairs={{0,1},{1,2},{2,3},{3,4},{4,5},{5,6},{6,7},{7,8},{8,9},{9,10},{10,1... | collective-permute-start | bytes 49160 | tf_op jit(solution)/shard_map/ppermute | solution.py:18
  43.0 1.9 collective-permute-start.6
  45.0 2.7 fusion.102
  48.5 2.3 collective-permute-start.18
  51.8 3.3 collective-permute-start.2
  59.7 1.7 fusion.43
  69.6 2.4 collective-permute-start.7
  72.1 1.8 collective-permute-done.7
  74.0 2.5 fusion.118
  77.7 4.5 %collective-permute-start.9 = (f32[2,2,1024]{2,0,1:T(2,128)S(1)}, f32[2,2,1024]{2,0,1:T(2,128)S(1)}, u32[]{:S(2)}, u32[]{:S(2)}) collective-permute-start(f32[2,2,1024]{2,0,1:T(2,128)S(1)} %pad_maximum_fusion.21), channel_id=1, source_target_pairs={{0,1},{1,2},{2,3},{3,4},{4,5},{5,6},{6,7},{7,8},{8,9},{9,10},{10,1... | collective-permute-start | bytes 49160 | tf_op jit(solution)/shard_map/ppermute | solution.py:18
  82.4 3.5 collective-permute-start.10
  86.0 2.0 collective-permute-done.10
  88.1 1.5 fusion.184
  97.7 1.5 pad_maximum_fusion.5
  105.0 1.9 collective-permute-start.11
  110.1 3.6 %fusion.126 = (f32[2,16,4096]{2,1,0:T(8,128)S(1)}, f32[2,16,4096]{2,1,0:T(8,128)}, f32[2,16,4096]{2,1,0:T(8,128)S(1)}) fusion(f32[2,16,4096]{2,1,0:T(8,128)} %copy-done.9, f32[2,16,4096]{2,1,0:T(8,128)S(1)} %get-tuple-element.36, f32[2,16,4096]{2,1,0:T(8,128)S(1)} %fusion.184, f32[2,16,64]{2,1,0:T(8,128)S(1)} %get-tuple-element.110, ...), kind=kLoop, calls=%fused_computation.132 | loop fusion | flops 3014656 | bytes 7900928 | tf_op jit(solution)/shard_map/sub | solution.py:50
  114.9 5.1 %collective-permute-start.13 = (f32[2,2,1024]{2,0,1:T(2,128)S(1)}, f32[2,2,1024]{2,0,1:T(2,128)S(1)}, u32[]{:S(2)}, u32[]{:S(2)}) collective-permute-start(f32[2,2,1024]{2,0,1:T(2,128)S(1)} %pad_maximum_fusion.23), channel_id=1, source_target_pairs={{0,1},{1,2},{2,3},{3,4},{4,5},{5,6},{6,7},{7,8},{8,9},{9,10},{10,1... | collective-permute-start | bytes 49160 | tf_op jit(solution)/shard_map/ppermute | solution.py:18
  121.1 3.7 %collective-permute-start.14 = (f32[2,2,1,4096]{3,1,2,0:T(2,128)S(1)}, f32[2,2,1,4096]{3,1,2,0:T(2,128)S(1)}, u32[]{:S(2)}, u32[]{:S(2)}) collective-permute-start(f32[2,2,1,4096]{3,1,2,0:T(2,128)S(1)} %pad_maximum_fusion.6), channel_id=1, source_target_pairs={{0,16},{16,32},{32,48},{48,64},{64,80},{80,96},{96,112},{1,17},{17... | collective-permute-start | bytes 196616 | tf_op jit(solution)/shard_map/ppermute | solution.py:18
  125.0 1.8 collective-permute-done.14
  126.8 1.8 fusion.191
  129.3 2.3 fusion.59
  136.5 1.5 collective-permute-start.16
  145.2 1.9 collective-permute-start.15
  150.3 3.0 fusion.134
  158.9 5.4 %collective-permute-start.17 = (f32[2,2,1024]{2,0,1:T(2,128)S(1)}, f32[2,2,1024]{2,0,1:T(2,128)}, u32[]{:S(2)}, u32[]{:S(2)}) collective-permute-start(f32[2,2,1024]{2,0,1:T(2,128)S(1)} %pad_maximum_fusion.25), channel_id=1, source_target_pairs={{0,1},{1,2},{2,3},{3,4},{4,5},{5,6},{6,7},{7,8},{8,9},{9,10},{10,1... | collective-permute-start | bytes 49160 | tf_op jit(solution)/shard_map/ppermute | solution.py:18
  165.8 3.7 %collective-permute-start.19 = (f32[2,2,1,4096]{3,1,2,0:T(2,128)}, f32[2,2,1,4096]{3,1,2,0:T(2,128)}, u32[]{:S(2)}, u32[]{:S(2)}) collective-permute-start(f32[2,2,1,4096]{3,1,2,0:T(2,128)} %pad_maximum_fusion.9), channel_id=1, source_target_pairs={{0,16},{16,32},{32,48},{48,64},{64,80},{80,96},{96,112},{1,17},{17... | collective-permute-start | bytes 196616 | tf_op jit(solution)/shard_map/ppermute | solution.py:18
  172.7 6.4 %fusion.166 = (f32[16,4096]{1,0:T(8,128)}, f32[2,16,4096]{2,1,0:T(8,128)S(1)}, f32[2,16,4096]{2,1,0:T(8,128)S(1)}, f32[2,16,4096]{2,1,0:T(8,128)S(1)}) fusion(f32[2,16,4096]{2,1,0:T(8,128)} %get-tuple-element.35, f32[2,16,4096]{2,1,0:T(8,128)} %copy-done.48, f32[2,16,4096]{2,1,0:T(8,128)S(1)} %get-tuple-element.34, f32[2,16,4096]{2,1,0:T(8,128)} %copy-done.50, ...), kind=kLoop, calls=%fused_computation.172 | loop fusion | flops 7536640 | bytes 14716440 | tf_op jit(solution)/shard_map/reduce_sum | solution.py:155
  182.5 1.9 slice.1112
  184.4 2.0 slice.1116
  186.5 2.0 slice.1120
  191.4 1.9 collective-permute-start.20
  195.6 4.1 %fusion.142 = (f32[2,16,4096]{2,1,0:T(8,128)S(1)}, f32[2,16,4096]{2,1,0:T(8,128)}, f32[2,16,4096]{2,1,0:T(8,128)S(1)}) fusion(f32[2,16,4096]{2,1,0:T(8,128)} %copy-done.37, f32[2,16,4096]{2,1,0:T(8,128)} %copy-done.33, f32[2,16,4096]{2,1,0:T(8,128)} %copy-done.20, f32[2,16,64]{2,1,0:T(8,128)S(1)} %get-tuple-element.98, f32[2,16,4032]{2,1,0:T(8,128)} %slice.1120, ...), kind=kLoop, calls=%fused_computation.148 | loop fusion | flops 3014656 | bytes 7900928 | tf_op jit(solution)/shard_map/sub | solution.py:50
  200.9 6.7 %collective-permute-start.22 = (f32[2,2,1024]{2,0,1:T(2,128)S(1)}, f32[2,2,1024]{2,0,1:T(2,128)}, u32[]{:S(2)}, u32[]{:S(2)}) collective-permute-start(f32[2,2,1024]{2,0,1:T(2,128)S(1)} %pad_maximum_fusion.27), channel_id=1, source_target_pairs={{0,1},{1,2},{2,3},{3,4},{4,5},{5,6},{6,7},{7,8},{8,9},{9,10},{10,1... | collective-permute-start | bytes 49160 | tf_op jit(solution)/shard_map/ppermute | solution.py:18
  209.3 3.6 %collective-permute-start.23 = (f32[2,2,1,4096]{3,1,2,0:T(2,128)}, f32[2,2,1,4096]{3,1,2,0:T(2,128)S(1)}, u32[]{:S(2)}, u32[]{:S(2)}) collective-permute-start(f32[2,2,1,4096]{3,1,2,0:T(2,128)} %pad_maximum_fusion.11), channel_id=1, source_target_pairs={{0,16},{16,32},{32,48},{48,64},{64,80},{80,96},{96,112},{1,17},{17... | collective-permute-start | bytes 196616 | tf_op jit(solution)/shard_map/ppermute | solution.py:18
  215.1 1.9 fusion.209
  221.7 1.9 slice.1140
  223.6 2.0 slice.1144
  225.6 2.0 slice.1150
  230.6 1.9 collective-permute-start.24
  234.8 4.1 %fusion.150 = (f32[2,16,4096]{2,1,0:T(8,128)S(1)}, f32[2,16,4096]{2,1,0:T(8,128)}, f32[2,16,4096]{2,1,0:T(8,128)S(1)}) fusion(f32[2,16,4096]{2,1,0:T(8,128)} %copy-done.7, f32[2,16,4096]{2,1,0:T(8,128)} %copy-done.36, f32[2,16,4096]{2,1,0:T(8,128)} %copy-done.18, f32[2,16,64]{2,1,0:T(8,128)S(1)} %get-tuple-element.94, f32[2,16,4032]{2,1,0:T(8,128)} %slice.1148, ...), kind=kLoop, calls=%fused_computation.156 | loop fusion | flops 3014656 | bytes 7900928 | tf_op jit(solution)/shard_map/sub | solution.py:50
  240.1 6.7 %collective-permute-start.26 = (f32[2,2,1024]{2,0,1:T(2,128)S(1)}, f32[2,2,1024]{2,0,1:T(2,128)}, u32[]{:S(2)}, u32[]{:S(2)}) collective-permute-start(f32[2,2,1024]{2,0,1:T(2,128)S(1)} %pad_maximum_fusion.29), channel_id=1, source_target_pairs={{0,1},{1,2},{2,3},{3,4},{4,5},{5,6},{6,7},{7,8},{8,9},{9,10},{10,1... | collective-permute-start | bytes 49160 | tf_op jit(solution)/shard_map/ppermute | solution.py:18
  248.5 3.6 %collective-permute-start.27 = (f32[2,2,1,4096]{3,1,2,0:T(2,128)}, f32[2,2,1,4096]{3,1,2,0:T(2,128)S(1)}, u32[]{:S(2)}, u32[]{:S(2)}) collective-permute-start(f32[2,2,1,4096]{3,1,2,0:T(2,128)} %pad_maximum_fusion.13), channel_id=1, source_target_pairs={{0,16},{16,32},{32,48},{48,64},{64,80},{80,96},{96,112},{1,17},{17... | collective-permute-start | bytes 196616 | tf_op jit(solution)/shard_map/ppermute | solution.py:18
  254.3 5.4 %add_reduce_fusion.1 = (f32[16,4096]{1,0:T(8,128)}, f32[16,4096]{1,0:T(8,128)}, f32[2,16,4096]{2,1,0:T(8,128)S(1)}, f32[2,16,4096]{2,1,0:T(8,128)S(1)}, f32[2,16,4096]{2,1,0:T(8,128)S(1)}) fusion(f32[2,16,4096]{2,1,0:T(8,128)} %copy-done.18, f32[2,16,4096]{2,1,0:T(8,128)S(1)} %fusion.191, f32[2,16,4096]{2,1,0:T(8,128)S(1)} %fusion.184, ...), kind=kLoop, calls=%fused_computation.295 | loop fusion | flops 5242880 | bytes 13405952 | tf_op jit(solution)/shard_map/reduce_sum | solution.py:155
  262.5 2.0 slice.1168
  264.5 2.0 slice.1172
  266.5 2.0 slice.1176
  271.4 1.9 collective-permute-start.28
  276.2 2.8 fusion.158
  280.4 6.1 %collective-permute-start.30 = (f32[2,2,1024]{2,0,1:T(2,128)S(1)}, f32[2,2,1024]{2,0,1:T(2,128)S(1)}, u32[]{:S(2)}, u32[]{:S(2)}) collective-permute-start(f32[2,2,1024]{2,0,1:T(2,128)S(1)} %pad_maximum_fusion.31), channel_id=1, source_target_pairs={{0,1},{1,2},{2,3},{3,4},{4,5},{5,6},{6,7},{7,8},{8,9},{9,10},{10,1... | collective-permute-start | bytes 49160 | tf_op jit(solution)/shard_map/ppermute | solution.py:18
  286.6 4.0 %collective-permute-start.31 = (f32[2,2,1,4096]{3,1,2,0:T(2,128)S(1)}, f32[2,2,1,4096]{3,1,2,0:T(2,128)S(1)}, u32[]{:S(2)}, u32[]{:S(2)}) collective-permute-start(f32[2,2,1,4096]{3,1,2,0:T(2,128)S(1)} %pad_maximum_fusion.15), channel_id=1, source_target_pairs={{0,16},{16,32},{32,48},{48,64},{64,80},{80,96},{96,112},{1,17},{17... | collective-permute-start | bytes 196616 | tf_op jit(solution)/shard_map/ppermute | solution.py:18
  292.2 4.2 %fusion.93 = f32[16,4096]{1,0:T(8,128)S(1)} fusion(f32[2,16,4096]{2,1,0:T(8,128)} %copy-done.39, f32[2,16,4096]{2,1,0:T(8,128)} %copy-done.49, f32[2,16,4096]{2,1,0:T(8,128)} %copy-done.31, f32[2,16,4096]{2,1,0:T(8,128)} %copy-done.51, f32[2,16,4096]{2,1,0:T(8,128)} %copy-done.47, f32[2,16,4032]{2,1,0:T(8,128)} %bitcast.413, ...), kind=kLoop, calls=%fused_computation.99 | loop fusion | flops 4128768 | bytes 9998080 | tf_op jit(solution)/shard_map/reduce_sum | solution.py:155
  298.6 1.7 copy.85
  300.3 2.9 reshape.295
  303.2 17.4 %all_to_all.17 = f32[2,1,32768]{2,1,0:T(1,128)S(1)} all-to-all(f32[2,1,32768]{2,1,0:T(1,128)S(1)} %reshape.295), channel_id=1, replica_groups=mesh['src'=2,'gx'=8,'gy'=16] {'src'}, dimensions={0} | all-to-all | bytes 524288 | tf_op jit(solution)/shard_map/all_to_all | solution.py:175
  322.6 2.8 reshape.296
  325.4 2.5 copy.86
  327.9 15.0 %all-to-all-start.1 = ((f32[16,4,2,512]{3,1,2,0:T(4,128)}), f32[16,4,2,512]{3,1,2,0:T(4,128)S(1)}, u32[]{:S(2)}, u32[]{:S(2)}) async-start(f32[16,4,2,512]{3,1,2,0:T(4,128)} %copy.86), calls=%async_computation.1 | async-start | bytes 524288 | tf_op jit(solution)/shard_map/all_to_all | solution.py:174
  342.9 8.7 %all-to-all-done.1 = f32[16,4,2,512]{3,1,2,0:T(4,128)S(1)} async-done(((f32[16,4,2,512]{3,1,2,0:T(4,128)}), f32[16,4,2,512]{3,1,2,0:T(4,128)S(1)}, u32[]{:S(2)}, u32[]{:S(2)}) %all-to-all-start.1) | async-done | bytes 262176 | tf_op jit(solution)/shard_map/all_to_all | solution.py:174
  (419 shorter events, 132.6 us)
Async XLA Ops:
  0.0 14.2 %copy-start.63 = (f32[2,4]{1,0:T(2,128)S(1)}, f32[2,4]{1,0:T(2,128)}, u32[]{:S(2)}) copy-start(f32[2,4]{1,0:T(2,128)} %param.11) | copy-start | bytes 100
  0.0 15.1 %copy-start.68 = (s32[4,16]{1,0:T(4,128)S(1)}, s32[4,16]{1,0:T(4,128)}, u32[]{:S(2)}) copy-start(s32[4,16]{1,0:T(4,128)} %param.13) | copy-start | bytes 772
  0.0 15.1 %copy-start.67 = (s32[4,16]{1,0:T(4,128)S(1)}, s32[4,16]{1,0:T(4,128)}, u32[]{:S(2)}) copy-start(s32[4,16]{1,0:T(4,128)} %param.14) | copy-start | bytes 772
  0.0 15.8 %copy-start.66 = (s32[2,3]{1,0:T(2,128)S(1)}, s32[2,3]{1,0:T(2,128)}, u32[]{:S(2)}) copy-start(s32[2,3]{1,0:T(2,128)} %param.12) | copy-start | bytes 76
  2.3 25.6 %collective-permute-start.3 = (f32[2,2,1,4096]{3,1,2,0:T(2,128)}, f32[2,2,1,4096]{3,1,2,0:T(2,128)}, u32[]{:S(2)}, u32[]{:S(2)}) collective-permute-start(f32[2,2,1,4096]{3,1,2,0:T(2,128)} %pad_maximum_fusion.1), channel_id=1, source_target_pairs={{16,0},{32,16},{48,32},{64,48},{80,64},{96,80},{112,96},{17,1},{33... | collective-permute-start | bytes 196616 | tf_op jit(solution)/shard_map/ppermute | solution.py:18
  4.4 22.1 %collective-permute-start.4 = (f32[2,2,1024]{2,0,1:T(2,128)S(1)}, f32[2,2,1024]{2,0,1:T(2,128)S(1)}, u32[]{:S(2)}, u32[]{:S(2)}) collective-permute-start(f32[2,2,1024]{2,0,1:T(2,128)S(1)} %pad_maximum_fusion.18), channel_id=1, source_target_pairs={{1,0},{2,1},{3,2},{4,3},{5,4},{6,5},{7,6},{8,7},{9,8},{10,9},{11,1... | collective-permute-start | bytes 49160 | tf_op jit(solution)/shard_map/ppermute | solution.py:18
  7.9 23.6 %collective-permute-start = (f32[2,2,1,4096]{3,1,2,0:T(2,128)}, f32[2,2,1,4096]{3,1,2,0:T(2,128)}, u32[]{:S(2)}, u32[]{:S(2)}) collective-permute-start(f32[2,2,1,4096]{3,1,2,0:T(2,128)} %pad_maximum_fusion), channel_id=1, source_target_pairs={{16,0},{32,16},{48,32},{64,48},{80,64},{96,80},{112,96},{17,1},{33... | collective-permute-start | bytes 196616 | tf_op jit(solution)/shard_map/ppermute | solution.py:18
  11.9 15.3 %collective-permute-start.1 = (f32[2,2,1024]{2,0,1:T(2,128)S(1)}, f32[2,2,1024]{2,0,1:T(2,128)S(1)}, u32[]{:S(2)}, u32[]{:S(2)}) collective-permute-start(f32[2,2,1024]{2,0,1:T(2,128)S(1)} %pad_maximum_fusion.16), channel_id=1, source_target_pairs={{1,0},{2,1},{3,2},{4,3},{5,4},{6,5},{7,6},{8,7},{9,8},{10,9},{11,1... | collective-permute-start | bytes 49160 | tf_op jit(solution)/shard_map/ppermute | solution.py:18
  15.9 72.1 %copy-start.64 = (s32[2]{0:T(128)}, s32[2]{0:T(128)S(1)}, u32[]{:S(2)}) copy-start(s32[2]{0:T(128)S(1)} %get-tuple-element.12) | copy-start | bytes 28
  25.5 7.0 %copy-start.56 = (f32[2,15,4096]{2,1,0:T(8,128)S(1)}, f32[2,15,4096]{2,1,0:T(8,128)}, u32[]{:S(2)}) copy-start(f32[2,15,4096]{2,1,0:T(8,128)} %slice.972) | copy-start | bytes 1474564
  26.5 6.0 %copy-start.57 = (f32[2,16,4032]{2,1,0:T(8,128)S(1)}, f32[2,16,4032]{2,1,0:T(8,128)}, u32[]{:S(2)}) copy-start(f32[2,16,4032]{2,1,0:T(8,128)} %slice.976) | copy-start | bytes 1548292
  28.9 6.0 %copy-start = (f32[2,6,16,4096]{3,2,1,0:T(8,128)S(1)}, f32[2,6,16,4096]{3,2,1,0:T(8,128)}, u32[]{:S(2)}) copy-start(f32[2,6,16,4096]{3,2,1,0:T(8,128)} %param.8) | copy-start | bytes 9437188
  28.9 6.0 %copy-start.52 = (f32[2,15,4096]{2,1,0:T(8,128)S(1)}, f32[2,15,4096]{2,1,0:T(8,128)}, u32[]{:S(2)}) copy-start(f32[2,15,4096]{2,1,0:T(8,128)} %slice.1007) | copy-start | bytes 1474564
  30.8 28.9 %copy-start.22 = (f32[2,16,4096]{2,1,0:T(8,128)}, f32[2,16,4096]{2,1,0:T(8,128)S(1)}, u32[]{:S(2)}) copy-start(f32[2,16,4096]{2,1,0:T(8,128)S(1)} %fusion.173) | copy-start | bytes 1572868
  34.0 13.6 %copy-start.13 = (f32[2,16,4096]{2,1,0:T(8,128)}, f32[2,16,4096]{2,1,0:T(8,128)S(1)}, u32[]{:S(2)}) copy-start(f32[2,16,4096]{2,1,0:T(8,128)S(1)} %fusion.170) | copy-start | bytes 1572868
  36.8 18.3 %collective-permute-start.5 = (f32[2,2,1024]{2,0,1:T(2,128)}, f32[2,2,1024]{2,0,1:T(2,128)}, u32[]{:S(2)}, u32[]{:S(2)}) collective-permute-start(f32[2,2,1024]{2,0,1:T(2,128)} %pad_maximum_fusion.19), channel_id=1, source_target_pairs={{0,1},{1,2},{2,3},{3,4},{4,5},{5,6},{6,7},{7,8},{8,9},{9,10},{10,1... | collective-permute-start | bytes 49160 | tf_op jit(solution)/shard_map/ppermute | solution.py:18
  43.0 14.2 %collective-permute-start.6 = (f32[2,2,1,4096]{3,1,2,0:T(2,128)}, f32[2,2,1,4096]{3,1,2,0:T(2,128)}, u32[]{:S(2)}, u32[]{:S(2)}) collective-permute-start(f32[2,2,1,4096]{3,1,2,0:T(2,128)} %pad_maximum_fusion.2), channel_id=1, source_target_pairs={{0,16},{16,32},{32,48},{48,64},{64,80},{80,96},{96,112},{1,17},{17... | collective-permute-start | bytes 196616 | tf_op jit(solution)/shard_map/ppermute | solution.py:18
  45.0 13.3 %copy-start.71 = (f32[2]{0:T(128)S(1)}, f32[2]{0:T(128)}, u32[]{:S(2)}) copy-start(f32[2]{0:T(128)} %get-tuple-element.9) | copy-start | bytes 28
  47.7 12.0 %copy-start.29 = (f32[2,16,4096]{2,1,0:T(8,128)}, f32[2,16,4096]{2,1,0:T(8,128)S(1)}, u32[]{:S(2)}) copy-start(f32[2,16,4096]{2,1,0:T(8,128)S(1)} %get-tuple-element.23) | copy-start | bytes 1572868
  47.7 12.0 %copy-start.37 = (f32[2,16,4096]{2,1,0:T(8,128)}, f32[2,16,4096]{2,1,0:T(8,128)S(1)}, u32[]{:S(2)}) copy-start(f32[2,16,4096]{2,1,0:T(8,128)S(1)} %get-tuple-element.22) | copy-start | bytes 1572868
  48.5 14.3 %collective-permute-start.18 = (f32[2,2,1,4096]{3,1,2,0:T(2,128)}, f32[2,2,1,4096]{3,1,2,0:T(2,128)}, u32[]{:S(2)}, u32[]{:S(2)}) collective-permute-start(f32[2,2,1,4096]{3,1,2,0:T(2,128)} %pad_maximum_fusion.8), channel_id=1, source_target_pairs={{0,16},{16,32},{32,48},{48,64},{64,80},{80,96},{96,112},{1,17},{17... | collective-permute-start | bytes 196616 | tf_op jit(solution)/shard_map/ppermute | solution.py:18
  51.8 4.8 %collective-permute-start.2 = (f32[2,2,1024]{2,0,1:T(2,128)S(1)}, f32[2,2,1024]{2,0,1:T(2,128)S(1)}, u32[]{:S(2)}, u32[]{:S(2)}) collective-permute-start(f32[2,2,1024]{2,0,1:T(2,128)S(1)} %pad_maximum_fusion.17), channel_id=1, source_target_pairs={{0,1},{1,2},{2,3},{3,4},{4,5},{5,6},{6,7},{7,8},{8,9},{9,10},{10,1... | collective-permute-start | bytes 49160 | tf_op jit(solution)/shard_map/ppermute | solution.py:18
  61.6 10.5 %collective-permute-start.8 = (f32[2,2,1024]{2,0,1:T(2,128)S(1)}, f32[2,2,1024]{2,0,1:T(2,128)S(1)}, u32[]{:S(2)}, u32[]{:S(2)}) collective-permute-start(f32[2,2,1024]{2,0,1:T(2,128)S(1)} %pad_maximum_fusion.20), channel_id=1, source_target_pairs={{1,0},{2,1},{3,2},{4,3},{5,4},{6,5},{7,6},{8,7},{9,8},{10,9},{11,1... | collective-permute-start | bytes 49160 | tf_op jit(solution)/shard_map/ppermute | solution.py:18
  69.6 4.3 %collective-permute-start.7 = (f32[2,2,1,4096]{3,1,2,0:T(2,128)S(1)}, f32[2,2,1,4096]{3,1,2,0:T(2,128)S(1)}, u32[]{:S(2)}, u32[]{:S(2)}) collective-permute-start(f32[2,2,1,4096]{3,1,2,0:T(2,128)S(1)} %pad_maximum_fusion.3), channel_id=1, source_target_pairs={{16,0},{32,16},{48,32},{64,48},{80,64},{96,80},{112,96},{17,1},{33... | collective-permute-start | bytes 196616 | tf_op jit(solution)/shard_map/ppermute | solution.py:18
  74.0 14.1 %copy-start.70 = (f32[2]{0:T(128)S(1)}, f32[2]{0:T(128)}, u32[]{:S(2)}) copy-start(f32[2]{0:T(128)} %get-tuple-element.8) | copy-start | bytes 28
  77.7 8.1 %collective-permute-start.9 = (f32[2,2,1024]{2,0,1:T(2,128)S(1)}, f32[2,2,1024]{2,0,1:T(2,128)S(1)}, u32[]{:S(2)}, u32[]{:S(2)}) collective-permute-start(f32[2,2,1024]{2,0,1:T(2,128)S(1)} %pad_maximum_fusion.21), channel_id=1, source_target_pairs={{0,1},{1,2},{2,3},{3,4},{4,5},{5,6},{6,7},{7,8},{8,9},{9,10},{10,1... | collective-permute-start | bytes 49160 | tf_op jit(solution)/shard_map/ppermute | solution.py:18
  82.4 5.6 %collective-permute-start.10 = (f32[2,2,1,4096]{3,1,2,0:T(2,128)S(1)}, f32[2,2,1,4096]{3,1,2,0:T(2,128)S(1)}, u32[]{:S(2)}, u32[]{:S(2)}) collective-permute-start(f32[2,2,1,4096]{3,1,2,0:T(2,128)S(1)} %pad_maximum_fusion.4), channel_id=1, source_target_pairs={{0,16},{16,32},{32,48},{48,64},{64,80},{80,96},{96,112},{1,17},{17... | collective-permute-start | bytes 196616 | tf_op jit(solution)/shard_map/ppermute | solution.py:18
  91.5 18.6 %copy-start.1 = (f32[2,16,4096]{2,1,0:T(8,128)}, f32[2,16,4096]{2,1,0:T(8,128)S(1)}, u32[]{:S(2)}) copy-start(f32[2,16,4096]{2,1,0:T(8,128)S(1)} %get-tuple-element.36) | copy-start | bytes 1572868
  95.7 6.3 %copy-start.6 = (f32[2,16,4096]{2,1,0:T(8,128)S(1)}, f32[2,16,4096]{2,1,0:T(8,128)}, u32[]{:S(2)}) copy-start(f32[2,16,4096]{2,1,0:T(8,128)} %get-tuple-element.37) | copy-start | bytes 1572868
  96.4 10.4 %collective-permute-start.12 = (f32[2,2,1024]{2,0,1:T(2,128)S(1)}, f32[2,2,1024]{2,0,1:T(2,128)}, u32[]{:S(2)}, u32[]{:S(2)}) collective-permute-start(f32[2,2,1024]{2,0,1:T(2,128)S(1)} %pad_maximum_fusion.22), channel_id=1, source_target_pairs={{1,0},{2,1},{3,2},{4,3},{5,4},{6,5},{7,6},{8,7},{9,8},{10,9},{11,1... | collective-permute-start | bytes 49160 | tf_op jit(solution)/shard_map/ppermute | solution.py:18
  105.0 4.1 %collective-permute-start.11 = (f32[2,2,1,4096]{3,1,2,0:T(2,128)}, f32[2,2,1,4096]{3,1,2,0:T(2,128)}, u32[]{:S(2)}, u32[]{:S(2)}) collective-permute-start(f32[2,2,1,4096]{3,1,2,0:T(2,128)} %pad_maximum_fusion.5), channel_id=1, source_target_pairs={{16,0},{32,16},{48,32},{64,48},{80,64},{96,80},{112,96},{17,1},{33... | collective-permute-start | bytes 196616 | tf_op jit(solution)/shard_map/ppermute | solution.py:18
  110.1 16.7 %copy-start.65 = (s32[2]{0:T(128)S(1)}, s32[2]{0:T(128)}, u32[]{:S(2)}) copy-start(s32[2]{0:T(128)} %copy-done.64) | copy-start | bytes 28
  110.1 16.7 %copy-start.69 = (f32[2]{0:T(128)S(1)}, f32[2]{0:T(128)}, u32[]{:S(2)}) copy-start(f32[2]{0:T(128)} %get-tuple-element.10) | copy-start | bytes 28
  114.9 9.9 %collective-permute-start.13 = (f32[2,2,1024]{2,0,1:T(2,128)S(1)}, f32[2,2,1024]{2,0,1:T(2,128)S(1)}, u32[]{:S(2)}, u32[]{:S(2)}) collective-permute-start(f32[2,2,1024]{2,0,1:T(2,128)S(1)} %pad_maximum_fusion.23), channel_id=1, source_target_pairs={{0,1},{1,2},{2,3},{3,4},{4,5},{5,6},{6,7},{7,8},{8,9},{9,10},{10,1... | collective-permute-start | bytes 49160 | tf_op jit(solution)/shard_map/ppermute | solution.py:18
  121.1 5.6 %collective-permute-start.14 = (f32[2,2,1,4096]{3,1,2,0:T(2,128)S(1)}, f32[2,2,1,4096]{3,1,2,0:T(2,128)S(1)}, u32[]{:S(2)}, u32[]{:S(2)}) collective-permute-start(f32[2,2,1,4096]{3,1,2,0:T(2,128)S(1)} %pad_maximum_fusion.6), channel_id=1, source_target_pairs={{0,16},{16,32},{32,48},{48,64},{64,80},{80,96},{96,112},{1,17},{17... | collective-permute-start | bytes 196616 | tf_op jit(solution)/shard_map/ppermute | solution.py:18
  135.7 6.4 %copy-start.5 = (f32[2,16,4096]{2,1,0:T(8,128)S(1)}, f32[2,16,4096]{2,1,0:T(8,128)}, u32[]{:S(2)}) copy-start(f32[2,16,4096]{2,1,0:T(8,128)} %get-tuple-element.35) | copy-start | bytes 1572868
  136.5 10.6 %collective-permute-start.16 = (f32[2,2,1024]{2,0,1:T(2,128)S(1)}, f32[2,2,1024]{2,0,1:T(2,128)}, u32[]{:S(2)}, u32[]{:S(2)}) collective-permute-start(f32[2,2,1024]{2,0,1:T(2,128)S(1)} %pad_maximum_fusion.24), channel_id=1, source_target_pairs={{1,0},{2,1},{3,2},{4,3},{5,4},{6,5},{7,6},{8,7},{9,8},{10,9},{11,1... | collective-permute-start | bytes 49160 | tf_op jit(solution)/shard_map/ppermute | solution.py:18
  145.2 4.1 %collective-permute-start.15 = (f32[2,2,1,4096]{3,1,2,0:T(2,128)}, f32[2,2,1,4096]{3,1,2,0:T(2,128)}, u32[]{:S(2)}, u32[]{:S(2)}) collective-permute-start(f32[2,2,1,4096]{3,1,2,0:T(2,128)} %pad_maximum_fusion.7), channel_id=1, source_target_pairs={{16,0},{32,16},{48,32},{64,48},{80,64},{96,80},{112,96},{17,1},{33... | collective-permute-start | bytes 196616 | tf_op jit(solution)/shard_map/ppermute | solution.py:18
  158.9 10.6 %collective-permute-start.17 = (f32[2,2,1024]{2,0,1:T(2,128)S(1)}, f32[2,2,1024]{2,0,1:T(2,128)}, u32[]{:S(2)}, u32[]{:S(2)}) collective-permute-start(f32[2,2,1024]{2,0,1:T(2,128)S(1)} %pad_maximum_fusion.25), channel_id=1, source_target_pairs={{0,1},{1,2},{2,3},{3,4},{4,5},{5,6},{6,7},{7,8},{8,9},{9,10},{10,1... | collective-permute-start | bytes 49160 | tf_op jit(solution)/shard_map/ppermute | solution.py:18
  165.8 5.9 %collective-permute-start.19 = (f32[2,2,1,4096]{3,1,2,0:T(2,128)}, f32[2,2,1,4096]{3,1,2,0:T(2,128)}, u32[]{:S(2)}, u32[]{:S(2)}) collective-permute-start(f32[2,2,1,4096]{3,1,2,0:T(2,128)} %pad_maximum_fusion.9), channel_id=1, source_target_pairs={{0,16},{16,32},{32,48},{48,64},{64,80},{80,96},{96,112},{1,17},{17... | collective-permute-start | bytes 196616 | tf_op jit(solution)/shard_map/ppermute | solution.py:18
  180.4 8.1 %copy-start.34 = (f32[2,16,4096]{2,1,0:T(8,128)S(1)}, f32[2,16,4096]{2,1,0:T(8,128)}, u32[]{:S(2)}) copy-start(f32[2,16,4096]{2,1,0:T(8,128)} %copy-done.33) | copy-start | bytes 1572868
  180.4 9.1 %copy-start.42 = (f32[2,16,4096]{2,1,0:T(8,128)S(1)}, f32[2,16,4096]{2,1,0:T(8,128)}, u32[]{:S(2)}) copy-start(f32[2,16,4096]{2,1,0:T(8,128)} %copy-done.41) | copy-start | bytes 1572868
  180.4 10.2 %copy-start.21 = (f32[2,16,4096]{2,1,0:T(8,128)S(1)}, f32[2,16,4096]{2,1,0:T(8,128)}, u32[]{:S(2)}) copy-start(f32[2,16,4096]{2,1,0:T(8,128)} %copy-done.20) | copy-start | bytes 1572868
  180.4 12.9 %collective-permute-start.21 = (f32[2,2,1024]{2,0,1:T(2,128)S(1)}, f32[2,2,1024]{2,0,1:T(2,128)}, u32[]{:S(2)}, u32[]{:S(2)}) collective-permute-start(f32[2,2,1024]{2,0,1:T(2,128)S(1)} %pad_maximum_fusion.26), channel_id=1, source_target_pairs={{1,0},{2,1},{3,2},{4,3},{5,4},{6,5},{7,6},{8,7},{9,8},{10,9},{11,1... | collective-permute-start | bytes 49160 | tf_op jit(solution)/shard_map/ppermute | solution.py:18
  191.4 4.1 %collective-permute-start.20 = (f32[2,2,1,4096]{3,1,2,0:T(2,128)}, f32[2,2,1,4096]{3,1,2,0:T(2,128)S(1)}, u32[]{:S(2)}, u32[]{:S(2)}) collective-permute-start(f32[2,2,1,4096]{3,1,2,0:T(2,128)} %pad_maximum_fusion.10), channel_id=1, source_target_pairs={{16,0},{32,16},{48,32},{64,48},{80,64},{96,80},{112,96},{17,1},{33... | collective-permute-start | bytes 196616 | tf_op jit(solution)/shard_map/ppermute | solution.py:18
  200.9 11.9 %collective-permute-start.22 = (f32[2,2,1024]{2,0,1:T(2,128)S(1)}, f32[2,2,1024]{2,0,1:T(2,128)}, u32[]{:S(2)}, u32[]{:S(2)}) collective-permute-start(f32[2,2,1024]{2,0,1:T(2,128)S(1)} %pad_maximum_fusion.27), channel_id=1, source_target_pairs={{0,1},{1,2},{2,3},{3,4},{4,5},{5,6},{6,7},{7,8},{8,9},{9,10},{10,1... | collective-permute-start | bytes 49160 | tf_op jit(solution)/shard_map/ppermute | solution.py:18
  209.3 5.8 %collective-permute-start.23 = (f32[2,2,1,4096]{3,1,2,0:T(2,128)}, f32[2,2,1,4096]{3,1,2,0:T(2,128)S(1)}, u32[]{:S(2)}, u32[]{:S(2)}) collective-permute-start(f32[2,2,1,4096]{3,1,2,0:T(2,128)} %pad_maximum_fusion.11), channel_id=1, source_target_pairs={{0,16},{16,32},{32,48},{48,64},{64,80},{80,96},{96,112},{1,17},{17... | collective-permute-start | bytes 196616 | tf_op jit(solution)/shard_map/ppermute | solution.py:18
  219.5 8.1 %copy-start.45 = (f32[2,16,4096]{2,1,0:T(8,128)S(1)}, f32[2,16,4096]{2,1,0:T(8,128)}, u32[]{:S(2)}) copy-start(f32[2,16,4096]{2,1,0:T(8,128)} %copy-done.44) | copy-start | bytes 1572868
  219.5 9.2 %copy-start.19 = (f32[2,16,4096]{2,1,0:T(8,128)S(1)}, f32[2,16,4096]{2,1,0:T(8,128)}, u32[]{:S(2)}) copy-start(f32[2,16,4096]{2,1,0:T(8,128)} %copy-done.18) | copy-start | bytes 1572868
  219.6 13.0 %collective-permute-start.25 = (f32[2,2,1024]{2,0,1:T(2,128)S(1)}, f32[2,2,1024]{2,0,1:T(2,128)}, u32[]{:S(2)}, u32[]{:S(2)}) collective-permute-start(f32[2,2,1024]{2,0,1:T(2,128)S(1)} %pad_maximum_fusion.28), channel_id=1, source_target_pairs={{1,0},{2,1},{3,2},{4,3},{5,4},{6,5},{7,6},{8,7},{9,8},{10,9},{11,1... | collective-permute-start | bytes 49160 | tf_op jit(solution)/shard_map/ppermute | solution.py:18
  230.6 4.1 %collective-permute-start.24 = (f32[2,2,1,4096]{3,1,2,0:T(2,128)}, f32[2,2,1,4096]{3,1,2,0:T(2,128)S(1)}, u32[]{:S(2)}, u32[]{:S(2)}) collective-permute-start(f32[2,2,1,4096]{3,1,2,0:T(2,128)} %pad_maximum_fusion.12), channel_id=1, source_target_pairs={{16,0},{32,16},{48,32},{64,48},{80,64},{96,80},{112,96},{17,1},{33... | collective-permute-start | bytes 196616 | tf_op jit(solution)/shard_map/ppermute | solution.py:18
  240.1 11.9 %collective-permute-start.26 = (f32[2,2,1024]{2,0,1:T(2,128)S(1)}, f32[2,2,1024]{2,0,1:T(2,128)}, u32[]{:S(2)}, u32[]{:S(2)}) collective-permute-start(f32[2,2,1024]{2,0,1:T(2,128)S(1)} %pad_maximum_fusion.29), channel_id=1, source_target_pairs={{0,1},{1,2},{2,3},{3,4},{4,5},{5,6},{6,7},{7,8},{8,9},{9,10},{10,1... | collective-permute-start | bytes 49160 | tf_op jit(solution)/shard_map/ppermute | solution.py:18
  248.5 5.8 %collective-permute-start.27 = (f32[2,2,1,4096]{3,1,2,0:T(2,128)}, f32[2,2,1,4096]{3,1,2,0:T(2,128)S(1)}, u32[]{:S(2)}, u32[]{:S(2)}) collective-permute-start(f32[2,2,1,4096]{3,1,2,0:T(2,128)} %pad_maximum_fusion.13), channel_id=1, source_target_pairs={{0,16},{16,32},{32,48},{48,64},{64,80},{80,96},{96,112},{1,17},{17... | collective-permute-start | bytes 196616 | tf_op jit(solution)/shard_map/ppermute | solution.py:18
  260.5 10.1 %copy-start.17 = (f32[2,16,4096]{2,1,0:T(8,128)S(1)}, f32[2,16,4096]{2,1,0:T(8,128)}, u32[]{:S(2)}) copy-start(f32[2,16,4096]{2,1,0:T(8,128)} %copy-done.16) | copy-start | bytes 1572868
  261.0 7.6 %copy-start.32 = (f32[2,16,4096]{2,1,0:T(8,128)S(1)}, f32[2,16,4096]{2,1,0:T(8,128)}, u32[]{:S(2)}) copy-start(f32[2,16,4096]{2,1,0:T(8,128)} %copy-done.31) | copy-start | bytes 1572868
  261.0 8.6 %copy-start.40 = (f32[2,16,4096]{2,1,0:T(8,128)S(1)}, f32[2,16,4096]{2,1,0:T(8,128)}, u32[]{:S(2)}) copy-start(f32[2,16,4096]{2,1,0:T(8,128)} %copy-done.39) | copy-start | bytes 1572868
  261.0 12.3 %collective-permute-start.29 = (f32[2,2,1024]{2,0,1:T(2,128)S(1)}, f32[2,2,1024]{2,0,1:T(2,128)}, u32[]{:S(2)}, u32[]{:S(2)}) collective-permute-start(f32[2,2,1024]{2,0,1:T(2,128)S(1)} %pad_maximum_fusion.30), channel_id=1, source_target_pairs={{1,0},{2,1},{3,2},{4,3},{5,4},{6,5},{7,6},{8,7},{9,8},{10,9},{11,1... | collective-permute-start | bytes 49160 | tf_op jit(solution)/shard_map/ppermute | solution.py:18
  262.5 13.7 %copy-start.15 = (f32[2,16,4096]{2,1,0:T(8,128)S(1)}, f32[2,16,4096]{2,1,0:T(8,128)}, u32[]{:S(2)}) copy-start(f32[2,16,4096]{2,1,0:T(8,128)} %copy-done.14) | copy-start | bytes 1572868
  262.5 13.7 %copy-start.30 = (f32[2,16,4096]{2,1,0:T(8,128)S(1)}, f32[2,16,4096]{2,1,0:T(8,128)}, u32[]{:S(2)}) copy-start(f32[2,16,4096]{2,1,0:T(8,128)} %get-tuple-element.42) | copy-start | bytes 1572868
  271.4 3.8 %collective-permute-start.28 = (f32[2,2,1,4096]{3,1,2,0:T(2,128)S(1)}, f32[2,2,1,4096]{3,1,2,0:T(2,128)}, u32[]{:S(2)}, u32[]{:S(2)}) collective-permute-start(f32[2,2,1,4096]{3,1,2,0:T(2,128)S(1)} %pad_maximum_fusion.14), channel_id=1, source_target_pairs={{16,0},{32,16},{48,32},{64,48},{80,64},{96,80},{112,96},{17,1},{33... | collective-permute-start | bytes 196616 | tf_op jit(solution)/shard_map/ppermute | solution.py:18
  280.4 10.2 %collective-permute-start.30 = (f32[2,2,1024]{2,0,1:T(2,128)S(1)}, f32[2,2,1024]{2,0,1:T(2,128)S(1)}, u32[]{:S(2)}, u32[]{:S(2)}) collective-permute-start(f32[2,2,1024]{2,0,1:T(2,128)S(1)} %pad_maximum_fusion.31), channel_id=1, source_target_pairs={{0,1},{1,2},{2,3},{3,4},{4,5},{5,6},{6,7},{7,8},{8,9},{9,10},{10,1... | collective-permute-start | bytes 49160 | tf_op jit(solution)/shard_map/ppermute | solution.py:18
  286.6 5.6 %collective-permute-start.31 = (f32[2,2,1,4096]{3,1,2,0:T(2,128)S(1)}, f32[2,2,1,4096]{3,1,2,0:T(2,128)S(1)}, u32[]{:S(2)}, u32[]{:S(2)}) collective-permute-start(f32[2,2,1,4096]{3,1,2,0:T(2,128)S(1)} %pad_maximum_fusion.15), channel_id=1, source_target_pairs={{0,16},{16,32},{32,48},{48,64},{64,80},{80,96},{96,112},{1,17},{17... | collective-permute-start | bytes 196616 | tf_op jit(solution)/shard_map/ppermute | solution.py:18
  303.2 39.7 %copy-start.72 = (s32[1,64]{1,0:T(1,128)S(1)}, s32[1,64]{1,0:T(1,128)}, u32[]{:S(2)}) copy-start(s32[1,64]{1,0:T(1,128)} %param.15) | copy-start | bytes 772
  327.9 23.7 %all-to-all-start.1 = ((f32[16,4,2,512]{3,1,2,0:T(4,128)}), f32[16,4,2,512]{3,1,2,0:T(4,128)S(1)}, u32[]{:S(2)}, u32[]{:S(2)}) async-start(f32[16,4,2,512]{3,1,2,0:T(4,128)} %copy.86), calls=%async_computation.1 | async-start | bytes 524288 | tf_op jit(solution)/shard_map/all_to_all | solution.py:174
  (42 other events, 110.0 us)
where the time goes:
time: 357 us; the launch traced here: 353 us
  local copies, waits for them, and re-layouts  122 us (34%)
  starting transfers between devices  113 us (32%)
  other arithmetic  71.6 us (20%)
  waiting for transfers between devices  26.9 us (8%)
  blocking collectives  17.4 us (5%)
    ppermute x32, starting transfers between devices, passed_along(): return lax.ppermute(shard, axis, pairs)  98.2 us
    sub x8, other arithmetic, magnetic_update(): magnetic[0]  23.2 us
    slice x16, local copies, waits for them, and re-layouts, upper_y(): return jnp.concatenate([values[..., z_cells:], ghosts], axis=-1)  21.3 us
    ppermute x32, waiting for transfers between devices, passed_along(): return lax.ppermute(shard, axis, pairs)  18.3 us
    all_to_all x1, blocking collectives, per_device(): lax.all_to_all(sectioned, 'src', split_axis=3, concat_axis=2, tiled=True)  17.4 us
    slice x16, local copies, waits for them, and re-layouts, upper_z(): values[..., 1:]  17.2 us
    reduce_sum x3, other arithmetic, per_device(): density = density + jnp.sum(intersection, axis=0)  16 us
    slice x16, local copies, waits for them, and re-layouts, upper_x(): return jnp.concatenate([values[..., 1:, :], ghosts], axis=-2)  15.9 us
  transfers between devices with their start and end apart: 33, of which 14 were waited for; matrix products, arithmetic and copies ran while one was open for 27% of the time, Pallas kernels for 0%

commit v1 on v0

v1 whole, which is shorter than its diff:
```python
import functools

import jax
import jax.numpy as jnp
from jax import lax
from jax.experimental import pallas as pl
from jax.experimental.pallas import tpu as pltpu
from jax.sharding import PartitionSpec as P

NZ = 64
STEPS = 4
BX = 4
BY = 4
HALO = 4
CX = 16
XR = CX + 2 * HALO
TJ = 32
TE = TJ + 4
ROWS = (TE + 2) * XR
W = 128
COURANT = 0.55
F32 = jnp.float32


def shifted_pairs(count, by):
    return [(i, i + by) for i in range(count) if 0 <= i + by < count]


def passed_along(shard, axis, by):
    return lax.ppermute(shard, axis, shifted_pairs(lax.axis_size(axis), by))


def lanes(tile):
    return pl.ds(tile * W, W)


def pack_first(adj, fwd_lo, fwd_hi, eps_lo, eps_hi, ax_up, ax_dn, fy_up, fy_dn):
    def one(k, _):
        s, c = k // 6, k % 6
        for j in range(TJ):
            row = pl.multiple_of((k * TJ + j) * 4, 4)
            ax_dn[pl.ds(row, 4), :] = adj[s, c, 0:4, lanes(j)]
            ax_up[pl.ds(row, 4), :] = adj[s, c, CX - 4 : CX, lanes(j)]
        for j in range(2):
            row = pl.multiple_of((k * 2 + j) * CX, CX)
            fy_dn[pl.ds(row, CX), :] = fwd_lo[s, c, :, lanes(j)]
            fy_up[pl.ds(row, CX), :] = fwd_hi[s, c, :, lanes(j)]
        return 0

    lax.fori_loop(0, 12, one, 0)
    for j in range(2):
        row = (12 * 2 + j) * CX
        fy_dn[pl.ds(row, CX), :] = COURANT / eps_lo[:, lanes(j)]
        fy_up[pl.ds(row, CX), :] = COURANT / eps_hi[:, lanes(j)]


def pack_forward_x(fwd, eps, fy_lo, fy_hi, fx_up, fx_dn):
    def ghosts(k):
        for j in range(2):
            src = pl.multiple_of((k * 2 + j) * CX, CX)
            lo = pl.multiple_of((k * TE + j) * 4, 4)
            hi = pl.multiple_of((k * TE + TJ + 2 + j) * 4, 4)
            fx_dn[pl.ds(lo, 4), :] = fy_lo[pl.ds(src, 4), :]
            fx_up[pl.ds(lo, 4), :] = fy_lo[pl.ds(src + CX - 4, 4), :]
            fx_dn[pl.ds(hi, 4), :] = fy_hi[pl.ds(src, 4), :]
            fx_up[pl.ds(hi, 4), :] = fy_hi[pl.ds(src + CX - 4, 4), :]

    def one(k, _):
        s, c = k // 6, k % 6
        for j in range(TJ):
            row = pl.multiple_of((k * TE + 2 + j) * 4, 4)
            fx_dn[pl.ds(row, 4), :] = fwd[s, c, 0:4, lanes(j)]
            fx_up[pl.ds(row, 4), :] = fwd[s, c, CX - 4 : CX, lanes(j)]
        ghosts(k)
        return 0

    lax.fori_loop(0, 12, one, 0)
    for j in range(TJ):
        row = (12 * TE + 2 + j) * 4
        fx_dn[pl.ds(row, 4), :] = COURANT / eps[0:4, lanes(j)]
        fx_up[pl.ds(row, 4), :] = COURANT / eps[CX - 4 : CX, lanes(j)]
    ghosts(12)


def pack_adjoint_y(adj_lo, adj_hi, ax_lo, ax_hi, ay_up, ay_dn):
    def one(k, _):
        s, c = k // 6, k % 6
        for j in range(2):
            base = pl.multiple_of((k * 2 + j) * XR, 8)
            for out, own, tile in ((ay_dn, adj_lo, j), (ay_up, adj_hi, TJ - 2 + j)):
                src = pl.multiple_of((k * TJ + tile) * 4, 4)
                out[pl.ds(base, 4), :] = ax_lo[pl.ds(src, 4), :]
                out[pl.ds(base + 4, CX), :] = own[s, c, :, lanes(j)]
                out[pl.ds(base + 4 + CX, 4), :] = ax_hi[pl.ds(src, 4), :]
        return 0

    lax.fori_loop(0, 12, one, 0)


def simulate(
    where,
    owners,
    slots,
    cells,
    wave,
    fwd,
    adj,
    eps,
    fy_lo,
    fy_hi,
    fx_lo,
    fx_hi,
    ax_lo,
    ax_hi,
    ay_lo,
    ay_hi,
    out,
    field,
    factor,
    inc,
    density,
    block,
):
    at_x0, at_x1, at_y0, at_y1, gx, gy = (where[i] for i in range(6))
    lane = lax.broadcasted_iota(jnp.int32, (8, W), 1)
    row8 = lax.broadcasted_iota(jnp.int32, (8, W), 0)
    low = lane < NZ
    z_first = (lane & (NZ - 1)) == 0
    z_last = (lane & (NZ - 1)) == NZ - 1
    coef_x = [
        jnp.where((row8 < 4) & (at_x0 == 1), 0.0, COURANT).astype(F32),
        jnp.full((8, W), COURANT, F32),
        jnp.where((row8 >= 4) & (at_x1 == 1), 0.0, COURANT).astype(F32),
    ]

    zeros = jnp.zeros((XR, W), F32)
    for k in range(12):
        field[k, pl.ds(0, XR), :] = zeros
        field[k, pl.ds((TE + 1) * XR, XR), :] = zeros
    factor[pl.ds(0, XR), :] = zeros
    factor[pl.ds((TE + 1) * XR, XR), :] = zeros

    def fill_forward(put, k, own):
        for j in range(TJ):
            r = (j + 3) * XR
            put(r + 4, own(j))
            src = pl.multiple_of((k * TE + 2 + j) * 4, 4)
            put(r, fx_lo[pl.ds(src, 4), :])
            put(r + 4 + CX, fx_hi[pl.ds(src, 4), :])
        for j, ghost, g in ((0, fy_lo, 0), (1, fy_lo, 1), (TE - 2, fy_hi, 0), (TE - 1, fy_hi, 1)):
            r = (j + 1) * XR
            src = pl.multiple_of((k * 2 + g) * CX, CX)
            put(r + 4, ghost[pl.ds(src, CX), :])
            src = pl.multiple_of((k * TE + j) * 4, 4)
            put(r, fx_lo[pl.ds(src, 4), :])
            put(r + 4 + CX, fx_hi[pl.ds(src, 4), :])

    def load_forward(k, _):
        def put(r, v):
            field[k, pl.ds(r, v.shape[0]), :] = v

        fill_forward(put, k, lambda j: fwd[k // 6, k % 6, :, lanes(j)])
        return 0

    def load_adjoint(k, _):
        def put(r, v):
            field[k, pl.ds(r, v.shape[0]), :] = v

        for j in range(TJ):
            r = (j + 3) * XR
            put(r + 4, adj[k // 6, k % 6, :, lanes(j)])
            src = pl.multiple_of((k * TJ + j) * 4, 4)
            put(r, ax_lo[pl.ds(src, 4), :])
            put(r + 4 + CX, ax_hi[pl.ds(src, 4), :])
        for j, ghost, g in ((0, ay_lo, 0), (1, ay_lo, 1), (TE - 2, ay_hi, 0), (TE - 1, ay_hi, 1)):
            src = pl.multiple_of((k * 2 + g) * XR, 8)
            put((j + 1) * XR, ghost[pl.ds(src, XR), :])
        return 0

    def up_z(v):
        return jnp.where(z_last, 0.0, pltpu.roll(v, W - 1, 1))

    def down_z(v):
        return jnp.where(z_first, 0.0, pltpu.roll(v, 1, 1))

    def up_y(v, after):
        return pltpu.roll(jnp.where(low, after, v), NZ, 1)

    def down_y(v, before):
        return pltpu.roll(jnp.where(low, v, before), NZ, 1)

    def magnetic(j, _):
        inside = jnp.where(
            ((j < 2) & (at_y0 == 1)) | ((j >= TE - 2) & (at_y1 == 1)), 0.0, 1.0
        ).astype(F32)
        done = []
        for t in range(3):
            b = pl.multiple_of((j + 1) * XR + 8 * t, 8)
            c = coef_x[t] * inside
            for s in range(2):
                k = 6 * s
                ex = field[k, pl.ds(b, 8), :]
                ey = field[k + 1, pl.ds(b, 8), :]
                ez = field[k + 2, pl.ds(b, 8), :]
                ex_y = up_y(ex, field[k, pl.ds(b + XR, 8), :])
                ez_y = up_y(ez, field[k + 2, pl.ds(b + XR, 8), :])
                ey_x = field[k + 1, pl.ds(b + 1, 8), :]
                ez_x = field[k + 2, pl.ds(b + 1, 8), :]
                hx = field[k + 3, pl.ds(b, 8), :]
                hy = field[k + 4, pl.ds(b, 8), :]
                hz = field[k + 5, pl.ds(b, 8), :]
                hx = hx - c * ((ez_y - ez) - (up_z(ey) - ey))
                hy = hy - c * ((up_z(ex) - ex) - (ez_x - ez))
                hz = hz - c * ((ey_x - ey) - (ex_y - ex))
                done.append((k, b, hx, hy, hz))
        for k, b, hx, hy, hz in done:
            field[k + 3, pl.ds(b, 8), :] = hx
            field[k + 4, pl.ds(b, 8), :] = hy
            field[k + 5, pl.ds(b, 8), :] = hz
        return 0

    def electric(j, step, adjoint):
        done = []
        for t in range(3):
            b = pl.multiple_of((j + 1) * XR + 8 * t, 8)
            a = pl.multiple_of(j * XR + 8 * t, 8)
            f = factor[pl.ds(b, 8), :]
            total = density[pl.ds(a, 8), :] if adjoint else None
            for s in range(2):
                k = 6 * s
                hx = field[k + 3, pl.ds(b, 8), :]
                hy = field[k + 4, pl.ds(b, 8), :]
                hz = field[k + 5, pl.ds(b, 8), :]
                hx_y = down_y(hx, field[k + 3, pl.ds(b - XR, 8), :])
                hz_y = down_y(hz, field[k + 5, pl.ds(b - XR, 8), :])
                hy_x = field[k + 4, pl.ds(b - 1, 8), :]
                hz_x = field[k + 5, pl.ds(b - 1, 8), :]
                ex = field[k, pl.ds(b, 8), :]
                ey = field[k + 1, pl.ds(b, 8), :]
                ez = field[k + 2, pl.ds(b, 8), :]
                nx = ex + f * ((hz - hz_y) - (hy - down_z(hy)))
                ny = ey + f * ((hx - down_z(hx)) - (hz - hz_x))
                nz = ez + f * ((hy - hy_x) - (hx - hx_y))
                i = 3 * s
                if adjoint:
                    total = total + (
                        nx * inc[step, i, pl.ds(a, 8), :]
                        + ny * inc[step, i + 1, pl.ds(a, 8), :]
                        + nz * inc[step, i + 2, pl.ds(a, 8), :]
                    )
                    done.append((k, i, a, b, nx, ny, nz, None))
                else:
                    done.append((k, i, a, b, nx, ny, nz, (nx - ex, ny - ey, nz - ez)))
            if adjoint:
                done.append((None, None, a, None, total, None, None, None))
        for k, i, a, b, nx, ny, nz, grown in done:
            if k is None:
                density[pl.ds(a, 8), :] = nx
                continue
            field[k, pl.ds(b, 8), :] = nx
            field[k + 1, pl.ds(b, 8), :] = ny
            field[k + 2, pl.ds(b, 8), :] = nz
            if grown is not None:
                for m in range(3):
                    inc[step, i + m, pl.ds(a, 8), :] = grown[m]
        return 0

    spans_h = ((0, TE), (0, TE - 1), (1, TE - 1), (1, TE - 2))
    spans_e = ((0, TE), (1, TE - 1), (1, TE - 1), (2, TE - 2))

    lax.fori_loop(0, 12, load_forward, 0)

    def put_factor(r, v):
        factor[pl.ds(r, v.shape[0]), :] = v

    fill_forward(put_factor, 12, lambda j: COURANT / eps[:, lanes(j)])

    for n in range(STEPS):
        lax.fori_loop(*spans_h[n], magnetic, 0)
        lax.fori_loop(*spans_e[n], lambda j, _: electric(j, n, False), 0)
        for s in range(2):
            x = cells[s, 0] - gx * CX + HALO
            y = cells[s, 1] - gy * (2 * TJ) + HALO
            z = cells[s, 2]

            @pl.when((x >= 0) & (x < XR) & (y >= 0) & (y < 2 * TE))
            def _():
                r = (y // 2) * XR + x
                here = lax.broadcasted_iota(jnp.int32, (1, W), 1) == (y % 2) * NZ + z
                pulse = jnp.where(here, wave[s, n], 0.0).astype(F32)
                field[6 * s + 2, pl.ds(r + XR, 1), :] += pulse
                inc[n, 3 * s + 2, pl.ds(r, 1), :] += pulse

    lax.fori_loop(0, 12, load_adjoint, 0)
    density[...] = jnp.zeros_like(density)
    for n in range(STEPS):
        lax.fori_loop(*spans_h[n], magnetic, 0)
        lax.fori_loop(*spans_e[n], lambda j, _: electric(j, STEPS - 1 - n, True), 0)

    for j in range(TJ):
        for t in range(2):
            g = density[pl.ds((j + 2) * XR + 4 + 8 * t, 8), :]
            g = -g / eps[8 * t : 8 * t + 8, lanes(j)]
            for h in range(2):
                b = ((2 * t + h) * (TJ // 2) + j // 2) * 8 + j % 2
                block[pl.ds(b, 4, stride=2), :] = g[4 * h : 4 * h + 4]
    out[...] = jnp.zeros_like(out)

    def send(i, _):
        o = owners[i]

        @pl.when(o >= 0)
        def _():
            c = pl.multiple_of(slots[i] * 4, 4)
            b = pl.multiple_of(i * 8, 8)
            out[o, pl.ds(c, 4), :] = block[pl.ds(b, 4), :]
            out[16 + o, pl.ds(c, 4), :] = block[pl.ds(b + 4, 4), :]

        return 0

    lax.fori_loop(0, 64, send, 0)


def place(rows, arrived, out, wide):
    def one(g, _):
        v = arrived[g] + arrived[16 + g]
        for c in range(4):
            r = pl.multiple_of(rows[g * 4 + c] * 4, 4)
            wide[pl.ds(r, 4), :] = v[c * 4 : c * 4 + 4]
        return 0

    lax.fori_loop(0, 16, one, 0)
    for i in range(8):
        for q in range(4):
            out[8 * i : 8 * i + 8, lanes(q)] = wide[pl.ds(32 * i + q, 8, stride=4), :]


def per_device(
    forward_state,
    adjoint_state,
    permittivity,
    waveform,
    source_cell,
    block_owner,
    block_slot,
    owner_rows,
):
    full = pl.BlockSpec(memory_space=pltpu.VMEM)
    scalars = pl.BlockSpec(memory_space=pltpu.SMEM)
    params = functools.partial(pltpu.CompilerParams)

    def buf(*shape):
        return jax.ShapeDtypeStruct(shape, F32)

    strip = (2, 6, CX, 2 * W)
    s_lo = pl.BlockSpec(strip, lambda i: (0, 0, 0, 0))
    s_hi = pl.BlockSpec(strip, lambda i: (0, 0, 0, TJ // 2 - 1))
    e_lo = pl.BlockSpec((CX, 2 * W), lambda i: (0, 0))
    e_hi = pl.BlockSpec((CX, 2 * W), lambda i: (0, TJ // 2 - 1))
    state = pl.BlockSpec((2, 6, CX, TJ * W), lambda i: (0, 0, 0, 0))
    whole = lambda *shape: pl.BlockSpec(shape, lambda i: (0,) * len(shape))

    ax_n, fy_n, fx_n, ay_n = 12 * TJ * 4, 13 * 2 * CX, 13 * TE * 4, 12 * 2 * XR
    ax_up, ax_dn, fy_up, fy_dn = pl.pallas_call(
        pack_first,
        grid=(1,),
        in_specs=[state, s_lo, s_hi, e_lo, e_hi],
        out_specs=[whole(ax_n, W)] * 2 + [whole(fy_n, W)] * 2,
        out_shape=[buf(ax_n, W)] * 2 + [buf(fy_n, W)] * 2,
        compiler_params=params(vmem_limit_bytes=24 << 20),
        name="pack_first",
    )(adjoint_state, forward_state, forward_state, permittivity, permittivity)

    ax_lo = passed_along(ax_up, "gx", 1)
    ax_hi = passed_along(ax_dn, "gx", -1)
    fy_lo = passed_along(fy_up, "gy", 1)
    fy_hi = passed_along(fy_dn, "gy", -1)

    fx_up, fx_dn = pl.pallas_call(
        pack_forward_x,
        in_specs=[full] * 4,
        out_specs=[full] * 2,
        out_shape=[buf(fx_n, W)] * 2,
        compiler_params=params(vmem_limit_bytes=24 << 20),
        name="pack_forward_x",
    )(forward_state, permittivity, fy_lo, fy_hi)
    fx_lo = passed_along(fx_up, "gx", 1)
    fx_hi = passed_along(fx_dn, "gx", -1)

    ay_up, ay_dn = pl.pallas_call(
        pack_adjoint_y,
        grid=(1,),
        in_specs=[s_lo, s_hi, whole(ax_n, W), whole(ax_n, W)],
        out_specs=[whole(ay_n, W)] * 2,
        out_shape=[buf(ay_n, W)] * 2,
        compiler_params=params(vmem_limit_bytes=24 << 20),
        name="pack_adjoint_y",
    )(adjoint_state, adjoint_state, ax_lo, ax_hi)
    ay_lo = passed_along(ay_up, "gy", 1)
    ay_hi = passed_along(ay_dn, "gy", -1)

    gx, gy = lax.axis_index("gx"), lax.axis_index("gy")
    where = jnp.stack(
        [
            gx == 0,
            gx == lax.axis_size("gx") - 1,
            gy == 0,
            gy == lax.axis_size("gy") - 1,
            gx,
            gy,
        ]
    ).astype(jnp.int32)
    outgoing = pl.pallas_call(
        simulate,
        in_specs=[scalars] * 5 + [full] * 11,
        out_specs=full,
        out_shape=buf(32, 16, W),
        scratch_shapes=[
            pltpu.VMEM((12, ROWS, W), F32),
            pltpu.VMEM((ROWS, W), F32),
            pltpu.VMEM((STEPS, 6, TE * XR, W), F32),
            pltpu.VMEM((TE * XR, W), F32),
            pltpu.VMEM((64 * 8, W), F32),
        ],
        compiler_params=params(vmem_limit_bytes=56 << 20),
        name="simulate",
    )(
        where,
        block_owner.reshape(-1),
        block_slot.reshape(-1),
        source_cell,
        waveform,
        forward_state,
        adjoint_state,
        permittivity,
        fy_lo,
        fy_hi,
        fx_lo,
        fx_hi,
        ax_lo,
        ax_hi,
        ay_lo,
        ay_hi,
    )
    arrived = lax.all_to_all(outgoing, ("src", "gy"), 0, 0, tiled=True)
    return pl.pallas_call(
        place,
        in_specs=[scalars, full],
        out_specs=full,
        out_shape=buf(64, 512),
        scratch_shapes=[pltpu.VMEM((256, W), F32)],
        name="place",
    )(owner_rows.reshape(-1), arrived)


def solution(mesh):
    in_specs = (
        P("src", None, "gx", "gy"),
        P("src", None, "gx", "gy"),
        P("gx", "gy"),
        P("src", None),
        P("src", None),
        P("gx", "gy"),
        P("gx", "gy"),
        P(("gx", "gy"), None),
    )
    out_specs = P(("gx", "gy"), "src")
    return jax.shard_map(
        per_device, mesh=mesh, in_specs=in_specs, out_specs=out_specs, check_vma=False
    )
```

time: 357 us -> 138 us (0.39)
  local copies, waits for them, and re-layouts: 122 us -> 9.32 us
  starting transfers between devices: 113 us -> 21.8 us
  other arithmetic: 71.6 us -> 0 us
  Pallas kernels: 0 us -> 65.1 us
  waiting for transfers between devices: 26.9 us -> 9.33 us
  blocking collectives: 17.4 us -> 31.6 us
    ppermute x32 -> x8, starting transfers between devices: 98.2 us -> 21.8 us  [passed_along(): return lax.ppermute(shard, axis, shifted_pairs(lax.axis_size(axis), by))]
    pallas_call x0 -> x5, Pallas kernels: none -> 65.1 us  [the longest x1 60.9 us: per_device(): pl.pallas_call(simulate, in_specs=[scalars] * 5 + [full] * 11, out_specs=...]
    slice x81 -> x0, local copies, waits for them, and re-layouts: 62.8 us -> none  [the longest x16 21.3 us: upper_y(): return jnp.concatenate([values[..., z_cells:], ghosts], axis=-1)]
    sub x11 -> x0, other arithmetic: 26.8 us -> none  [the longest x8 23.2 us: magnetic_update(): magnetic[0]]
    reduce_sum x4 -> x0, other arithmetic: 16.1 us -> none  [the longest x3 16 us: per_device(): density = density + jnp.sum(intersection, axis=0)]
    all_to_all x1 -> x0, starting transfers between devices: 15 us -> none  [per_device(): lax.all_to_all(lax.all_to_all(sectioned, 'src', split_axis=3, concat_axis...]
    another operation x62 -> x1, local copies, waits for them, and re-layouts: 15.6 us -> 0.67 us  [per_device(): jnp.stack([gx == 0, gx == lax.axis_size('gx') - 1, gy == 0, gy == lax.axi...]
    all_to_all x1, blocking collectives: 17.4 us -> 31.6 us  [per_device(): arrived = lax.all_to_all(outgoing, ('src', 'gy'), 0, 0, tiled=True)]
  transfers between devices with their start and end apart: 33 -> 8, of which waited for: 14 -> 4; matrix products, arithmetic and copies ran while one was open for 27% -> 1% of each run, Pallas kernels for 0% -> 1%
where the time goes in v1:
time: 138 us; the launch traced here: 137 us
  Pallas kernels  65.1 us (47%)
  blocking collectives  31.6 us (23%)
  starting transfers between devices  21.8 us (16%)
  waiting for transfers between devices  9.33 us (7%)
  local copies, waits for them, and re-layouts  9.32 us (7%)
    pallas_call x1, Pallas kernels, per_device(): pl.pallas_call(simulate, in_specs=[scalars] * 5 + [full] * 11, out_specs=...  60.9 us
    all_to_all x1, blocking collectives, per_device(): arrived = lax.all_to_all(outgoing, ('src', 'gy'), 0, 0, tiled=True)  31.6 us
    ppermute x8, starting transfers between devices, passed_along(): return lax.ppermute(shard, axis, shifted_pairs(lax.axis_size(axis), by))  21.8 us
    ppermute x8, waiting for transfers between devices, passed_along(): return lax.ppermute(shard, axis, shifted_pairs(lax.axis_size(axis), by))  9.33 us
    unnamed x28, local copies, waits for them, and re-layouts  7.39 us
  transfers between devices with their start and end apart: 8, of which 4 were waited for; matrix products, arithmetic and copies ran while one was open for 1% of the time, Pallas kernels for 1%

profile of v1, /device:TPU:32, one launch (start us, length us, event | category | flops | bytes accessed | tf_op | source)
XLA Modules:
  0.0 137.3 jit_solution(16841089197591253023)
XLA Ops:
  0.0 0.0 copy-start
  0.0 1.9 %copy-done = f32[2,6,16,4096]{3,2,1,0:T(8,128)S(1)} copy-done((f32[2,6,16,4096]{3,2,1,0:T(8,128)S(1)}, f32[2,6,16,4096]{3,2,1,0:T(8,128)}, u32[]{:S(2)}) %copy-start) | copy-done | bytes 3145752
  1.9 0.0 copy-start.2
  1.9 1.9 %copy-done.2 = f32[2,6,16,4096]{3,2,1,0:T(8,128)S(1)} copy-done((f32[2,6,16,4096]{3,2,1,0:T(8,128)S(1)}, f32[2,6,16,4096]{3,2,1,0:T(8,128)}, u32[]{:S(2)}) %copy-start.2) | copy-done | bytes 3145752
  3.8 0.0 copy-start.3
  3.8 0.9 copy-done.3
  4.7 0.0 copy-start.1
  4.7 0.5 pack_first.1
  5.2 3.5 %collective-permute-start = (f32[416,128]{1,0:T(8,128)S(1)}, f32[416,128]{1,0:T(8,128)S(1)}, u32[]{:S(2)}, u32[]{:S(2)}) collective-permute-start(f32[416,128]{1,0:T(8,128)S(1)} %get-tuple-element.13), channel_id=1, source_target_pairs={{0,1},{1,2},{2,3},{3,4},{4,5},{5,6},{6,7},{7,8},{8,9},{9,10},{10,1... | collective-permute-start | bytes 638984 | tf_op jit(solution)/shard_map/ppermute | solution.py:30
  8.8 1.3 collective-permute-start.1
  10.1 1.9 %collective-permute-start.4 = (f32[1536,128]{1,0:T(8,128)S(1)}, f32[1536,128]{1,0:T(8,128)S(1)}, u32[]{:S(2)}, u32[]{:S(2)}) collective-permute-start(f32[1536,128]{1,0:T(8,128)S(1)} %get-tuple-element.17), channel_id=1, source_target_pairs={{0,16},{16,32},{32,48},{48,64},{64,80},{80,96},{96,112},{1,17},{17... | collective-permute-start | bytes 2359304 | tf_op jit(solution)/shard_map/ppermute | solution.py:30
  12.0 3.6 %collective-permute-start.5 = (f32[1536,128]{1,0:T(8,128)S(1)}, f32[1536,128]{1,0:T(8,128)S(1)}, u32[]{:S(2)}, u32[]{:S(2)}) collective-permute-start(f32[1536,128]{1,0:T(8,128)S(1)} %get-tuple-element.18), channel_id=1, source_target_pairs={{16,0},{32,16},{48,32},{64,48},{80,64},{96,80},{112,96},{17,1},{33... | collective-permute-start | bytes 2359304 | tf_op jit(solution)/shard_map/ppermute | solution.py:30
  15.7 0.0 collective-permute-done.fy_lo
  15.7 0.0 copy-start.6
  15.7 1.7 %collective-permute-done.1.fy_hi = f32[416,128]{1,0:T(8,128)S(1)} collective-permute-done((f32[416,128]{1,0:T(8,128)S(1)}, f32[416,128]{1,0:T(8,128)S(1)}, u32[]{:S(2)}, u32[]{:S(2)}) %collective-permute-start.1) | collective-permute-done | bytes 213024 | tf_op jit(solution)/shard_map/ppermute | solution.py:30
  17.4 0.0 copy-done.1
  17.4 0.0 copy-start.7
  17.4 1.8 %pack_forward_x.1 = (f32[1872,128]{1,0:T(8,128)}, f32[1872,128]{1,0:T(8,128)}) custom-call(f32[2,6,16,4096]{3,2,1,0:T(8,128)S(1)} %copy-done.1, f32[16,4096]{1,0:T(8,128)S(1)} %copy-done.3, f32[416,128]{1,0:T(8,128)S(1)} %collective-permute-done.fy_lo, f32[416,128]{1,0:T(8,128)S(1)} %collective-permute-done.1.fy_hi), custom_call_target="tpu_custom_call" | custom-call | tf_op jit(solution)/shard_map/pack_forward_x/pallas_call | solution.py:379
  19.2 1.9 %collective-permute-start.2 = (f32[1872,128]{1,0:T(8,128)}, f32[1872,128]{1,0:T(8,128)S(1)}, u32[]{:S(2)}, u32[]{:S(2)}) collective-permute-start(f32[1872,128]{1,0:T(8,128)} %get-tuple-element.15), channel_id=1, source_target_pairs={{0,16},{16,32},{32,48},{48,64},{64,80},{80,96},{96,112},{1,17},{17... | collective-permute-start | bytes 2875400 | tf_op jit(solution)/shard_map/ppermute | solution.py:30
  21.1 0.0 copy-start.12
  21.1 0.0 copy-start.13
  21.1 3.6 %collective-permute-start.3 = (f32[1872,128]{1,0:T(8,128)}, f32[1872,128]{1,0:T(8,128)S(1)}, u32[]{:S(2)}, u32[]{:S(2)}) collective-permute-start(f32[1872,128]{1,0:T(8,128)} %get-tuple-element.16), channel_id=1, source_target_pairs={{16,0},{32,16},{48,32},{64,48},{80,64},{96,80},{112,96},{17,1},{33... | collective-permute-start | bytes 2875400 | tf_op jit(solution)/shard_map/ppermute | solution.py:30
  24.8 0.0 collective-permute-done.4.ax_lo
  24.8 0.0 copy-start.4
  24.8 0.4 collective-permute-done.5.ax_hi
  25.2 0.0 copy-start.5
  25.2 0.2 pack_adjoint_y.1
  25.4 0.0 copy-done.6
  25.4 0.0 copy-done.7
  25.4 0.3 copy-done.4
  25.7 0.4 copy-done.5
  26.0 4.6 %collective-permute-start.6 = (f32[576,128]{1,0:T(8,128)S(1)}, f32[576,128]{1,0:T(8,128)S(1)}, u32[]{:S(2)}, u32[]{:S(2)}) collective-permute-start(f32[576,128]{1,0:T(8,128)S(1)} %get-tuple-element.19), channel_id=1, source_target_pairs={{0,1},{1,2},{2,3},{3,4},{4,5},{5,6},{6,7},{7,8},{8,9},{9,10},{10,1... | collective-permute-start | bytes 884744 | tf_op jit(solution)/shard_map/ppermute | solution.py:30
  30.6 1.3 collective-permute-start.7
  31.9 0.0 copy-done.12
  31.9 0.6 reshape.10.owners
  32.6 0.0 copy-done.13
  32.6 0.6 reshape.11.slots
  33.2 0.7 stack.43.where
  33.9 2.5 %collective-permute-done.6.ay_lo = f32[576,128]{1,0:T(8,128)S(1)} collective-permute-done((f32[576,128]{1,0:T(8,128)S(1)}, f32[576,128]{1,0:T(8,128)S(1)}, u32[]{:S(2)}, u32[]{:S(2)}) %collective-permute-start.6) | collective-permute-done | bytes 294944 | tf_op jit(solution)/shard_map/ppermute | solution.py:30
  36.4 0.0 copy-start.10
  36.4 4.7 %collective-permute-done.7.ay_hi = f32[576,128]{1,0:T(8,128)S(1)} collective-permute-done((f32[576,128]{1,0:T(8,128)S(1)}, f32[576,128]{1,0:T(8,128)S(1)}, u32[]{:S(2)}, u32[]{:S(2)}) %collective-permute-start.7) | collective-permute-done | bytes 294944 | tf_op jit(solution)/shard_map/ppermute | solution.py:30
  41.1 0.0 copy-start.11
  41.1 0.0 collective-permute-done.2.fx_lo
  41.1 0.0 copy-start.8
  41.1 0.0 collective-permute-done.3.fx_hi
  41.1 0.0 copy-done.10
  41.1 0.7 copy-done.11
  41.8 0.4 copy-done.8
  42.2 0.0 copy-start.9
  42.2 0.9 copy-done.9
  43.1 60.9 %simulate.1 = f32[32,16,128]{2,1,0:T(8,128)} custom-call(s32[6]{0:T(128)} %stack.43.where, s32[64]{0:T(128)} %reshape.10.owners, s32[64]{0:T(128)} %reshape.11.slots, s32[2,3]{1,0:T(2,128)} %cells.1, f32[2,4]{1,0:T(2,128)} %wave.1, f32[2,6,16,4096]{3,2,1,0:T(8,128)} %fwd.3, f32[2,6,16,4096]{3,2,1,0:T(8,128)} %adj.3, f32[16,4096]{1,0:T(8,128)} %eps.3, ...), custom_call_target="tpu_custom_call" | custom-call | tf_op jit(solution)/shard_map/simulate/pallas_call | solution.py:413
  104.0 31.6 %all_to_all.5.arrived = f32[32,16,128]{2,1,0:T(8,128)} all-to-all(f32[32,16,128]{2,1,0:T(8,128)} %simulate.1), channel_id=1, replica_groups=mesh['src'=2,'gx'=8,'gy'=16] {'src','gy'}, dimensions={0} | all-to-all | bytes 524288 | tf_op jit(solution)/shard_map/all_to_all | solution.py:445
  135.6 1.7 %place.1 = f32[64,512]{1,0:T(8,128)} custom-call(s32[64]{0:T(128)} %bitcast.7, f32[32,16,128]{2,1,0:T(8,128)} %all_to_all.5.arrived), custom_call_target="tpu_custom_call" | custom-call | tf_op jit(solution)/shard_map/place/pallas_call | solution.py:446
Async XLA Ops:
  0.0 1.9 %copy-start = (f32[2,6,16,4096]{3,2,1,0:T(8,128)S(1)}, f32[2,6,16,4096]{3,2,1,0:T(8,128)}, u32[]{:S(2)}) copy-start(f32[2,6,16,4096]{3,2,1,0:T(8,128)} %fwd.3) | copy-start | bytes 9437188
  1.9 1.9 %copy-start.2 = (f32[2,6,16,4096]{3,2,1,0:T(8,128)S(1)}, f32[2,6,16,4096]{3,2,1,0:T(8,128)}, u32[]{:S(2)}) copy-start(f32[2,6,16,4096]{3,2,1,0:T(8,128)} %adj.3) | copy-start | bytes 9437188
  3.8 0.9 copy-start.3
  4.7 12.7 %copy-start.1 = (f32[2,6,16,4096]{3,2,1,0:T(8,128)S(1)}, f32[2,6,16,4096]{3,2,1,0:T(8,128)}, u32[]{:S(2)}) copy-start(f32[2,6,16,4096]{3,2,1,0:T(8,128)} %fwd.3) | copy-start | bytes 9437188
  5.2 10.4 %collective-permute-start = (f32[416,128]{1,0:T(8,128)S(1)}, f32[416,128]{1,0:T(8,128)S(1)}, u32[]{:S(2)}, u32[]{:S(2)}) collective-permute-start(f32[416,128]{1,0:T(8,128)S(1)} %get-tuple-element.13), channel_id=1, source_target_pairs={{0,1},{1,2},{2,3},{3,4},{4,5},{5,6},{6,7},{7,8},{8,9},{9,10},{10,1... | collective-permute-start | bytes 638984 | tf_op jit(solution)/shard_map/ppermute | solution.py:30
  8.8 8.6 %collective-permute-start.1 = (f32[416,128]{1,0:T(8,128)S(1)}, f32[416,128]{1,0:T(8,128)S(1)}, u32[]{:S(2)}, u32[]{:S(2)}) collective-permute-start(f32[416,128]{1,0:T(8,128)S(1)} %get-tuple-element.14), channel_id=1, source_target_pairs={{1,0},{2,1},{3,2},{4,3},{5,4},{6,5},{7,6},{8,7},{9,8},{10,9},{11,1... | collective-permute-start | bytes 638984 | tf_op jit(solution)/shard_map/ppermute | solution.py:30
  10.1 14.7 %collective-permute-start.4 = (f32[1536,128]{1,0:T(8,128)S(1)}, f32[1536,128]{1,0:T(8,128)S(1)}, u32[]{:S(2)}, u32[]{:S(2)}) collective-permute-start(f32[1536,128]{1,0:T(8,128)S(1)} %get-tuple-element.17), channel_id=1, source_target_pairs={{0,16},{16,32},{32,48},{48,64},{64,80},{80,96},{96,112},{1,17},{17... | collective-permute-start | bytes 2359304 | tf_op jit(solution)/shard_map/ppermute | solution.py:30
  12.0 13.1 %collective-permute-start.5 = (f32[1536,128]{1,0:T(8,128)S(1)}, f32[1536,128]{1,0:T(8,128)S(1)}, u32[]{:S(2)}, u32[]{:S(2)}) collective-permute-start(f32[1536,128]{1,0:T(8,128)S(1)} %get-tuple-element.18), channel_id=1, source_target_pairs={{16,0},{32,16},{48,32},{64,48},{80,64},{96,80},{112,96},{17,1},{33... | collective-permute-start | bytes 2359304 | tf_op jit(solution)/shard_map/ppermute | solution.py:30
  15.7 9.7 %copy-start.6 = (f32[416,128]{1,0:T(8,128)}, f32[416,128]{1,0:T(8,128)S(1)}, u32[]{:S(2)}) copy-start(f32[416,128]{1,0:T(8,128)S(1)} %collective-permute-done.fy_lo) | copy-start | bytes 638980
  17.4 8.0 %copy-start.7 = (f32[416,128]{1,0:T(8,128)}, f32[416,128]{1,0:T(8,128)S(1)}, u32[]{:S(2)}) copy-start(f32[416,128]{1,0:T(8,128)S(1)} %collective-permute-done.1.fy_hi) | copy-start | bytes 638980
  19.2 21.9 %collective-permute-start.2 = (f32[1872,128]{1,0:T(8,128)}, f32[1872,128]{1,0:T(8,128)S(1)}, u32[]{:S(2)}, u32[]{:S(2)}) collective-permute-start(f32[1872,128]{1,0:T(8,128)} %get-tuple-element.15), channel_id=1, source_target_pairs={{0,16},{16,32},{32,48},{48,64},{64,80},{80,96},{96,112},{1,17},{17... | collective-permute-start | bytes 2875400 | tf_op jit(solution)/shard_map/ppermute | solution.py:30
  21.1 10.8 %copy-start.12 = (s32[4,16]{1,0:T(4,128)S(1)}, s32[4,16]{1,0:T(4,128)}, u32[]{:S(2)}) copy-start(s32[4,16]{1,0:T(4,128)} %param.13) | copy-start | bytes 772
  21.1 11.5 %copy-start.13 = (s32[4,16]{1,0:T(4,128)S(1)}, s32[4,16]{1,0:T(4,128)}, u32[]{:S(2)}) copy-start(s32[4,16]{1,0:T(4,128)} %param.14) | copy-start | bytes 772
  21.1 20.0 %collective-permute-start.3 = (f32[1872,128]{1,0:T(8,128)}, f32[1872,128]{1,0:T(8,128)S(1)}, u32[]{:S(2)}, u32[]{:S(2)}) collective-permute-start(f32[1872,128]{1,0:T(8,128)} %get-tuple-element.16), channel_id=1, source_target_pairs={{16,0},{32,16},{48,32},{64,48},{80,64},{96,80},{112,96},{17,1},{33... | collective-permute-start | bytes 2875400 | tf_op jit(solution)/shard_map/ppermute | solution.py:30
  24.8 0.9 copy-start.4
  25.2 0.9 copy-start.5
  26.0 10.3 %collective-permute-start.6 = (f32[576,128]{1,0:T(8,128)S(1)}, f32[576,128]{1,0:T(8,128)S(1)}, u32[]{:S(2)}, u32[]{:S(2)}) collective-permute-start(f32[576,128]{1,0:T(8,128)S(1)} %get-tuple-element.19), channel_id=1, source_target_pairs={{0,1},{1,2},{2,3},{3,4},{4,5},{5,6},{6,7},{7,8},{8,9},{9,10},{10,1... | collective-permute-start | bytes 884744 | tf_op jit(solution)/shard_map/ppermute | solution.py:30
  30.6 10.5 %collective-permute-start.7 = (f32[576,128]{1,0:T(8,128)S(1)}, f32[576,128]{1,0:T(8,128)S(1)}, u32[]{:S(2)}, u32[]{:S(2)}) collective-permute-start(f32[576,128]{1,0:T(8,128)S(1)} %get-tuple-element.20), channel_id=1, source_target_pairs={{1,0},{2,1},{3,2},{4,3},{5,4},{6,5},{7,6},{8,7},{9,8},{10,9},{11,1... | collective-permute-start | bytes 884744 | tf_op jit(solution)/shard_map/ppermute | solution.py:30
  36.4 4.7 %copy-start.10 = (f32[576,128]{1,0:T(8,128)}, f32[576,128]{1,0:T(8,128)S(1)}, u32[]{:S(2)}) copy-start(f32[576,128]{1,0:T(8,128)S(1)} %collective-permute-done.6.ay_lo) | copy-start | bytes 884740
  41.1 0.7 copy-start.11
  41.1 1.1 copy-start.8
  42.2 1.0 copy-start.9

commit v2 on v0

v2 whole, which is shorter than its diff:
```python
import jax
import jax.numpy as jnp
from jax import lax
from jax.experimental import pallas as pl
from jax.experimental.pallas import tpu as pltpu
from jax.sharding import PartitionSpec as P

NZ = 64
STEPS = 4
HALO = 4
CX = 16
XR = CX + 2 * HALO
CY = 64
TJ = CY // 2
HY = CY // 2
TR = HY + 2 * HALO
ROWS = TR * XR
UNROLL = 4
W = 128
COURANT = 0.55
F32 = jnp.float32


def passed_along(shard, axis, by):
    count = lax.axis_size(axis)
    pairs = [(i, i + by) for i in range(count) if 0 <= i + by < count]
    return lax.ppermute(shard, axis, pairs)


def lanes(tile):
    return pl.ds(tile * W, W)


def aligned(index, step):
    return index if isinstance(index, int) else pl.multiple_of(index, step)


def pack_x(state, *rest):
    eps, up, dn = rest if len(rest) == 3 else (None, *rest)

    def put(k, get):
        for j in range(TJ):
            row = aligned((k * TJ + j) * 4, 4)
            dn[pl.ds(row, 4), :] = get(pl.ds(0, 4), lanes(j))
            up[pl.ds(row, 4), :] = get(pl.ds(CX - 4, 4), lanes(j))

    def one(k, _):
        put(k, lambda x, j: state[k // 6, k % 6, x, j])
        return 0

    lax.fori_loop(0, 12, one, 0)
    if eps is not None:
        put(12, lambda x, j: COURANT / eps[x, j])


def pack_y(own_lo, own_hi, *rest):
    eps = None
    if len(rest) == 6:
        eps, rest = rest[:2], rest[2:]
    x_lo, x_hi, up, dn = rest

    def put(k, get):
        for j in range(2):
            base = aligned((k * 2 + j) * XR, 8)
            for out, side, tile in ((dn, 0, j), (up, 1, TJ - 2 + j)):
                row = aligned((k * TJ + tile) * 4, 4)
                out[pl.ds(base, 4), :] = x_lo[pl.ds(row, 4), :]
                out[pl.ds(base + 4, CX), :] = get(side, lanes(j))
                out[pl.ds(base + 4 + CX, 4), :] = x_hi[pl.ds(row, 4), :]

    def one(k, _):
        put(k, lambda side, j: (own_lo, own_hi)[side][k // 6, k % 6, :, j])
        return 0

    lax.fori_loop(0, 12, one, 0)
    if eps is not None:
        put(12, lambda side, j: COURANT / eps[side][:, j])


def place_field(put, own, k, x_lo, x_hi, y_lo, y_hi, low):
    pieces = ((0, 4), (4, 8), (12, 8), (20, 4))

    def source(j, x, n):
        if j < 0 or j >= TJ:
            ghost, g = (y_lo, j + 2) if j < 0 else (y_hi, j - TJ)
            return ghost[pl.ds(aligned((k * 2 + g) * XR, 8) + x, n), :]
        if n == 8:
            return own(x - 4, j)
        return (x_lo if x == 0 else x_hi)[pl.ds(aligned((k * TJ + j) * 4, 4), 4), :]

    for u in range(TR // 2):
        for x, n in pieces:
            a = source(u - 2, x, n)
            b = source(u - 2 + TJ // 2, x, n)
            first = low[:n]
            put(2 * u * XR + x, jnp.where(first, a, pltpu.roll(b, NZ, 1)))
            put((2 * u + 1) * XR + x, jnp.where(first, pltpu.roll(a, NZ, 1), b))


def masks():
    lane = lax.broadcasted_iota(jnp.int32, (8, W), 1)
    return lane < NZ, (lane & (NZ - 1)) == 0, (lane & (NZ - 1)) == NZ - 1


def half_steps(where, fe, fh, factor):
    low, z_first, z_last = masks()
    row8 = lax.broadcasted_iota(jnp.int32, (8, W), 0)
    at_x0, at_x1, at_y0, at_y1 = (where[i] for i in range(4))
    coef_x = [
        jnp.where((row8 < 4) & (at_x0 == 1), 0.0, COURANT).astype(F32),
        jnp.full((8, W), COURANT, F32),
        jnp.where((row8 >= 4) & (at_x1 == 1), 0.0, COURANT).astype(F32),
    ]

    def up_z(v):
        return jnp.where(z_last, 0.0, pltpu.roll(v, W - 1, 1))

    def down_z(v):
        return jnp.where(z_first, 0.0, pltpu.roll(v, 1, 1))

    def magnetic(r):
        in_low = jnp.where((r < HALO) & (at_y0 == 1), 0.0, 1.0).astype(F32)
        in_high = jnp.where((r >= HALO + HY) & (at_y1 == 1), 0.0, 1.0).astype(F32)
        inside = jnp.where(low, in_low, in_high)
        for t in range(3):
            b = pl.multiple_of(r * XR + 8 * t, 8)
            c = coef_x[t] * inside
            for s in range(2):
                k = 3 * s
                ex = fe[k, pl.ds(b, 8), :]
                ey = fe[k + 1, pl.ds(b, 8), :]
                ez = fe[k + 2, pl.ds(b, 8), :]
                ex_y = fe[k, pl.ds(b + XR, 8), :]
                ez_y = fe[k + 2, pl.ds(b + XR, 8), :]
                ey_x = fe[k + 1, pl.ds(b + 1, 8), :]
                ez_x = fe[k + 2, pl.ds(b + 1, 8), :]
                hx = fh[k, pl.ds(b, 8), :] - c * ((ez_y - ez) - (up_z(ey) - ey))
                hy = fh[k + 1, pl.ds(b, 8), :] - c * ((up_z(ex) - ex) - (ez_x - ez))
                hz = fh[k + 2, pl.ds(b, 8), :] - c * ((ey_x - ey) - (ex_y - ex))
                fh[k, pl.ds(b, 8), :] = hx
                fh[k + 1, pl.ds(b, 8), :] = hy
                fh[k + 2, pl.ds(b, 8), :] = hz

    def electric(r, use):
        for t in range(3):
            b = pl.multiple_of(r * XR + 8 * t, 8)
            f = factor[pl.ds(b, 8), :]
            olds, news = [], []
            for s in range(2):
                k = 3 * s
                hx = fh[k, pl.ds(b, 8), :]
                hy = fh[k + 1, pl.ds(b, 8), :]
                hz = fh[k + 2, pl.ds(b, 8), :]
                hx_y = fh[k, pl.ds(b - XR, 8), :]
                hz_y = fh[k + 2, pl.ds(b - XR, 8), :]
                hy_x = fh[k + 1, pl.ds(b - 1, 8), :]
                hz_x = fh[k + 2, pl.ds(b - 1, 8), :]
                ex, ey, ez = (fe[k + c, pl.ds(b, 8), :] for c in range(3))
                nx = ex + f * ((hz - hz_y) - (hy - down_z(hy)))
                ny = ey + f * ((hx - down_z(hx)) - (hz - hz_x))
                nz = ez + f * ((hy - hy_x) - (hx - hx_y))
                fe[k, pl.ds(b, 8), :] = nx
                fe[k + 1, pl.ds(b, 8), :] = ny
                fe[k + 2, pl.ds(b, 8), :] = nz
                olds += [ex, ey, ez]
                news += [nx, ny, nz]
            use(b, olds, news)

    def over(first, last, one):
        def body(r, _):
            one(r)
            return 0

        lax.fori_loop(first, last, body, 0, unroll=UNROLL)

    def step(n, use):
        over(n, TR - 1 - n, magnetic)
        over(n + 1, TR - 1 - n, lambda r: electric(r, use))

    return step


def forward(
    where, cells, wave, state, eps, x_lo, x_hi, y_lo, y_hi, inc, factor, fe, fh
):
    low = masks()[0]

    def load(k, _):
        for ref, c in ((fe, 0), (fh, 3)):
            q = 6 * (k // 3) + k % 3 + c

            def put(r, v):
                ref[k, pl.ds(r, v.shape[0]), :] = v

            own = lambda x, j: state[k // 3, k % 3 + c, pl.ds(x, 8), lanes(j)]
            place_field(put, own, q, x_lo, x_hi, y_lo, y_hi, low)
        return 0

    lax.fori_loop(0, 6, load, 0)

    def put(r, v):
        factor[pl.ds(r, v.shape[0]), :] = v

    place_field(
        put, lambda x, j: COURANT / eps[pl.ds(x, 8), lanes(j)], 12, x_lo, x_hi, y_lo, y_hi, low
    )
    step = half_steps(where, fe, fh, factor)
    lane = lax.broadcasted_iota(jnp.int32, (1, W), 1)
    for n in range(STEPS):

        def use(b, olds, news):
            for i in range(6):
                inc[n, i, pl.ds(b, 8), :] = news[i] - olds[i]

        step(n, use)
        for s in range(2):
            x = cells[s, 0] - where[4] * CX + HALO
            y = cells[s, 1] - where[5] * CY + HALO
            for h in range(2):
                r = y - h * HY

                @pl.when((x >= 0) & (x < XR) & (r >= 0) & (r < TR))
                def _():
                    at = pl.ds(r * XR + x, 1)
                    pulse = jnp.where(lane == h * NZ + cells[s, 2], wave[s, n], 0.0).astype(F32)
                    fe[3 * s + 2, at, :] += pulse
                    inc[n, 3 * s + 2, at, :] += pulse


def adjoint(
    where, owners, slots, state, factor, inc, x_lo, x_hi, y_lo, y_hi, out, fe, fh, density, block
):
    low = masks()[0]

    def load(k, _):
        for ref, c in ((fe, 0), (fh, 3)):
            q = 6 * (k // 3) + k % 3 + c

            def put(r, v):
                ref[k, pl.ds(r, v.shape[0]), :] = v

            own = lambda x, j: state[k // 3, k % 3 + c, pl.ds(x, 8), lanes(j)]
            place_field(put, own, q, x_lo, x_hi, y_lo, y_hi, low)
        return 0

    lax.fori_loop(0, 6, load, 0)
    step = half_steps(where, fe, fh, factor)
    for n in range(STEPS):

        def use(b, olds, news):
            terms = [news[i] * inc[STEPS - 1 - n, i, pl.ds(b, 8), :] for i in range(6)]
            total = ((terms[0] + terms[1]) + terms[2]) + ((terms[3] + terms[4]) + terms[5])
            if n > 0:
                total = total + density[pl.ds(b, 8), :]
            density[pl.ds(b, 8), :] = total

        step(n, use)

    for j in range(TJ // 2):
        for t in range(2):
            g = []
            for r in (2 * j + HALO, 2 * j + HALO + 1):
                at = pl.ds(r * XR + HALO + 8 * t, 8)
                g.append(density[at, :] * (factor[at, :] * (-1.0 / COURANT)))
            for tile, v in (
                (j, jnp.where(low, g[0], pltpu.roll(g[1], NZ, 1))),
                (j + TJ // 2, jnp.where(low, pltpu.roll(g[0], NZ, 1), g[1])),
            ):
                for h in range(2):
                    b = ((2 * t + h) * (TJ // 2) + tile // 2) * 8 + tile % 2
                    block[pl.ds(b, 4, stride=2), :] = v[4 * h : 4 * h + 4]
    out[...] = jnp.zeros_like(out)

    def send(i, _):
        o = owners[i]

        @pl.when(o >= 0)
        def _():
            c = pl.multiple_of(slots[i] * 4, 4)
            b = pl.multiple_of(i * 8, 8)
            out[o, pl.ds(c, 4), :] = block[pl.ds(b, 4), :]
            out[16 + o, pl.ds(c, 4), :] = block[pl.ds(b + 4, 4), :]

        return 0

    lax.fori_loop(0, 64, send, 0)


def place(rows, arrived, out, wide):
    def one(g, _):
        v = arrived[g] + arrived[16 + g]
        for c in range(4):
            r = pl.multiple_of(rows[g * 4 + c] * 4, 4)
            wide[pl.ds(r, 4), :] = v[c * 4 : c * 4 + 4]
        return 0

    lax.fori_loop(0, 16, one, 0)
    for i in range(8):
        for q in range(4):
            out[8 * i : 8 * i + 8, lanes(q)] = wide[pl.ds(32 * i + q, 8, stride=4), :]


FULL = pl.BlockSpec(memory_space=pltpu.VMEM)
SCALARS = pl.BlockSpec(memory_space=pltpu.SMEM)


def buf(*shape):
    return jax.ShapeDtypeStruct(shape, F32)


def call(kernel, n_scalars, n_arrays, outs, scratch=(), mib=24, us=2):
    return pl.pallas_call(
        kernel,
        in_specs=[SCALARS] * n_scalars + [FULL] * n_arrays,
        out_specs=[FULL] * len(outs),
        out_shape=list(outs),
        scratch_shapes=[pltpu.VMEM(shape, F32) for shape in scratch],
        compiler_params=pltpu.CompilerParams(vmem_limit_bytes=mib << 20),
        cost_estimate=pl.CostEstimate(
            flops=us * 1000000, bytes_accessed=us * 3000000, transcendentals=0
        ),
        name=kernel.__name__,
    )


def call_pack_y(n_own, count, rows):
    strip = (2, 6, CX, 2 * W)
    whole = lambda n: pl.BlockSpec((n, W), lambda i: (0, 0))
    specs = [
        pl.BlockSpec(strip, lambda i: (0, 0, 0, 0)),
        pl.BlockSpec(strip, lambda i: (0, 0, 0, TJ // 2 - 1)),
    ]
    if count == 13:
        specs += [
            pl.BlockSpec((CX, 2 * W), lambda i: (0, 0)),
            pl.BlockSpec((CX, 2 * W), lambda i: (0, TJ // 2 - 1)),
        ]
    return pl.pallas_call(
        pack_y,
        grid=(1,),
        in_specs=specs + [whole(count * TJ * 4)] * 2,
        out_specs=[whole(rows)] * 2,
        out_shape=[buf(rows, W)] * 2,
        compiler_params=pltpu.CompilerParams(vmem_limit_bytes=24 << 20),
        name="pack_y",
    )


FIELD = (6, ROWS, W)
SENT = (32, 16, W)


def call_forward():
    return call(forward, 3, 6, [buf(STEPS, *FIELD), buf(ROWS, W)], [FIELD, FIELD], 32, 15)


def call_adjoint():
    return call(adjoint, 3, 7, [buf(*SENT)], [FIELD, FIELD, (ROWS, W), (64 * 8, W)], 36, 15)


def per_device(
    forward_state,
    adjoint_state,
    permittivity,
    waveform,
    source_cell,
    block_owner,
    block_slot,
    owner_rows,
):
    gx, gy = lax.axis_index("gx"), lax.axis_index("gy")
    where = jnp.stack(
        [
            gx == 0,
            gx == lax.axis_size("gx") - 1,
            gy == 0,
            gy == lax.axis_size("gy") - 1,
            gx,
            gy,
        ]
    ).astype(jnp.int32)

    fx_up, fx_dn = call(pack_x, 0, 2, [buf(13 * TJ * 4, W)] * 2)(forward_state, permittivity)
    fx_lo, fx_hi = passed_along(fx_up, "gx", 1), passed_along(fx_dn, "gx", -1)
    ax_up, ax_dn = call(pack_x, 0, 1, [buf(12 * TJ * 4, W)] * 2)(adjoint_state)
    ax_lo, ax_hi = passed_along(ax_up, "gx", 1), passed_along(ax_dn, "gx", -1)

    fy_up, fy_dn = call_pack_y(4, 13, 13 * 2 * XR)(
        forward_state, forward_state, permittivity, permittivity, fx_lo, fx_hi
    )
    fy_lo, fy_hi = passed_along(fy_up, "gy", 1), passed_along(fy_dn, "gy", -1)
    ay_up, ay_dn = call_pack_y(2, 12, 12 * 2 * XR)(adjoint_state, adjoint_state, ax_lo, ax_hi)
    ay_lo, ay_hi = passed_along(ay_up, "gy", 1), passed_along(ay_dn, "gy", -1)

    inc, factor = call_forward()(
        where, source_cell, waveform, forward_state, permittivity, fx_lo, fx_hi, fy_lo, fy_hi
    )
    (outgoing,) = call_adjoint()(
        where,
        block_owner.reshape(-1),
        block_slot.reshape(-1),
        adjoint_state,
        factor,
        inc,
        ax_lo,
        ax_hi,
        ay_lo,
        ay_hi,
    )
    arrived = lax.all_to_all(outgoing, ("src", "gy"), 0, 0, tiled=True)
    (placed,) = call(place, 1, 1, [buf(64, 512)], [(256, W)])(owner_rows.reshape(-1), arrived)
    return placed


def solution(mesh):
    in_specs = (
        P("src", None, "gx", "gy"),
        P("src", None, "gx", "gy"),
        P("gx", "gy"),
        P("src", None),
        P("src", None),
        P("gx", "gy"),
        P("gx", "gy"),
        P(("gx", "gy"), None),
    )
    out_specs = P(("gx", "gy"), "src")
    return jax.shard_map(
        per_device, mesh=mesh, in_specs=in_specs, out_specs=out_specs, check_vma=False
    )
```

time: 357 us -> 107 us (0.30); the launches traced: 353 us -> 107 us
  local copies, waits for them, and re-layouts: 122 us -> 16 us
  starting transfers between devices: 113 us -> 22.2 us
  other arithmetic: 71.6 us -> 0 us
  Pallas kernels: 0 us -> 33.6 us
  waiting for transfers between devices: 26.9 us -> 5.53 us
  blocking collectives: 17.4 us -> 29.2 us
    ppermute x32 -> x8, starting transfers between devices: 98.2 us -> 22.2 us  [passed_along(): return lax.ppermute(shard, axis, pairs)]
    slice x81 -> x0, local copies, waits for them, and re-layouts: 62.8 us -> none  [the longest x16 21.3 us: upper_y(): return jnp.concatenate([values[..., z_cells:], ghosts], axis=-1)]
    pallas_call x0 -> x7, Pallas kernels: none -> 33.6 us  [the longest x1 15.1 us: per_device(): call_adjoint()]
    sub x11 -> x0, other arithmetic: 26.8 us -> none  [the longest x8 23.2 us: magnetic_update(): magnetic[0]]
    reduce_sum x4 -> x0, other arithmetic: 16.1 us -> none  [the longest x3 16 us: per_device(): density = density + jnp.sum(intersection, axis=0)]
    another operation x62 -> x1, local copies, waits for them, and re-layouts: 15.6 us -> 0.08 us  [per_device(): jnp.stack([gx == 0, gx == lax.axis_size('gx') - 1, gy == 0, gy == lax.axi...]
    all_to_all x1 -> x0, starting transfers between devices: 15 us -> none  [per_device(): lax.all_to_all(lax.all_to_all(sectioned, 'src', split_axis=3, concat_axis...]
    another operation x32 -> x0, other arithmetic: 13.3 us -> none  [the longest x8 5.79 us: upper_ghosts(): planes = jnp.stack([electric[1][:, :1, :], electric[2][:, :1, :]], axis=1)]
  transfers between devices with their start and end apart: 33 -> 8, of which waited for: 14 -> 4; matrix products, arithmetic and copies ran while one was open for 27% -> 0% of each run, Pallas kernels for 0% -> 16%
where the time goes in v2:
time: 107 us
  Pallas kernels  33.6 us (31%)
  blocking collectives  29.2 us (27%)
  starting transfers between devices  22.2 us (21%)
  local copies, waits for them, and re-layouts  16 us (15%)
  waiting for transfers between devices  5.53 us (5%)
    all_to_all x1, blocking collectives, per_device(): arrived = lax.all_to_all(outgoing, ('src', 'gy'), 0, 0, tiled=True)  29.2 us
    ppermute x8, starting transfers between devices, passed_along(): return lax.ppermute(shard, axis, pairs)  22.2 us
    unnamed x42, local copies, waits for them, and re-layouts  15.8 us
    pallas_call x1, Pallas kernels, per_device(): call_adjoint()  15.1 us
    pallas_call x1, Pallas kernels, per_device(): call_forward()  14 us
    ppermute x8, waiting for transfers between devices, passed_along(): return lax.ppermute(shard, axis, pairs)  5.53 us
  transfers between devices with their start and end apart: 8, of which 4 were waited for; matrix products, arithmetic and copies ran while one was open for 0% of the time, Pallas kernels for 16%

profile of v2, /device:TPU:32, one launch (start us, length us, event | category | flops | bytes accessed | tf_op | source)
XLA Modules:
  0.0 106.7 jit_solution(15105517483688671670)
XLA Ops:
  0.0 0.0 copy-start
  0.0 1.9 %copy-done = f32[2,6,16,4096]{3,2,1,0:T(8,128)S(1)} copy-done((f32[2,6,16,4096]{3,2,1,0:T(8,128)S(1)}, f32[2,6,16,4096]{3,2,1,0:T(8,128)}, u32[]{:S(2)}) %copy-start) | copy-done | bytes 3145752
  1.9 0.0 copy-start.6
  1.9 0.9 copy-done.6
  2.8 0.0 copy-start.1
  2.8 0.0 copy-start.7
  2.8 0.5 pack_x.2
  3.3 2.1 %collective-permute-start = (f32[1664,128]{1,0:T(8,128)S(1)}, f32[1664,128]{1,0:T(8,128)S(1)}, u32[]{:S(2)}, u32[]{:S(2)}) collective-permute-start(f32[1664,128]{1,0:T(8,128)S(1)} %get-tuple-element.15), channel_id=1, source_target_pairs={{0,16},{16,32},{32,48},{48,64},{64,80},{80,96},{96,112},{1,17},{17... | collective-permute-start | bytes 2555912 | tf_op jit(solution)/shard_map/ppermute | solution.py:27
  5.4 3.6 %collective-permute-start.1 = (f32[1664,128]{1,0:T(8,128)S(1)}, f32[1664,128]{1,0:T(8,128)S(1)}, u32[]{:S(2)}, u32[]{:S(2)}) collective-permute-start(f32[1664,128]{1,0:T(8,128)S(1)} %get-tuple-element.16), channel_id=1, source_target_pairs={{16,0},{32,16},{48,32},{64,48},{80,64},{96,80},{112,96},{17,1},{33... | collective-permute-start | bytes 2555912 | tf_op jit(solution)/shard_map/ppermute | solution.py:27
  9.1 0.0 copy-start.2
  9.1 1.9 %copy-done.2 = f32[2,6,16,4096]{3,2,1,0:T(8,128)S(1)} copy-done((f32[2,6,16,4096]{3,2,1,0:T(8,128)S(1)}, f32[2,6,16,4096]{3,2,1,0:T(8,128)}, u32[]{:S(2)}) %copy-start.2) | copy-done | bytes 3145752
  10.9 0.5 pack_x.3
  11.4 2.2 %collective-permute-start.4 = (f32[1536,128]{1,0:T(8,128)S(1)}, f32[1536,128]{1,0:T(8,128)S(1)}, u32[]{:S(2)}, u32[]{:S(2)}) collective-permute-start(f32[1536,128]{1,0:T(8,128)S(1)} %get-tuple-element.21), channel_id=1, source_target_pairs={{0,16},{16,32},{32,48},{48,64},{64,80},{80,96},{96,112},{1,17},{17... | collective-permute-start | bytes 2359304 | tf_op jit(solution)/shard_map/ppermute | solution.py:27
  13.6 3.4 %collective-permute-start.5 = (f32[1536,128]{1,0:T(8,128)S(1)}, f32[1536,128]{1,0:T(8,128)S(1)}, u32[]{:S(2)}, u32[]{:S(2)}) collective-permute-start(f32[1536,128]{1,0:T(8,128)S(1)} %get-tuple-element.22), channel_id=1, source_target_pairs={{16,0},{32,16},{48,32},{64,48},{80,64},{96,80},{112,96},{17,1},{33... | collective-permute-start | bytes 2359304 | tf_op jit(solution)/shard_map/ppermute | solution.py:27
  17.0 0.5 collective-permute-done.rest_2_.x_lo
  17.5 1.8 %collective-permute-done.1.rest_3_.x_hi = f32[1664,128]{1,0:T(8,128)S(1)} collective-permute-done((f32[1664,128]{1,0:T(8,128)S(1)}, f32[1664,128]{1,0:T(8,128)S(1)}, u32[]{:S(2)}, u32[]{:S(2)}) %collective-permute-start.1) | collective-permute-done | bytes 852000 | tf_op jit(solution)/shard_map/ppermute | solution.py:27
  19.2 0.0 copy-done.1
  19.2 0.0 copy-done.7
  19.2 0.0 copy-start.10
  19.2 1.1 %pack_y.2 = (f32[624,128]{1,0:T(8,128)}, f32[624,128]{1,0:T(8,128)}) custom-call(f32[2,6,16,4096]{3,2,1,0:T(8,128)S(1)} %copy-done.1, f32[2,6,16,4096]{3,2,1,0:T(8,128)S(1)} %copy-done.1, f32[16,4096]{1,0:T(8,128)S(1)} %copy-done.7, f32[16,4096]{1,0:T(8,128)S(1)} %copy-done.7, f32[1664,128]{1,0:T(8,128)S(1)} %collective-permute-done.rest_2_.x_lo, ...), custom_call_target="tpu_custom_call" | custom-call | tf_op jit(solution)/shard_map/pack_y/pallas_call | solution.py:388
  20.4 0.0 copy-done.8
  20.4 0.0 copy-done.10
  20.4 4.1 %collective-permute-start.2 = (f32[624,128]{1,0:T(8,128)}, f32[624,128]{1,0:T(8,128)}, u32[]{:S(2)}, u32[]{:S(2)}) collective-permute-start(f32[624,128]{1,0:T(8,128)} %get-tuple-element.17), channel_id=1, source_target_pairs={{0,1},{1,2},{2,3},{3,4},{4,5},{5,6},{6,7},{7,8},{8,9},{9,10},{10,1... | collective-permute-start | bytes 958472 | tf_op jit(solution)/shard_map/ppermute | solution.py:27
  24.5 0.0 copy-start.19
  24.5 0.0 copy-start.20
  24.5 0.0 copy-start.16
  24.5 0.0 copy-start.17
  24.5 1.4 %collective-permute-start.3 = (f32[624,128]{1,0:T(8,128)}, f32[624,128]{1,0:T(8,128)}, u32[]{:S(2)}, u32[]{:S(2)}) collective-permute-start(f32[624,128]{1,0:T(8,128)} %get-tuple-element.18), channel_id=1, source_target_pairs={{1,0},{2,1},{3,2},{4,3},{5,4},{6,5},{7,6},{8,7},{9,8},{10,9},{11,1... | collective-permute-start | bytes 958472 | tf_op jit(solution)/shard_map/ppermute | solution.py:27
  25.9 0.0 collective-permute-done.4.rest_0_.x_lo
  25.9 0.0 copy-start.12
  26.0 1.7 %collective-permute-done.5.rest_1_.x_hi = f32[1536,128]{1,0:T(8,128)S(1)} collective-permute-done((f32[1536,128]{1,0:T(8,128)S(1)}, f32[1536,128]{1,0:T(8,128)S(1)}, u32[]{:S(2)}, u32[]{:S(2)}) %collective-permute-start.5) | collective-permute-done | bytes 786464 | tf_op jit(solution)/shard_map/ppermute | solution.py:27
  27.7 0.0 copy-start.14
  27.7 1.1 %pack_y.3 = (f32[576,128]{1,0:T(8,128)}, f32[576,128]{1,0:T(8,128)}) custom-call(f32[2,6,16,4096]{3,2,1,0:T(8,128)S(1)} %copy-done.2, f32[2,6,16,4096]{3,2,1,0:T(8,128)S(1)} %copy-done.2, f32[1536,128]{1,0:T(8,128)S(1)} %collective-permute-done.4.rest_0_.x_lo, f32[1536,128]{1,0:T(8,128)S(1)} %collective-permute-done.5.rest_1_.x_hi), custom_call_target="tpu_custom_call" | custom-call | tf_op jit(solution)/shard_map/pack_y/pallas_call | solution.py:392
  28.8 0.0 copy-done.12
  28.8 0.0 copy-done.14
  28.8 4.1 %collective-permute-start.6 = (f32[576,128]{1,0:T(8,128)}, f32[576,128]{1,0:T(8,128)}, u32[]{:S(2)}, u32[]{:S(2)}) collective-permute-start(f32[576,128]{1,0:T(8,128)} %get-tuple-element.23), channel_id=1, source_target_pairs={{0,1},{1,2},{2,3},{3,4},{4,5},{5,6},{6,7},{7,8},{8,9},{9,10},{10,1... | collective-permute-start | bytes 884744 | tf_op jit(solution)/shard_map/ppermute | solution.py:27
  32.9 1.3 %collective-permute-start.7 = (f32[576,128]{1,0:T(8,128)}, f32[576,128]{1,0:T(8,128)}, u32[]{:S(2)}, u32[]{:S(2)}) collective-permute-start(f32[576,128]{1,0:T(8,128)} %get-tuple-element.24), channel_id=1, source_target_pairs={{1,0},{2,1},{3,2},{4,3},{5,4},{6,5},{7,6},{8,7},{9,8},{10,9},{11,1... | collective-permute-start | bytes 884744 | tf_op jit(solution)/shard_map/ppermute | solution.py:27
  34.2 0.0 copy-done.19
  34.2 0.1 reshape.10.owners
  34.3 0.0 copy-done.20
  34.3 0.1 reshape.11.slots
  34.3 0.1 stack.43.where
  34.4 0.0 collective-permute-done.2.y_lo
  34.4 1.6 %collective-permute-done.3.y_hi = f32[624,128]{1,0:T(8,128)} collective-permute-done((f32[624,128]{1,0:T(8,128)}, f32[624,128]{1,0:T(8,128)}, u32[]{:S(2)}, u32[]{:S(2)}) %collective-permute-start.3) | collective-permute-done | bytes 319520 | tf_op jit(solution)/shard_map/ppermute | solution.py:27
  36.0 0.0 copy-done.16
  36.0 0.0 copy-done.17
  36.0 0.0 copy-start.9
  36.0 1.2 %copy-done.9 = f32[1664,128]{1,0:T(8,128)S(1)} copy-done((f32[1664,128]{1,0:T(8,128)S(1)}, f32[1664,128]{1,0:T(8,128)}, u32[]{:S(2)}) %copy-start.9) | copy-done | bytes 851992
  37.1 0.0 copy-start.11
  37.2 1.2 %copy-done.11 = f32[1664,128]{1,0:T(8,128)S(1)} copy-done((f32[1664,128]{1,0:T(8,128)S(1)}, f32[1664,128]{1,0:T(8,128)}, u32[]{:S(2)}) %copy-start.11) | copy-done | bytes 851992
  38.3 14.0 %forward.1 = (f32[4,6,960,128]{3,2,1,0:T(8,128)S(1)}, f32[960,128]{1,0:T(8,128)S(1)}) custom-call(s32[6]{0:T(128)S(1)} %stack.43.where, s32[2,3]{1,0:T(2,128)S(1)} %copy-done.16, f32[2,4]{1,0:T(2,128)S(1)} %copy-done.17, f32[2,6,16,4096]{3,2,1,0:T(8,128)S(1)} %copy-done.1, f32[16,4096]{1,0:T(8,128)S(1)} %copy-done.7, f32[1664,128]{1,0:T(8,128)S(1)} %copy-done.9, ...), custom_call_target="tpu_custom_call" | custom-call | flops 15000000 | bytes 45000000 | tf_op jit(solution)/shard_map/forward/pallas_call | solution.py:395
  52.3 0.0 copy-start.4
  52.3 4.3 %copy-done.4 = f32[4,6,960,128]{3,2,1,0:T(8,128)} copy-done((f32[4,6,960,128]{3,2,1,0:T(8,128)}, f32[4,6,960,128]{3,2,1,0:T(8,128)S(1)}, u32[]{:S(2)}) %copy-start.4) | copy-done | bytes 11796504
  56.6 0.0 collective-permute-done.6.y_lo
  56.6 0.0 collective-permute-done.7.y_hi
  56.6 0.0 copy-done.3
  56.7 0.0 copy-done.13
  56.7 0.0 copy-done.15
  56.7 0.0 copy-start.5
  56.7 4.3 %copy-done.5 = f32[4,6,960,128]{3,2,1,0:T(8,128)S(1)} copy-done((f32[4,6,960,128]{3,2,1,0:T(8,128)S(1)}, f32[4,6,960,128]{3,2,1,0:T(8,128)}, u32[]{:S(2)}) %copy-start.5) | copy-done | bytes 11796504
  61.0 15.1 %adjoint.1 = f32[32,16,128]{2,1,0:T(8,128)S(1)} custom-call(s32[6]{0:T(128)S(1)} %stack.43.where, s32[64]{0:T(128)S(1)} %reshape.10.owners, s32[64]{0:T(128)S(1)} %reshape.11.slots, f32[2,6,16,4096]{3,2,1,0:T(8,128)S(1)} %copy-done.3, f32[960,128]{1,0:T(8,128)S(1)} %get-tuple-element.19.factor, f32[4,6,960,128]{3,2,1,0:T(8,128)S(1)} %copy-done.5, ...), custom_call_target="tpu_custom_call" | custom-call | flops 15000000 | bytes 45000000 | tf_op jit(solution)/shard_map/adjoint/pallas_call | solution.py:398
  76.1 29.2 %all_to_all.5.arrived = f32[32,16,128]{2,1,0:T(8,128)S(1)} all-to-all(f32[32,16,128]{2,1,0:T(8,128)S(1)} %adjoint.1), channel_id=1, replica_groups=mesh['src'=2,'gx'=8,'gy'=16] {'src','gy'}, dimensions={0} | all-to-all | bytes 524288 | tf_op jit(solution)/shard_map/all_to_all | solution.py:410
  105.4 0.0 copy-done.18
  105.4 1.3 %place.1 = f32[64,512]{1,0:T(8,128)} custom-call(s32[64]{0:T(128)S(1)} %bitcast.7, f32[32,16,128]{2,1,0:T(8,128)S(1)} %all_to_all.5.arrived), custom_call_target="tpu_custom_call" | custom-call | flops 2000000 | bytes 6000000 | tf_op jit(solution)/shard_map/place/pallas_call | solution.py:411
  (5 shorter events, 0.0 us)
Async XLA Ops:
  0.0 1.9 %copy-start = (f32[2,6,16,4096]{3,2,1,0:T(8,128)S(1)}, f32[2,6,16,4096]{3,2,1,0:T(8,128)}, u32[]{:S(2)}) copy-start(f32[2,6,16,4096]{3,2,1,0:T(8,128)} %state.5) | copy-start | bytes 9437188
  1.9 0.9 copy-start.6
  2.8 16.4 %copy-start.1 = (f32[2,6,16,4096]{3,2,1,0:T(8,128)S(1)}, f32[2,6,16,4096]{3,2,1,0:T(8,128)}, u32[]{:S(2)}) copy-start(f32[2,6,16,4096]{3,2,1,0:T(8,128)} %state.5) | copy-start | bytes 9437188
  2.8 16.4 %copy-start.7 = (f32[16,4096]{1,0:T(8,128)S(1)}, f32[16,4096]{1,0:T(8,128)}, u32[]{:S(2)}) copy-start(f32[16,4096]{1,0:T(8,128)} %eps.1) | copy-start | bytes 786436
  3.3 14.1 %collective-permute-start = (f32[1664,128]{1,0:T(8,128)S(1)}, f32[1664,128]{1,0:T(8,128)S(1)}, u32[]{:S(2)}, u32[]{:S(2)}) collective-permute-start(f32[1664,128]{1,0:T(8,128)S(1)} %get-tuple-element.15), channel_id=1, source_target_pairs={{0,16},{16,32},{32,48},{48,64},{64,80},{80,96},{96,112},{1,17},{17... | collective-permute-start | bytes 2555912 | tf_op jit(solution)/shard_map/ppermute | solution.py:27
  5.4 13.8 %collective-permute-start.1 = (f32[1664,128]{1,0:T(8,128)S(1)}, f32[1664,128]{1,0:T(8,128)S(1)}, u32[]{:S(2)}, u32[]{:S(2)}) collective-permute-start(f32[1664,128]{1,0:T(8,128)S(1)} %get-tuple-element.16), channel_id=1, source_target_pairs={{16,0},{32,16},{48,32},{64,48},{80,64},{96,80},{112,96},{17,1},{33... | collective-permute-start | bytes 2555912 | tf_op jit(solution)/shard_map/ppermute | solution.py:27
  9.1 1.9 %copy-start.2 = (f32[2,6,16,4096]{3,2,1,0:T(8,128)S(1)}, f32[2,6,16,4096]{3,2,1,0:T(8,128)}, u32[]{:S(2)}) copy-start(f32[2,6,16,4096]{3,2,1,0:T(8,128)} %state.7) | copy-start | bytes 9437188
  11.4 14.5 %collective-permute-start.4 = (f32[1536,128]{1,0:T(8,128)S(1)}, f32[1536,128]{1,0:T(8,128)S(1)}, u32[]{:S(2)}, u32[]{:S(2)}) collective-permute-start(f32[1536,128]{1,0:T(8,128)S(1)} %get-tuple-element.21), channel_id=1, source_target_pairs={{0,16},{16,32},{32,48},{48,64},{64,80},{80,96},{96,112},{1,17},{17... | collective-permute-start | bytes 2359304 | tf_op jit(solution)/shard_map/ppermute | solution.py:27
  13.6 14.0 %collective-permute-start.5 = (f32[1536,128]{1,0:T(8,128)S(1)}, f32[1536,128]{1,0:T(8,128)S(1)}, u32[]{:S(2)}, u32[]{:S(2)}) collective-permute-start(f32[1536,128]{1,0:T(8,128)S(1)} %get-tuple-element.22), channel_id=1, source_target_pairs={{16,0},{32,16},{48,32},{64,48},{80,64},{96,80},{112,96},{17,1},{33... | collective-permute-start | bytes 2359304 | tf_op jit(solution)/shard_map/ppermute | solution.py:27
  17.5 2.9 %copy-start.8 = (f32[1664,128]{1,0:T(8,128)}, f32[1664,128]{1,0:T(8,128)S(1)}, u32[]{:S(2)}) copy-start(f32[1664,128]{1,0:T(8,128)S(1)} %collective-permute-done.rest_2_.x_lo) | copy-start | bytes 2555908
  19.2 1.1 %copy-start.10 = (f32[1664,128]{1,0:T(8,128)}, f32[1664,128]{1,0:T(8,128)S(1)}, u32[]{:S(2)}) copy-start(f32[1664,128]{1,0:T(8,128)S(1)} %collective-permute-done.1.rest_3_.x_hi) | copy-start | bytes 2555908
  20.4 14.0 %collective-permute-start.2 = (f32[624,128]{1,0:T(8,128)}, f32[624,128]{1,0:T(8,128)}, u32[]{:S(2)}, u32[]{:S(2)}) collective-permute-start(f32[624,128]{1,0:T(8,128)} %get-tuple-element.17), channel_id=1, source_target_pairs={{0,1},{1,2},{2,3},{3,4},{4,5},{5,6},{6,7},{7,8},{8,9},{9,10},{10,1... | collective-permute-start | bytes 958472 | tf_op jit(solution)/shard_map/ppermute | solution.py:27
  24.5 9.7 %copy-start.19 = (s32[4,16]{1,0:T(4,128)S(1)}, s32[4,16]{1,0:T(4,128)}, u32[]{:S(2)}) copy-start(s32[4,16]{1,0:T(4,128)} %param.13) | copy-start | bytes 772
  24.5 9.8 %copy-start.20 = (s32[4,16]{1,0:T(4,128)S(1)}, s32[4,16]{1,0:T(4,128)}, u32[]{:S(2)}) copy-start(s32[4,16]{1,0:T(4,128)} %param.14) | copy-start | bytes 772
  24.5 11.5 %copy-start.16 = (s32[2,3]{1,0:T(2,128)S(1)}, s32[2,3]{1,0:T(2,128)}, u32[]{:S(2)}) copy-start(s32[2,3]{1,0:T(2,128)} %cells.1) | copy-start | bytes 76
  24.5 11.5 %copy-start.17 = (f32[2,4]{1,0:T(2,128)S(1)}, f32[2,4]{1,0:T(2,128)}, u32[]{:S(2)}) copy-start(f32[2,4]{1,0:T(2,128)} %wave.1) | copy-start | bytes 100
  24.5 11.5 %collective-permute-start.3 = (f32[624,128]{1,0:T(8,128)}, f32[624,128]{1,0:T(8,128)}, u32[]{:S(2)}, u32[]{:S(2)}) collective-permute-start(f32[624,128]{1,0:T(8,128)} %get-tuple-element.18), channel_id=1, source_target_pairs={{1,0},{2,1},{3,2},{4,3},{5,4},{6,5},{7,6},{8,7},{9,8},{10,9},{11,1... | collective-permute-start | bytes 958472 | tf_op jit(solution)/shard_map/ppermute | solution.py:27
  25.9 2.8 %copy-start.12 = (f32[1536,128]{1,0:T(8,128)}, f32[1536,128]{1,0:T(8,128)S(1)}, u32[]{:S(2)}) copy-start(f32[1536,128]{1,0:T(8,128)S(1)} %collective-permute-done.4.rest_0_.x_lo) | copy-start | bytes 2359300
  27.7 1.1 %copy-start.14 = (f32[1536,128]{1,0:T(8,128)}, f32[1536,128]{1,0:T(8,128)S(1)}, u32[]{:S(2)}) copy-start(f32[1536,128]{1,0:T(8,128)S(1)} %collective-permute-done.5.rest_1_.x_hi) | copy-start | bytes 2359300
  28.8 27.9 %collective-permute-start.6 = (f32[576,128]{1,0:T(8,128)}, f32[576,128]{1,0:T(8,128)}, u32[]{:S(2)}, u32[]{:S(2)}) collective-permute-start(f32[576,128]{1,0:T(8,128)} %get-tuple-element.23), channel_id=1, source_target_pairs={{0,1},{1,2},{2,3},{3,4},{4,5},{5,6},{6,7},{7,8},{8,9},{9,10},{10,1... | collective-permute-start | bytes 884744 | tf_op jit(solution)/shard_map/ppermute | solution.py:27
  32.9 23.8 %collective-permute-start.7 = (f32[576,128]{1,0:T(8,128)}, f32[576,128]{1,0:T(8,128)}, u32[]{:S(2)}, u32[]{:S(2)}) collective-permute-start(f32[576,128]{1,0:T(8,128)} %get-tuple-element.24), channel_id=1, source_target_pairs={{1,0},{2,1},{3,2},{4,3},{5,4},{6,5},{7,6},{8,7},{9,8},{10,9},{11,1... | collective-permute-start | bytes 884744 | tf_op jit(solution)/shard_map/ppermute | solution.py:27
  34.4 22.2 %copy-start.3 = (f32[2,6,16,4096]{3,2,1,0:T(8,128)S(1)}, f32[2,6,16,4096]{3,2,1,0:T(8,128)}, u32[]{:S(2)}) copy-start(f32[2,6,16,4096]{3,2,1,0:T(8,128)} %state.7) | copy-start | bytes 9437188
  36.0 1.2 %copy-start.9 = (f32[1664,128]{1,0:T(8,128)S(1)}, f32[1664,128]{1,0:T(8,128)}, u32[]{:S(2)}) copy-start(f32[1664,128]{1,0:T(8,128)} %copy-done.8) | copy-start | bytes 2555908
  37.1 1.2 %copy-start.11 = (f32[1664,128]{1,0:T(8,128)S(1)}, f32[1664,128]{1,0:T(8,128)}, u32[]{:S(2)}) copy-start(f32[1664,128]{1,0:T(8,128)} %copy-done.10) | copy-start | bytes 2555908
  38.3 18.4 %copy-start.13 = (f32[1536,128]{1,0:T(8,128)S(1)}, f32[1536,128]{1,0:T(8,128)}, u32[]{:S(2)}) copy-start(f32[1536,128]{1,0:T(8,128)} %copy-done.12) | copy-start | bytes 2359300
  38.3 18.4 %copy-start.15 = (f32[1536,128]{1,0:T(8,128)S(1)}, f32[1536,128]{1,0:T(8,128)}, u32[]{:S(2)}) copy-start(f32[1536,128]{1,0:T(8,128)} %copy-done.14) | copy-start | bytes 2359300
  52.3 4.3 %copy-start.4 = (f32[4,6,960,128]{3,2,1,0:T(8,128)}, f32[4,6,960,128]{3,2,1,0:T(8,128)S(1)}, u32[]{:S(2)}) copy-start(f32[4,6,960,128]{3,2,1,0:T(8,128)S(1)} %get-tuple-element.20.inc) | copy-start | bytes 35389444
  56.7 4.4 %copy-start.5 = (f32[4,6,960,128]{3,2,1,0:T(8,128)S(1)}, f32[4,6,960,128]{3,2,1,0:T(8,128)}, u32[]{:S(2)}) copy-start(f32[4,6,960,128]{3,2,1,0:T(8,128)} %copy-done.4) | copy-start | bytes 35389444
  61.0 44.3 %copy-start.18 = (s32[1,64]{1,0:T(1,128)S(1)}, s32[1,64]{1,0:T(1,128)}, u32[]{:S(2)}) copy-start(s32[1,64]{1,0:T(1,128)} %param.15) | copy-start | bytes 772

commit v3 on v2

--- a/solution.py
+++ b/solution.py
@@ -308,7 +308,7 @@
     return jax.ShapeDtypeStruct(shape, F32)
 
 
-def call(kernel, n_scalars, n_arrays, outs, scratch=(), mib=24, us=2):
+def call(kernel, n_scalars, n_arrays, outs, scratch=(), mib=8, us=2):
     return pl.pallas_call(
         kernel,
         in_specs=[SCALARS] * n_scalars + [FULL] * n_arrays,
@@ -341,7 +341,7 @@
         in_specs=specs + [whole(count * TJ * 4)] * 2,
         out_specs=[whole(rows)] * 2,
         out_shape=[buf(rows, W)] * 2,
-        compiler_params=pltpu.CompilerParams(vmem_limit_bytes=24 << 20),
+        compiler_params=pltpu.CompilerParams(vmem_limit_bytes=8 << 20),
         name="pack_y",
     )
 
@@ -351,11 +351,11 @@
 
 
 def call_forward():
-    return call(forward, 3, 6, [buf(STEPS, *FIELD), buf(ROWS, W)], [FIELD, FIELD], 32, 15)
+    return call(forward, 3, 6, [buf(STEPS, *FIELD), buf(ROWS, W)], [FIELD, FIELD], 12, 15)
 
 
 def call_adjoint():
-    return call(adjoint, 3, 7, [buf(*SENT)], [FIELD, FIELD, (ROWS, W), (64 * 8, W)], 36, 15)
+    return call(adjoint, 3, 7, [buf(*SENT)], [FIELD, FIELD, (ROWS, W), (64 * 8, W)], 12, 15)
 
 
 def per_device(

time: 107 us -> 98.5 us (0.921)
  local copies, waits for them, and re-layouts: 16 us -> 7.34 us
    unnamed x42 -> x38, local copies, waits for them, and re-layouts: 15.8 us -> 7.09 us
  transfers between devices with their start and end apart: 8 -> 8, of which waited for: 4 -> 4; matrix products, arithmetic and copies ran while one was open for 0% -> 0% of each run, Pallas kernels for 16% -> 17%
where the time goes in v3:
time: 98.5 us; the launch traced here: 97.9 us
  Pallas kernels  33.5 us (34%)
  blocking collectives  29.2 us (30%)
  starting transfers between devices  22.2 us (23%)
  local copies, waits for them, and re-layouts  7.34 us (7%)
  waiting for transfers between devices  5.49 us (6%)
    all_to_all x1, blocking collectives, per_device(): arrived = lax.all_to_all(outgoing, ('src', 'gy'), 0, 0, tiled=True)  29.2 us
    ppermute x8, starting transfers between devices, passed_along(): return lax.ppermute(shard, axis, pairs)  22.2 us
    pallas_call x1, Pallas kernels, per_device(): call_adjoint()  14.9 us
    pallas_call x1, Pallas kernels, per_device(): call_forward()  14 us
    unnamed x38, local copies, waits for them, and re-layouts  7.09 us
    ppermute x8, waiting for transfers between devices, passed_along(): return lax.ppermute(shard, axis, pairs)  5.49 us
  transfers between devices with their start and end apart: 8, of which 4 were waited for; matrix products, arithmetic and copies ran while one was open for 0% of the time, Pallas kernels for 17%

profile of v3, /device:TPU:32, one launch (start us, length us, event | category | flops | bytes accessed | tf_op | source)
XLA Modules:
  0.0 97.9 jit_solution(3049245158207187472)
XLA Ops:
  0.0 0.0 copy-start
  0.0 1.9 %copy-done = f32[2,6,16,4096]{3,2,1,0:T(8,128)S(1)} copy-done((f32[2,6,16,4096]{3,2,1,0:T(8,128)S(1)}, f32[2,6,16,4096]{3,2,1,0:T(8,128)}, u32[]{:S(2)}) %copy-start) | copy-done | bytes 3145752
  1.9 0.0 copy-start.4
  1.9 0.9 copy-done.4
  2.8 0.0 copy-start.1
  2.8 0.0 copy-start.5
  2.8 0.5 pack_x.2
  3.3 2.1 %collective-permute-start = (f32[1664,128]{1,0:T(8,128)S(1)}, f32[1664,128]{1,0:T(8,128)S(1)}, u32[]{:S(2)}, u32[]{:S(2)}) collective-permute-start(f32[1664,128]{1,0:T(8,128)S(1)} %get-tuple-element.15), channel_id=1, source_target_pairs={{0,16},{16,32},{32,48},{48,64},{64,80},{80,96},{96,112},{1,17},{17... | collective-permute-start | bytes 2555912 | tf_op jit(solution)/shard_map/ppermute | solution.py:27
  5.4 3.6 %collective-permute-start.1 = (f32[1664,128]{1,0:T(8,128)S(1)}, f32[1664,128]{1,0:T(8,128)S(1)}, u32[]{:S(2)}, u32[]{:S(2)}) collective-permute-start(f32[1664,128]{1,0:T(8,128)S(1)} %get-tuple-element.16), channel_id=1, source_target_pairs={{16,0},{32,16},{48,32},{64,48},{80,64},{96,80},{112,96},{17,1},{33... | collective-permute-start | bytes 2555912 | tf_op jit(solution)/shard_map/ppermute | solution.py:27
  9.1 0.0 copy-start.2
  9.1 1.9 %copy-done.2 = f32[2,6,16,4096]{3,2,1,0:T(8,128)S(1)} copy-done((f32[2,6,16,4096]{3,2,1,0:T(8,128)S(1)}, f32[2,6,16,4096]{3,2,1,0:T(8,128)}, u32[]{:S(2)}) %copy-start.2) | copy-done | bytes 3145752
  10.9 0.5 pack_x.3
  11.4 2.2 %collective-permute-start.4 = (f32[1536,128]{1,0:T(8,128)S(1)}, f32[1536,128]{1,0:T(8,128)S(1)}, u32[]{:S(2)}, u32[]{:S(2)}) collective-permute-start(f32[1536,128]{1,0:T(8,128)S(1)} %get-tuple-element.21), channel_id=1, source_target_pairs={{0,16},{16,32},{32,48},{48,64},{64,80},{80,96},{96,112},{1,17},{17... | collective-permute-start | bytes 2359304 | tf_op jit(solution)/shard_map/ppermute | solution.py:27
  13.6 3.4 %collective-permute-start.5 = (f32[1536,128]{1,0:T(8,128)S(1)}, f32[1536,128]{1,0:T(8,128)S(1)}, u32[]{:S(2)}, u32[]{:S(2)}) collective-permute-start(f32[1536,128]{1,0:T(8,128)S(1)} %get-tuple-element.22), channel_id=1, source_target_pairs={{16,0},{32,16},{48,32},{64,48},{80,64},{96,80},{112,96},{17,1},{33... | collective-permute-start | bytes 2359304 | tf_op jit(solution)/shard_map/ppermute | solution.py:27
  17.0 0.5 collective-permute-done.rest_2_.x_lo
  17.5 0.0 copy-start.6
  17.5 1.8 %collective-permute-done.1.rest_3_.x_hi = f32[1664,128]{1,0:T(8,128)S(1)} collective-permute-done((f32[1664,128]{1,0:T(8,128)S(1)}, f32[1664,128]{1,0:T(8,128)S(1)}, u32[]{:S(2)}, u32[]{:S(2)}) %collective-permute-start.1) | collective-permute-done | bytes 852000 | tf_op jit(solution)/shard_map/ppermute | solution.py:27
  19.2 0.0 copy-done.1
  19.2 0.0 copy-done.5
  19.2 0.0 copy-start.8
  19.2 1.2 %pack_y.2 = (f32[624,128]{1,0:T(8,128)}, f32[624,128]{1,0:T(8,128)}) custom-call(f32[2,6,16,4096]{3,2,1,0:T(8,128)S(1)} %copy-done.1, f32[2,6,16,4096]{3,2,1,0:T(8,128)S(1)} %copy-done.1, f32[16,4096]{1,0:T(8,128)S(1)} %copy-done.5, f32[16,4096]{1,0:T(8,128)S(1)} %copy-done.5, f32[1664,128]{1,0:T(8,128)S(1)} %collective-permute-done.rest_2_.x_lo, ...), custom_call_target="tpu_custom_call" | custom-call | tf_op jit(solution)/shard_map/pack_y/pallas_call | solution.py:388
  20.5 0.0 copy-done.6
  20.5 0.0 copy-done.8
  20.5 4.1 %collective-permute-start.2 = (f32[624,128]{1,0:T(8,128)}, f32[624,128]{1,0:T(8,128)}, u32[]{:S(2)}, u32[]{:S(2)}) collective-permute-start(f32[624,128]{1,0:T(8,128)} %get-tuple-element.17), channel_id=1, source_target_pairs={{0,1},{1,2},{2,3},{3,4},{4,5},{5,6},{6,7},{7,8},{8,9},{9,10},{10,1... | collective-permute-start | bytes 958472 | tf_op jit(solution)/shard_map/ppermute | solution.py:27
  24.6 0.0 copy-start.17
  24.6 0.0 copy-start.18
  24.6 0.0 copy-start.15
  24.6 1.4 %collective-permute-start.3 = (f32[624,128]{1,0:T(8,128)}, f32[624,128]{1,0:T(8,128)}, u32[]{:S(2)}, u32[]{:S(2)}) collective-permute-start(f32[624,128]{1,0:T(8,128)} %get-tuple-element.18), channel_id=1, source_target_pairs={{1,0},{2,1},{3,2},{4,3},{5,4},{6,5},{7,6},{8,7},{9,8},{10,9},{11,1... | collective-permute-start | bytes 958472 | tf_op jit(solution)/shard_map/ppermute | solution.py:27
  26.0 0.0 collective-permute-done.4.rest_0_.x_lo
  26.0 0.0 copy-start.10
  26.0 1.6 %collective-permute-done.5.rest_1_.x_hi = f32[1536,128]{1,0:T(8,128)S(1)} collective-permute-done((f32[1536,128]{1,0:T(8,128)S(1)}, f32[1536,128]{1,0:T(8,128)S(1)}, u32[]{:S(2)}, u32[]{:S(2)}) %collective-permute-start.5) | collective-permute-done | bytes 786464 | tf_op jit(solution)/shard_map/ppermute | solution.py:27
  27.7 0.0 copy-start.12
  27.7 1.1 %pack_y.3 = (f32[576,128]{1,0:T(8,128)}, f32[576,128]{1,0:T(8,128)}) custom-call(f32[2,6,16,4096]{3,2,1,0:T(8,128)S(1)} %copy-done.2, f32[2,6,16,4096]{3,2,1,0:T(8,128)S(1)} %copy-done.2, f32[1536,128]{1,0:T(8,128)S(1)} %collective-permute-done.4.rest_0_.x_lo, f32[1536,128]{1,0:T(8,128)S(1)} %collective-permute-done.5.rest_1_.x_hi), custom_call_target="tpu_custom_call" | custom-call | tf_op jit(solution)/shard_map/pack_y/pallas_call | solution.py:392
  28.8 0.0 copy-done.10
  28.8 0.0 copy-done.12
  28.8 4.1 %collective-permute-start.6 = (f32[576,128]{1,0:T(8,128)}, f32[576,128]{1,0:T(8,128)}, u32[]{:S(2)}, u32[]{:S(2)}) collective-permute-start(f32[576,128]{1,0:T(8,128)} %get-tuple-element.23), channel_id=1, source_target_pairs={{0,1},{1,2},{2,3},{3,4},{4,5},{5,6},{6,7},{7,8},{8,9},{9,10},{10,1... | collective-permute-start | bytes 884744 | tf_op jit(solution)/shard_map/ppermute | solution.py:27
  32.9 1.3 %collective-permute-start.7 = (f32[576,128]{1,0:T(8,128)}, f32[576,128]{1,0:T(8,128)}, u32[]{:S(2)}, u32[]{:S(2)}) collective-permute-start(f32[576,128]{1,0:T(8,128)} %get-tuple-element.24), channel_id=1, source_target_pairs={{1,0},{2,1},{3,2},{4,3},{5,4},{6,5},{7,6},{8,7},{9,8},{10,9},{11,1... | collective-permute-start | bytes 884744 | tf_op jit(solution)/shard_map/ppermute | solution.py:27
  34.2 0.0 copy-done.17
  34.2 0.1 reshape.10.owners
  34.3 0.0 copy-done.18
  34.3 0.1 reshape.11.slots
  34.4 0.1 stack.43.where
  34.5 0.0 copy-start.3
  34.5 0.0 collective-permute-done.2.y_lo
  34.5 1.6 %collective-permute-done.3.y_hi = f32[624,128]{1,0:T(8,128)} collective-permute-done((f32[624,128]{1,0:T(8,128)}, f32[624,128]{1,0:T(8,128)}, u32[]{:S(2)}, u32[]{:S(2)}) %collective-permute-start.3) | collective-permute-done | bytes 319520 | tf_op jit(solution)/shard_map/ppermute | solution.py:27
  36.1 0.0 copy-done.14
  36.1 0.0 copy-done.15
  36.1 0.0 copy-start.7
  36.1 1.2 %copy-done.7 = f32[1664,128]{1,0:T(8,128)S(1)} copy-done((f32[1664,128]{1,0:T(8,128)S(1)}, f32[1664,128]{1,0:T(8,128)}, u32[]{:S(2)}) %copy-start.7) | copy-done | bytes 851992
  37.2 0.0 copy-start.9
  37.2 1.2 %copy-done.9 = f32[1664,128]{1,0:T(8,128)S(1)} copy-done((f32[1664,128]{1,0:T(8,128)S(1)}, f32[1664,128]{1,0:T(8,128)}, u32[]{:S(2)}) %copy-start.9) | copy-done | bytes 851992
  38.4 0.0 copy-start.11
  38.4 0.0 copy-start.13
  38.4 14.0 %forward.1 = (f32[4,6,960,128]{3,2,1,0:T(8,128)S(1)}, f32[960,128]{1,0:T(8,128)S(1)}) custom-call(s32[6]{0:T(128)S(1)} %stack.43.where, s32[2,3]{1,0:T(2,128)S(1)} %copy-done.14, f32[2,4]{1,0:T(2,128)S(1)} %copy-done.15, f32[2,6,16,4096]{3,2,1,0:T(8,128)S(1)} %copy-done.1, f32[16,4096]{1,0:T(8,128)S(1)} %copy-done.5, f32[1664,128]{1,0:T(8,128)S(1)} %copy-done.7, ...), custom_call_target="tpu_custom_call" | custom-call | flops 15000000 | bytes 45000000 | tf_op jit(solution)/shard_map/forward/pallas_call | solution.py:395
  52.4 0.0 collective-permute-done.6.y_lo
  52.4 0.0 collective-permute-done.7.y_hi
  52.4 0.0 copy-done.3
  52.4 0.0 copy-done.11
  52.4 0.0 copy-done.13
  52.4 0.0 copy-start.16
  52.4 14.9 %adjoint.1 = f32[32,16,128]{2,1,0:T(8,128)S(1)} custom-call(s32[6]{0:T(128)S(1)} %stack.43.where, s32[64]{0:T(128)S(1)} %reshape.10.owners, s32[64]{0:T(128)S(1)} %reshape.11.slots, f32[2,6,16,4096]{3,2,1,0:T(8,128)S(1)} %copy-done.3, f32[960,128]{1,0:T(8,128)S(1)} %get-tuple-element.19.factor, f32[4,6,960,128]{3,2,1,0:T(8,128)S(1)} %get-tuple-element.20.inc, ...), custom_call_target="tpu_custom_call" | custom-call | flops 15000000 | bytes 45000000 | tf_op jit(solution)/shard_map/adjoint/pallas_call | solution.py:398
  67.3 29.2 %all_to_all.5.arrived = f32[32,16,128]{2,1,0:T(8,128)S(1)} all-to-all(f32[32,16,128]{2,1,0:T(8,128)S(1)} %adjoint.1), channel_id=1, replica_groups=mesh['src'=2,'gx'=8,'gy'=16] {'src','gy'}, dimensions={0} | all-to-all | bytes 524288 | tf_op jit(solution)/shard_map/all_to_all | solution.py:410
  96.6 0.0 copy-done.16
  96.6 1.3 %place.1 = f32[64,512]{1,0:T(8,128)} custom-call(s32[64]{0:T(128)S(1)} %bitcast.7, f32[32,16,128]{2,1,0:T(8,128)S(1)} %all_to_all.5.arrived), custom_call_target="tpu_custom_call" | custom-call | flops 2000000 | bytes 6000000 | tf_op jit(solution)/shard_map/place/pallas_call | solution.py:411
  (1 shorter events, 0.0 us)
Async XLA Ops:
  0.0 1.9 %copy-start = (f32[2,6,16,4096]{3,2,1,0:T(8,128)S(1)}, f32[2,6,16,4096]{3,2,1,0:T(8,128)}, u32[]{:S(2)}) copy-start(f32[2,6,16,4096]{3,2,1,0:T(8,128)} %state.5) | copy-start | bytes 9437188
  1.9 0.9 copy-start.4
  2.8 16.4 %copy-start.1 = (f32[2,6,16,4096]{3,2,1,0:T(8,128)S(1)}, f32[2,6,16,4096]{3,2,1,0:T(8,128)}, u32[]{:S(2)}) copy-start(f32[2,6,16,4096]{3,2,1,0:T(8,128)} %state.5) | copy-start | bytes 9437188
  2.8 16.4 %copy-start.5 = (f32[16,4096]{1,0:T(8,128)S(1)}, f32[16,4096]{1,0:T(8,128)}, u32[]{:S(2)}) copy-start(f32[16,4096]{1,0:T(8,128)} %eps.1) | copy-start | bytes 786436
  3.3 14.1 %collective-permute-start = (f32[1664,128]{1,0:T(8,128)S(1)}, f32[1664,128]{1,0:T(8,128)S(1)}, u32[]{:S(2)}, u32[]{:S(2)}) collective-permute-start(f32[1664,128]{1,0:T(8,128)S(1)} %get-tuple-element.15), channel_id=1, source_target_pairs={{0,16},{16,32},{32,48},{48,64},{64,80},{80,96},{96,112},{1,17},{17... | collective-permute-start | bytes 2555912 | tf_op jit(solution)/shard_map/ppermute | solution.py:27
  5.4 13.8 %collective-permute-start.1 = (f32[1664,128]{1,0:T(8,128)S(1)}, f32[1664,128]{1,0:T(8,128)S(1)}, u32[]{:S(2)}, u32[]{:S(2)}) collective-permute-start(f32[1664,128]{1,0:T(8,128)S(1)} %get-tuple-element.16), channel_id=1, source_target_pairs={{16,0},{32,16},{48,32},{64,48},{80,64},{96,80},{112,96},{17,1},{33... | collective-permute-start | bytes 2555912 | tf_op jit(solution)/shard_map/ppermute | solution.py:27
  9.1 1.9 %copy-start.2 = (f32[2,6,16,4096]{3,2,1,0:T(8,128)S(1)}, f32[2,6,16,4096]{3,2,1,0:T(8,128)}, u32[]{:S(2)}) copy-start(f32[2,6,16,4096]{3,2,1,0:T(8,128)} %state.7) | copy-start | bytes 9437188
  11.4 14.6 %collective-permute-start.4 = (f32[1536,128]{1,0:T(8,128)S(1)}, f32[1536,128]{1,0:T(8,128)S(1)}, u32[]{:S(2)}, u32[]{:S(2)}) collective-permute-start(f32[1536,128]{1,0:T(8,128)S(1)} %get-tuple-element.21), channel_id=1, source_target_pairs={{0,16},{16,32},{32,48},{48,64},{64,80},{80,96},{96,112},{1,17},{17... | collective-permute-start | bytes 2359304 | tf_op jit(solution)/shard_map/ppermute | solution.py:27
  13.6 14.0 %collective-permute-start.5 = (f32[1536,128]{1,0:T(8,128)S(1)}, f32[1536,128]{1,0:T(8,128)S(1)}, u32[]{:S(2)}, u32[]{:S(2)}) collective-permute-start(f32[1536,128]{1,0:T(8,128)S(1)} %get-tuple-element.22), channel_id=1, source_target_pairs={{16,0},{32,16},{48,32},{64,48},{80,64},{96,80},{112,96},{17,1},{33... | collective-permute-start | bytes 2359304 | tf_op jit(solution)/shard_map/ppermute | solution.py:27
  17.5 3.0 %copy-start.6 = (f32[1664,128]{1,0:T(8,128)}, f32[1664,128]{1,0:T(8,128)S(1)}, u32[]{:S(2)}) copy-start(f32[1664,128]{1,0:T(8,128)S(1)} %collective-permute-done.rest_2_.x_lo) | copy-start | bytes 2555908
  19.2 1.2 %copy-start.8 = (f32[1664,128]{1,0:T(8,128)}, f32[1664,128]{1,0:T(8,128)S(1)}, u32[]{:S(2)}) copy-start(f32[1664,128]{1,0:T(8,128)S(1)} %collective-permute-done.1.rest_3_.x_hi) | copy-start | bytes 2555908
  20.5 14.0 %collective-permute-start.2 = (f32[624,128]{1,0:T(8,128)}, f32[624,128]{1,0:T(8,128)}, u32[]{:S(2)}, u32[]{:S(2)}) collective-permute-start(f32[624,128]{1,0:T(8,128)} %get-tuple-element.17), channel_id=1, source_target_pairs={{0,1},{1,2},{2,3},{3,4},{4,5},{5,6},{6,7},{7,8},{8,9},{9,10},{10,1... | collective-permute-start | bytes 958472 | tf_op jit(solution)/shard_map/ppermute | solution.py:27
  24.6 9.6 %copy-start.17 = (s32[4,16]{1,0:T(4,128)S(1)}, s32[4,16]{1,0:T(4,128)}, u32[]{:S(2)}) copy-start(s32[4,16]{1,0:T(4,128)} %param.13) | copy-start | bytes 772
  24.6 9.7 %copy-start.18 = (s32[4,16]{1,0:T(4,128)S(1)}, s32[4,16]{1,0:T(4,128)}, u32[]{:S(2)}) copy-start(s32[4,16]{1,0:T(4,128)} %param.14) | copy-start | bytes 772
  24.6 11.5 %copy-start.14 = (s32[2,3]{1,0:T(2,128)S(1)}, s32[2,3]{1,0:T(2,128)}, u32[]{:S(2)}) copy-start(s32[2,3]{1,0:T(2,128)} %cells.1) | copy-start | bytes 76
  24.6 11.5 %copy-start.15 = (f32[2,4]{1,0:T(2,128)S(1)}, f32[2,4]{1,0:T(2,128)}, u32[]{:S(2)}) copy-start(f32[2,4]{1,0:T(2,128)} %wave.1) | copy-start | bytes 100
  24.6 11.5 %collective-permute-start.3 = (f32[624,128]{1,0:T(8,128)}, f32[624,128]{1,0:T(8,128)}, u32[]{:S(2)}, u32[]{:S(2)}) collective-permute-start(f32[624,128]{1,0:T(8,128)} %get-tuple-element.18), channel_id=1, source_target_pairs={{1,0},{2,1},{3,2},{4,3},{5,4},{6,5},{7,6},{8,7},{9,8},{10,9},{11,1... | collective-permute-start | bytes 958472 | tf_op jit(solution)/shard_map/ppermute | solution.py:27
  26.0 2.8 %copy-start.10 = (f32[1536,128]{1,0:T(8,128)}, f32[1536,128]{1,0:T(8,128)S(1)}, u32[]{:S(2)}) copy-start(f32[1536,128]{1,0:T(8,128)S(1)} %collective-permute-done.4.rest_0_.x_lo) | copy-start | bytes 2359300
  27.7 1.1 %copy-start.12 = (f32[1536,128]{1,0:T(8,128)}, f32[1536,128]{1,0:T(8,128)S(1)}, u32[]{:S(2)}) copy-start(f32[1536,128]{1,0:T(8,128)S(1)} %collective-permute-done.5.rest_1_.x_hi) | copy-start | bytes 2359300
  28.8 23.6 %collective-permute-start.6 = (f32[576,128]{1,0:T(8,128)}, f32[576,128]{1,0:T(8,128)}, u32[]{:S(2)}, u32[]{:S(2)}) collective-permute-start(f32[576,128]{1,0:T(8,128)} %get-tuple-element.23), channel_id=1, source_target_pairs={{0,1},{1,2},{2,3},{3,4},{4,5},{5,6},{6,7},{7,8},{8,9},{9,10},{10,1... | collective-permute-start | bytes 884744 | tf_op jit(solution)/shard_map/ppermute | solution.py:27
  32.9 19.5 %collective-permute-start.7 = (f32[576,128]{1,0:T(8,128)}, f32[576,128]{1,0:T(8,128)}, u32[]{:S(2)}, u32[]{:S(2)}) collective-permute-start(f32[576,128]{1,0:T(8,128)} %get-tuple-element.24), channel_id=1, source_target_pairs={{1,0},{2,1},{3,2},{4,3},{5,4},{6,5},{7,6},{8,7},{9,8},{10,9},{11,1... | collective-permute-start | bytes 884744 | tf_op jit(solution)/shard_map/ppermute | solution.py:27
  34.5 17.9 %copy-start.3 = (f32[2,6,16,4096]{3,2,1,0:T(8,128)S(1)}, f32[2,6,16,4096]{3,2,1,0:T(8,128)}, u32[]{:S(2)}) copy-start(f32[2,6,16,4096]{3,2,1,0:T(8,128)} %state.7) | copy-start | bytes 9437188
  36.1 1.2 %copy-start.7 = (f32[1664,128]{1,0:T(8,128)S(1)}, f32[1664,128]{1,0:T(8,128)}, u32[]{:S(2)}) copy-start(f32[1664,128]{1,0:T(8,128)} %copy-done.6) | copy-start | bytes 2555908
  37.2 1.2 %copy-start.9 = (f32[1664,128]{1,0:T(8,128)S(1)}, f32[1664,128]{1,0:T(8,128)}, u32[]{:S(2)}) copy-start(f32[1664,128]{1,0:T(8,128)} %copy-done.8) | copy-start | bytes 2555908
  38.4 14.0 %copy-start.11 = (f32[1536,128]{1,0:T(8,128)S(1)}, f32[1536,128]{1,0:T(8,128)}, u32[]{:S(2)}) copy-start(f32[1536,128]{1,0:T(8,128)} %copy-done.10) | copy-start | bytes 2359300
  38.4 14.0 %copy-start.13 = (f32[1536,128]{1,0:T(8,128)S(1)}, f32[1536,128]{1,0:T(8,128)}, u32[]{:S(2)}) copy-start(f32[1536,128]{1,0:T(8,128)} %copy-done.12) | copy-start | bytes 2359300
  52.4 44.1 %copy-start.16 = (s32[1,64]{1,0:T(1,128)S(1)}, s32[1,64]{1,0:T(1,128)}, u32[]{:S(2)}) copy-start(s32[1,64]{1,0:T(1,128)} %param.15) | copy-start | bytes 772

commit v4 on v3

v4 whole, which is shorter than its diff:
```python
import jax
import jax.numpy as jnp
from jax import lax
from jax.experimental import pallas as pl
from jax.experimental.pallas import tpu as pltpu
from jax.sharding import PartitionSpec as P

NZ = 64
STEPS = 4
HALO = 4
CX = 16
XR = CX + 2 * HALO
CY = 64
TJ = CY // 2
HY = CY // 2
TR = HY + 2 * HALO
TE = TJ + 4
ROWS = TR * XR
UNROLL = 6
W = 128
COURANT = 0.55
F32 = jnp.float32


def swapped(far, near, axis):
    count = lax.axis_size(axis)
    out = []
    for shard, first in ((near, 0), (far, 1)):
        pairs = [(i, i + 1) for i in range(first, count - 1, 2)]
        out.append(lax.ppermute(shard, axis, pairs + [(j, i) for i, j in pairs]))
    return out[0], out[1]


def lanes(tile):
    return pl.ds(tile * W, W)


def aligned(index, step):
    return index if isinstance(index, int) else pl.multiple_of(index, step)


def odd(axis):
    return lax.axis_index(axis) & 1


def pack_y(fwd, adj, eps, far, near, rim, sems):
    at = (1 - odd("gy")) * (TJ - 2)
    copies = []
    for i, (out, tile) in enumerate(((far, TJ - 2 - at), (near, at))):
        where = pl.ds(pl.multiple_of(tile * W, W), 2 * W)
        copies.append(pltpu.make_async_copy(eps.at[:, where], rim.at[i], sems.at[i, 4]))
        for n in range(4):
            state, src = (fwd, adj)[n // 2], n % 2
            copies.append(
                pltpu.make_async_copy(
                    state.at[src, :, :, where], out.at[pl.ds(6 * n, 6)], sems.at[i, n]
                )
            )
    for copy in copies:
        copy.start()
    for i, out in enumerate((far, near)):
        copies[5 * i].wait()
        out[24] = COURANT / rim[i]
    for copy in copies[1:5] + copies[6:]:
        copy.wait()


def to_halves(own, put, low):
    for u in range(TR // 2):
        for x in (0, 8):
            a = own(x, u - 2) if u >= 2 else jnp.zeros((8, W), F32)
            b = own(x, u + 14) if u + 14 < TJ else jnp.zeros((8, W), F32)
            put(2 * u * CX + x, jnp.where(low, a, pltpu.roll(b, NZ, 1)))
            put((2 * u + 1) * CX + x, jnp.where(low, pltpu.roll(a, NZ, 1), b))


def convert(state, *rest):
    eps, e, h, factor = rest if len(rest) == 4 else (None, *rest, None)
    low = masks()[0]

    def one(k, _):
        for ref, c in ((e, 0), (h, 3)):

            def put(r, v):
                ref[k, pl.ds(r, 8), :] = v

            to_halves(lambda x, j: state[k // 3, k % 3 + c, x : x + 8, lanes(j)], put, low)
        return 0

    lax.fori_loop(0, 6, one, 0)
    if eps is not None:

        def put(r, v):
            factor[pl.ds(r, 8), :] = v

        to_halves(lambda x, j: COURANT / eps[x : x + 8, lanes(j)], put, low)


def pack_x(first, state, *rest):
    eps, y_far, y_near, far, near = rest if len(rest) == 5 else (None, *rest)

    def fill(lo, hi, dn, up):
        def put(k, q, get):
            for j in range(TE):
                row = aligned((k * TE + j) * 4, 4)
                for out, x in ((dn, 0), (up, CX - 4)):
                    if j < 2:
                        v = lo[q, x : x + 4, lanes(j)]
                    elif j >= TE - 2:
                        v = hi[q, x : x + 4, lanes(j - TE + 2)]
                    else:
                        v = get(x, lanes(j - 2))
                    out[pl.ds(row, 4), :] = v

        def one(k, _):
            put(k, first + k, lambda x, j: state[k // 6, k % 6, x : x + 4, j])
            return 0

        lax.fori_loop(0, 12, one, 0)
        if eps is not None:
            put(12, 24, lambda x, j: COURANT / eps[x : x + 4, j])

    for px in range(2):
        for py in range(2):

            @pl.when((odd("gx") == px) & (odd("gy") == py))
            def _():
                ghosts = (y_far, y_near) if py == 0 else (y_near, y_far)
                outs = (far, near) if px == 0 else (near, far)
                fill(*ghosts, *outs)


def place_field(put, own, k, xg, yg, low):
    def from_x(side, j):
        return xg[side, pl.ds(aligned((k * TE + j + 2) * 4, 4), 4), :]

    for u in range(TR // 2):
        for side, x in ((0, 0), (1, HALO + CX)):
            a, b = from_x(side, u - 2), from_x(side, u - 2 + TJ // 2)
            put(2 * u * XR + x, jnp.where(low[:4], a, pltpu.roll(b, NZ, 1)))
            put((2 * u + 1) * XR + x, jnp.where(low[:4], pltpu.roll(a, NZ, 1), b))
        for x in (0, 8):
            for r in (2 * u, 2 * u + 1):
                v = own(pl.ds(r * CX + x, 8))
                if u < 2 or u >= TR // 2 - 2:
                    below = u < 2
                    g = yg[int(not below), k, pl.ds(x, 8), lanes(u if below else u - TR // 2 + 2)]
                    if below == bool(r % 2):
                        g = pltpu.roll(g, NZ, 1)
                    v = jnp.where(low, g, v) if below else jnp.where(low, v, g)
                put(r * XR + HALO + x, v)


def order_ghosts(x_near, x_far, y_near, y_far, first, count, xg, yg):
    px, py = odd("gx"), odd("gy")
    xg[1 - px] = x_near[...]
    xg[px] = x_far[...]
    yg[1 - py, 0:12] = y_near[first : first + 12]
    yg[py, 0:12] = y_far[first : first + 12]
    if count == 13:
        yg[1 - py, 12] = y_near[24]
        yg[py, 12] = y_far[24]


def masks():
    lane = lax.broadcasted_iota(jnp.int32, (8, W), 1)
    return lane < NZ, (lane & (NZ - 1)) == 0, (lane & (NZ - 1)) == NZ - 1


def half_steps(fe, fh, factor):
    low, z_first, z_last = masks()
    row8 = lax.broadcasted_iota(jnp.int32, (8, W), 0)
    gx, gy = lax.axis_index("gx"), lax.axis_index("gy")
    at_x0, at_x1 = gx == 0, gx == lax.axis_size("gx") - 1
    at_y0, at_y1 = gy == 0, gy == lax.axis_size("gy") - 1
    coef_x = [
        jnp.where((row8 < 4) & at_x0, 0.0, COURANT).astype(F32),
        jnp.full((8, W), COURANT, F32),
        jnp.where((row8 >= 4) & at_x1, 0.0, COURANT).astype(F32),
    ]

    def up_z(v):
        return jnp.where(z_last, 0.0, pltpu.roll(v, W - 1, 1))

    def down_z(v):
        return jnp.where(z_first, 0.0, pltpu.roll(v, 1, 1))

    def magnetic(r):
        in_low = jnp.where((r < HALO) & at_y0, 0.0, 1.0).astype(F32)
        in_high = jnp.where((r >= HALO + HY) & at_y1, 0.0, 1.0).astype(F32)
        inside = jnp.where(low, in_low, in_high)
        for t in range(3):
            b = pl.multiple_of(r * XR + 8 * t, 8)
            c = coef_x[t] * inside
            for s in range(2):
                k = 3 * s
                ex = fe[k, pl.ds(b, 8), :]
                ey = fe[k + 1, pl.ds(b, 8), :]
                ez = fe[k + 2, pl.ds(b, 8), :]
                ex_y = fe[k, pl.ds(b + XR, 8), :]
                ez_y = fe[k + 2, pl.ds(b + XR, 8), :]
                ey_x = fe[k + 1, pl.ds(b + 1, 8), :]
                ez_x = fe[k + 2, pl.ds(b + 1, 8), :]
                hx = fh[k, pl.ds(b, 8), :] - c * ((ez_y - ez) - (up_z(ey) - ey))
                hy = fh[k + 1, pl.ds(b, 8), :] - c * ((up_z(ex) - ex) - (ez_x - ez))
                hz = fh[k + 2, pl.ds(b, 8), :] - c * ((ey_x - ey) - (ex_y - ex))
                fh[k, pl.ds(b, 8), :] = hx
                fh[k + 1, pl.ds(b, 8), :] = hy
                fh[k + 2, pl.ds(b, 8), :] = hz

    def electric(r, use):
        for t in range(3):
            b = pl.multiple_of(r * XR + 8 * t, 8)
            f = factor[pl.ds(b, 8), :]
            olds, news = [], []
            for s in range(2):
                k = 3 * s
                hx = fh[k, pl.ds(b, 8), :]
                hy = fh[k + 1, pl.ds(b, 8), :]
                hz = fh[k + 2, pl.ds(b, 8), :]
                hx_y = fh[k, pl.ds(b - XR, 8), :]
                hz_y = fh[k + 2, pl.ds(b - XR, 8), :]
                hy_x = fh[k + 1, pl.ds(b - 1, 8), :]
                hz_x = fh[k + 2, pl.ds(b - 1, 8), :]
                ex, ey, ez = (fe[k + c, pl.ds(b, 8), :] for c in range(3))
                nx = ex + f * ((hz - hz_y) - (hy - down_z(hy)))
                ny = ey + f * ((hx - down_z(hx)) - (hz - hz_x))
                nz = ez + f * ((hy - hy_x) - (hx - hx_y))
                fe[k, pl.ds(b, 8), :] = nx
                fe[k + 1, pl.ds(b, 8), :] = ny
                fe[k + 2, pl.ds(b, 8), :] = nz
                olds += [ex, ey, ez]
                news += [nx, ny, nz]
            use(b, olds, news)

    def over(first, last, one):
        def body(r, _):
            one(r)
            return 0

        lax.fori_loop(first, last, body, 0, unroll=UNROLL)

    def step(n, use):
        over(n, TR - 1 - n, magnetic)
        over(n + 1, TR - 1 - n, lambda r: electric(r, use))

    return step


def forward(
    cells,
    wave,
    own_e,
    own_h,
    own_f,
    x_far,
    x_near,
    y_far,
    y_near,
    inc,
    factor,
    fe,
    fh,
    xg,
    yg,
):
    low = masks()[0]
    order_ghosts(x_near, x_far, y_near, y_far, 0, 13, xg, yg)

    def load(k, _):
        for ref, own, c in ((fe, own_e, 0), (fh, own_h, 3)):
            q = 6 * (k // 3) + k % 3 + c

            def put(r, v):
                ref[k, pl.ds(r, v.shape[0]), :] = v

            place_field(put, lambda at: own[k, at, :], q, xg, yg, low)
        return 0

    lax.fori_loop(0, 6, load, 0)

    def put(r, v):
        factor[pl.ds(r, v.shape[0]), :] = v

    place_field(put, lambda at: own_f[at, :], 12, xg, yg, low)
    step = half_steps(fe, fh, factor)
    lane = lax.broadcasted_iota(jnp.int32, (1, W), 1)
    for n in range(STEPS):

        def use(b, olds, news):
            for i in range(6):
                inc[n, i, pl.ds(b, 8), :] = news[i] - olds[i]

        step(n, use)
        for s in range(2):
            x = cells[s, 0] - lax.axis_index("gx") * CX + HALO
            y = cells[s, 1] - lax.axis_index("gy") * CY + HALO
            for h in range(2):
                r = y - h * HY

                @pl.when((x >= 0) & (x < XR) & (r >= 0) & (r < TR))
                def _():
                    at = pl.ds(r * XR + x, 1)
                    pulse = jnp.where(lane == h * NZ + cells[s, 2], wave[s, n], 0.0).astype(F32)
                    fe[3 * s + 2, at, :] += pulse
                    inc[n, 3 * s + 2, at, :] += pulse


def adjoint(
    owners,
    slots,
    own_e,
    own_h,
    factor,
    inc,
    x_far,
    x_near,
    y_far,
    y_near,
    out,
    fe,
    fh,
    xg,
    yg,
    density,
    block,
):
    low = masks()[0]
    order_ghosts(x_near, x_far, y_near, y_far, 12, 12, xg, yg)

    def load(k, _):
        for ref, own, c in ((fe, own_e, 0), (fh, own_h, 3)):
            q = 6 * (k // 3) + k % 3 + c

            def put(r, v):
                ref[k, pl.ds(r, v.shape[0]), :] = v

            place_field(put, lambda at: own[k, at, :], q, xg, yg, low)
        return 0

    lax.fori_loop(0, 6, load, 0)
    step = half_steps(fe, fh, factor)
    for n in range(STEPS):

        def use(b, olds, news):
            terms = [news[i] * inc[STEPS - 1 - n, i, pl.ds(b, 8), :] for i in range(6)]
            total = ((terms[0] + terms[1]) + terms[2]) + ((terms[3] + terms[4]) + terms[5])
            if n > 0:
                total = total + density[pl.ds(b, 8), :]
            density[pl.ds(b, 8), :] = total

        step(n, use)

    for j in range(TJ // 2):
        for t in range(2):
            g = []
            for r in (2 * j + HALO, 2 * j + HALO + 1):
                at = pl.ds(r * XR + HALO + 8 * t, 8)
                g.append(density[at, :] * (factor[at, :] * (-1.0 / COURANT)))
            for tile, v in (
                (j, jnp.where(low, g[0], pltpu.roll(g[1], NZ, 1))),
                (j + TJ // 2, jnp.where(low, pltpu.roll(g[0], NZ, 1), g[1])),
            ):
                for h in range(2):
                    b = ((2 * t + h) * (TJ // 2) + tile // 2) * 8 + tile % 2
                    block[pl.ds(b, 4, stride=2), :] = v[4 * h : 4 * h + 4]
    out[...] = jnp.zeros_like(out)

    def send(i, _):
        o = owners[i // 16, i % 16]

        @pl.when(o >= 0)
        def _():
            c = pl.multiple_of(slots[i // 16, i % 16] * 4, 4)
            b = pl.multiple_of(i * 8, 8)
            out[o, pl.ds(c, 4), :] = block[pl.ds(b, 4), :]
            out[16 + o, pl.ds(c, 4), :] = block[pl.ds(b + 4, 4), :]

        return 0

    lax.fori_loop(0, 64, send, 0)


def place(rows, arrived, out, wide):
    def one(g, _):
        v = arrived[g] + arrived[16 + g]
        for c in range(4):
            r = pl.multiple_of(rows[0, g * 4 + c] * 4, 4)
            wide[pl.ds(r, 4), :] = v[c * 4 : c * 4 + 4]
        return 0

    lax.fori_loop(0, 16, one, 0)
    for i in range(8):
        for q in range(4):
            out[8 * i : 8 * i + 8, lanes(q)] = wide[pl.ds(32 * i + q, 8, stride=4), :]


FULL = pl.BlockSpec(memory_space=pltpu.VMEM)
SCALARS = pl.BlockSpec(memory_space=pltpu.SMEM)


def buf(*shape):
    return jax.ShapeDtypeStruct(shape, F32)


def call(kernel, n_scalars, n_arrays, outs, scratch=(), mib=8, us=2):
    return pl.pallas_call(
        kernel,
        in_specs=[SCALARS] * n_scalars + [FULL] * n_arrays,
        out_specs=[FULL] * len(outs),
        out_shape=list(outs),
        scratch_shapes=[pltpu.VMEM(shape, F32) for shape in scratch],
        compiler_params=pltpu.CompilerParams(vmem_limit_bytes=mib << 20),
        cost_estimate=pl.CostEstimate(
            flops=us * 1000000, bytes_accessed=us * 3000000, transcendentals=0
        ),
        name=kernel.__name__,
    )


RIM = (25, CX, 2 * W)


def call_pack_y():
    hbm = pl.BlockSpec(memory_space=pltpu.HBM)
    return pl.pallas_call(
        pack_y,
        in_specs=[hbm] * 3,
        out_specs=[FULL] * 2,
        out_shape=[buf(*RIM)] * 2,
        scratch_shapes=[pltpu.VMEM((2, CX, 2 * W), F32), pltpu.SemaphoreType.DMA((2, 5))],
        compiler_params=pltpu.CompilerParams(vmem_limit_bytes=62 << 20),
        name="pack_y",
    )


def call_pack_x(first, count):
    def kernel(*refs):
        pack_x(first, *refs)

    kernel.__name__ = "pack_x"
    return call(kernel, 0, 3 + (count == 13), [buf(count * TE * 4, W)] * 2, us=1)


FIELD = (6, ROWS, W)
SENT = (32, 16, W)


def call_forward():
    ghosts = [(2, 13 * TE * 4, W), (2, 13, CX, 2 * W)]
    return call(
        forward, 2, 7, [buf(STEPS, *FIELD), buf(ROWS, W)], [FIELD, FIELD, *ghosts], 12, 15
    )


def call_adjoint():
    ghosts = [(2, 12 * TE * 4, W), (2, 12, CX, 2 * W)]
    return call(
        adjoint,
        2,
        8,
        [buf(*SENT)],
        [FIELD, FIELD, *ghosts, (ROWS, W), (64 * 8, W)],
        12,
        15,
    )


def per_device(
    forward_state,
    adjoint_state,
    permittivity,
    waveform,
    source_cell,
    block_owner,
    block_slot,
    owner_rows,
):
    y_near, y_far = swapped(
        *call_pack_y()(forward_state, adjoint_state, permittivity), "gy"
    )
    own = [buf(6, TR * CX, W)] * 2
    forward_own = call(convert, 0, 2, [*own, buf(TR * CX, W)])(forward_state, permittivity)
    adjoint_own = call(convert, 0, 1, own)(adjoint_state)
    y_near, y_far, forward_own, adjoint_own = lax.optimization_barrier(
        (y_near, y_far, forward_own, adjoint_own)
    )
    fx_near, fx_far = swapped(
        *call_pack_x(0, 13)(forward_state, permittivity, y_far, y_near), "gx"
    )
    ax_near, ax_far = swapped(*call_pack_x(12, 12)(adjoint_state, y_far, y_near), "gx")
    inc, factor = call_forward()(
        source_cell, waveform, *forward_own, fx_far, fx_near, y_far, y_near
    )
    (outgoing,) = call_adjoint()(
        block_owner,
        block_slot,
        *adjoint_own,
        factor,
        inc,
        ax_far,
        ax_near,
        y_far,
        y_near,
    )
    arrived = lax.all_to_all(outgoing, ("src", "gy"), 0, 0, tiled=True)
    (placed,) = call(place, 1, 1, [buf(64, 512)], [(256, W)])(owner_rows, arrived)
    return placed


def solution(mesh):
    in_specs = (
        P("src", None, "gx", "gy"),
        P("src", None, "gx", "gy"),
        P("gx", "gy"),
        P("src", None),
        P("src", None),
        P("gx", "gy"),
        P("gx", "gy"),
        P(("gx", "gy"), None),
    )
    out_specs = P(("gx", "gy"), "src")
    return jax.shard_map(
        per_device, mesh=mesh, in_specs=in_specs, out_specs=out_specs, check_vma=False
    )
```

time: 98.5 us -> 87 us (0.88)
  starting transfers between devices: 22.2 us -> 10.3 us
  waiting for transfers between devices: 5.49 us -> 10.6 us
  local copies, waits for them, and re-layouts: 7.34 us -> 2.27 us
  blocking collectives: 29.2 us -> 31.4 us
  Pallas kernels: 33.5 us -> 32.4 us
    ppermute x8 -> x6, starting transfers between devices: 22.2 us -> 10.3 us  [swapped(): out.append(lax.ppermute(shard, axis, pairs + [(j, i) for i, j in pairs]))]
    ppermute x8 -> x6, waiting for transfers between devices: 5.49 us -> 10.6 us  [swapped(): out.append(lax.ppermute(shard, axis, pairs + [(j, i) for i, j in pairs]))]
    unnamed x38 -> x18, local copies, waits for them, and re-layouts: 7.09 us -> 2.27 us
    pallas_call x5 -> x6, Pallas kernels: 4.6 us -> 7.54 us  [the longest x1 2.26 us: per_device(): call_pack_y()(forward_state, adjoint_state, permittivity)]
    pallas_call x1, Pallas kernels: 14 us -> 11.5 us  [per_device(): call_forward()]
    all_to_all x1, blocking collectives: 29.2 us -> 31.4 us  [per_device(): arrived = lax.all_to_all(outgoing, ('src', 'gy'), 0, 0, tiled=True)]
    pallas_call x1, Pallas kernels: 14.9 us -> 13.4 us  [per_device(): call_adjoint()]
  transfers between devices with their start and end apart: 8 -> 6, of which waited for: 4 -> 2; matrix products, arithmetic and copies ran while one was open for 0% -> 0% of each run, Pallas kernels for 17% -> 17%
where the time goes in v4:
time: 87 us; the launch traced here: 87.2 us
  Pallas kernels  32.4 us (37%)
  blocking collectives  31.4 us (36%)
  waiting for transfers between devices  10.6 us (12%)
  starting transfers between devices  10.3 us (12%)
  local copies, waits for them, and re-layouts  2.27 us (3%)
    all_to_all x1, blocking collectives, per_device(): arrived = lax.all_to_all(outgoing, ('src', 'gy'), 0, 0, tiled=True)  31.4 us
    pallas_call x1, Pallas kernels, per_device(): call_adjoint()  13.4 us
    pallas_call x1, Pallas kernels, per_device(): call_forward()  11.5 us
    ppermute x6, waiting for transfers between devices, swapped(): out.append(lax.ppermute(shard, axis, pairs + [(j, i) for i, j in pairs]))  10.6 us
    ppermute x6, starting transfers between devices, swapped(): out.append(lax.ppermute(shard, axis, pairs + [(j, i) for i, j in pairs]))  10.3 us
    unnamed x18, local copies, waits for them, and re-layouts  2.27 us
    pallas_call x1, Pallas kernels, per_device(): call_pack_y()(forward_state, adjoint_state, permittivity)  2.26 us
  transfers between devices with their start and end apart: 6, of which 2 were waited for; matrix products, arithmetic and copies ran while one was open for 0% of the time, Pallas kernels for 17%

profile of v4, /device:TPU:32, one launch (start us, length us, event | category | flops | bytes accessed | tf_op | source)
XLA Modules:
  0.0 87.2 jit_solution(10694477111353102648)
XLA Ops:
  0.0 0.0 copy-start.3
  0.0 2.3 %pack_y.1 = (f32[25,16,256]{2,1,0:T(8,128)}, f32[25,16,256]{2,1,0:T(8,128)}) custom-call(f32[2,6,16,4096]{3,2,1,0:T(8,128)} %refs_0_.2, f32[2,6,16,4096]{3,2,1,0:T(8,128)} %refs_0_.3, f32[16,4096]{1,0:T(8,128)} %refs_1_.1), custom_call_target="tpu_custom_call" | custom-call | tf_op jit(solution)/shard_map/pack_y/pallas_call | solution.py:480
  2.3 1.6 %collective-permute-start = (f32[25,16,256]{2,1,0:T(8,128)}, f32[25,16,256]{2,1,0:T(8,128)S(1)}, u32[]{:S(2)}, u32[]{:S(2)}) collective-permute-start(f32[25,16,256]{2,1,0:T(8,128)} %get-tuple-element.25), channel_id=1, source_target_pairs={{0,1},{2,3},{4,5},{6,7},{8,9},{10,11},{12,13},{14,15},{1,0},{3,2},... | collective-permute-start | bytes 1228808 | tf_op jit(solution)/shard_map/ppermute | solution.py:30
  3.8 0.7 collective-permute-start.1
  4.5 0.0 copy-done.3
  4.5 0.0 copy-start
  4.6 1.9 %copy-done = f32[2,6,16,4096]{3,2,1,0:T(8,128)S(1)} copy-done((f32[2,6,16,4096]{3,2,1,0:T(8,128)S(1)}, f32[2,6,16,4096]{3,2,1,0:T(8,128)}, u32[]{:S(2)}) %copy-start) | copy-done | bytes 3145752
  6.4 0.0 copy-start.2
  6.4 1.5 %convert.2 = (f32[6,640,128]{2,1,0:T(8,128)S(1)}, f32[6,640,128]{2,1,0:T(8,128)S(1)}, f32[640,128]{1,0:T(8,128)S(1)}) custom-call(f32[2,6,16,4096]{3,2,1,0:T(8,128)S(1)} %copy-done, f32[16,4096]{1,0:T(8,128)S(1)} %copy-done.3), custom_call_target="tpu_custom_call" | custom-call | flops 2000000 | bytes 6000000 | tf_op jit(solution)/shard_map/convert/pallas_call | solution.py:483
  8.0 0.3 copy-done.2
  8.3 0.0 copy-start.1
  8.3 1.4 %convert.3 = (f32[6,640,128]{2,1,0:T(8,128)S(1)}, f32[6,640,128]{2,1,0:T(8,128)S(1)}) custom-call(f32[2,6,16,4096]{3,2,1,0:T(8,128)S(1)} %copy-done.2), custom_call_target="tpu_custom_call" | custom-call | flops 2000000 | bytes 6000000 | tf_op jit(solution)/shard_map/convert/pallas_call | solution.py:484
  9.7 4.0 %collective-permute-done.refs_3_.y_near.refs_2_ = f32[25,16,256]{2,1,0:T(8,128)S(1)} collective-permute-done((f32[25,16,256]{2,1,0:T(8,128)}, f32[25,16,256]{2,1,0:T(8,128)S(1)}, u32[]{:S(2)}, u32[]{:S(2)}) %collective-permute-start) | collective-permute-done | bytes 409632 | tf_op jit(solution)/shard_map/ppermute | solution.py:30
  13.8 0.0 collective-permute-done.1.refs_2_.y_far.refs_1_
  13.8 0.0 copy-done.1
  13.8 0.5 pack_x.2
  14.3 1.9 %collective-permute-start.2 = (f32[1872,128]{1,0:T(8,128)S(1)}, f32[1872,128]{1,0:T(8,128)S(1)}, u32[]{:S(2)}, u32[]{:S(2)}) collective-permute-start(f32[1872,128]{1,0:T(8,128)S(1)} %get-tuple-element.39), channel_id=1, source_target_pairs={{16,32},{48,64},{80,96},{32,16},{64,48},{96,80},{17,33},{49,65},{8... | collective-permute-start | bytes 2875400 | tf_op jit(solution)/shard_map/ppermute | solution.py:30
  16.2 0.0 copy-start.6
  16.3 0.0 copy-start.7
  16.3 2.1 %collective-permute-start.3 = (f32[1872,128]{1,0:T(8,128)S(1)}, f32[1872,128]{1,0:T(8,128)S(1)}, u32[]{:S(2)}, u32[]{:S(2)}) collective-permute-start(f32[1872,128]{1,0:T(8,128)S(1)} %get-tuple-element.40), channel_id=1, source_target_pairs={{0,16},{32,48},{64,80},{96,112},{16,0},{48,32},{80,64},{112,96},{1... | collective-permute-start | bytes 2875400 | tf_op jit(solution)/shard_map/ppermute | solution.py:30
  18.4 0.5 pack_x.3
  18.9 1.9 %collective-permute-start.4 = (f32[1728,128]{1,0:T(8,128)S(1)}, f32[1728,128]{1,0:T(8,128)S(1)}, u32[]{:S(2)}, u32[]{:S(2)}) collective-permute-start(f32[1728,128]{1,0:T(8,128)S(1)} %get-tuple-element.43), channel_id=1, source_target_pairs={{16,32},{48,64},{80,96},{32,16},{64,48},{96,80},{17,33},{49,65},{8... | collective-permute-start | bytes 2654216 | tf_op jit(solution)/shard_map/ppermute | solution.py:30
  20.8 0.0 copy-start.4
  20.8 0.0 copy-start.5
  20.8 2.1 %collective-permute-start.5 = (f32[1728,128]{1,0:T(8,128)S(1)}, f32[1728,128]{1,0:T(8,128)S(1)}, u32[]{:S(2)}, u32[]{:S(2)}) collective-permute-start(f32[1728,128]{1,0:T(8,128)S(1)} %get-tuple-element.44), channel_id=1, source_target_pairs={{0,16},{32,48},{64,80},{96,112},{16,0},{48,32},{80,64},{112,96},{1... | collective-permute-start | bytes 2654216 | tf_op jit(solution)/shard_map/ppermute | solution.py:30
  22.9 6.5 %collective-permute-done.2.x_far = f32[1872,128]{1,0:T(8,128)S(1)} collective-permute-done((f32[1872,128]{1,0:T(8,128)S(1)}, f32[1872,128]{1,0:T(8,128)S(1)}, u32[]{:S(2)}, u32[]{:S(2)}) %collective-permute-start.2) | collective-permute-done | bytes 958496 | tf_op jit(solution)/shard_map/ppermute | solution.py:30
  29.5 0.0 collective-permute-done.3.x_near
  29.5 0.0 copy-done.6
  29.5 0.0 copy-done.7
  29.5 11.5 %forward.1 = (f32[4,6,960,128]{3,2,1,0:T(8,128)S(1)}, f32[960,128]{1,0:T(8,128)S(1)}) custom-call(s32[2,3]{1,0:T(2,128)S(1)} %copy-done.6, f32[2,4]{1,0:T(2,128)S(1)} %copy-done.7, f32[6,640,128]{2,1,0:T(8,128)S(1)} %get-tuple-element.34.own_e, f32[6,640,128]{2,1,0:T(8,128)S(1)} %get-tuple-element.35.own_h, f32[640,128]{1,0:T(8,128)S(1)} %get-tuple-element.36.own_f, ...), custom_call_target="tpu_custom_call" | custom-call | flops 15000000 | bytes 45000000 | tf_op jit(solution)/shard_map/forward/pallas_call | solution.py:492
  41.0 0.0 collective-permute-done.4.x_far
  41.0 0.0 collective-permute-done.5.x_near
  41.0 0.0 copy-done.4
  41.0 0.0 copy-done.5
  41.0 0.0 copy-start.8
  41.0 13.4 %adjoint.1 = f32[32,16,128]{2,1,0:T(8,128)S(1)} custom-call(s32[4,16]{1,0:T(4,128)S(1)} %copy-done.4, s32[4,16]{1,0:T(4,128)S(1)} %copy-done.5, f32[6,640,128]{2,1,0:T(8,128)S(1)} %get-tuple-element.32.own_e, f32[6,640,128]{2,1,0:T(8,128)S(1)} %get-tuple-element.33.own_h, f32[960,128]{1,0:T(8,128)S(1)} %get-tuple-element.41.factor, ...), custom_call_target="tpu_custom_call" | custom-call | flops 15000000 | bytes 45000000 | tf_op jit(solution)/shard_map/adjoint/pallas_call | solution.py:495
  54.4 31.4 %all_to_all.5.arrived = f32[32,16,128]{2,1,0:T(8,128)S(1)} all-to-all(f32[32,16,128]{2,1,0:T(8,128)S(1)} %adjoint.1), channel_id=1, replica_groups=mesh['src'=2,'gx'=8,'gy'=16] {'src','gy'}, dimensions={0} | all-to-all | bytes 524288 | tf_op jit(solution)/shard_map/all_to_all | solution.py:506
  85.9 0.0 copy-done.8
  85.9 1.3 %place.1 = f32[64,512]{1,0:T(8,128)} custom-call(s32[1,64]{1,0:T(1,128)S(1)} %copy-done.8, f32[32,16,128]{2,1,0:T(8,128)S(1)} %all_to_all.5.arrived), custom_call_target="tpu_custom_call" | custom-call | flops 2000000 | bytes 6000000 | tf_op jit(solution)/shard_map/place/pallas_call | solution.py:507
Async XLA Ops:
  0.0 4.5 %copy-start.3 = (f32[16,4096]{1,0:T(8,128)S(1)}, f32[16,4096]{1,0:T(8,128)}, u32[]{:S(2)}) copy-start(f32[16,4096]{1,0:T(8,128)} %refs_1_.1) | copy-start | bytes 786436
  2.3 11.5 %collective-permute-start = (f32[25,16,256]{2,1,0:T(8,128)}, f32[25,16,256]{2,1,0:T(8,128)S(1)}, u32[]{:S(2)}, u32[]{:S(2)}) collective-permute-start(f32[25,16,256]{2,1,0:T(8,128)} %get-tuple-element.25), channel_id=1, source_target_pairs={{0,1},{2,3},{4,5},{6,7},{8,9},{10,11},{12,13},{14,15},{1,0},{3,2},... | collective-permute-start | bytes 1228808 | tf_op jit(solution)/shard_map/ppermute | solution.py:30
  3.8 9.9 %collective-permute-start.1 = (f32[25,16,256]{2,1,0:T(8,128)}, f32[25,16,256]{2,1,0:T(8,128)S(1)}, u32[]{:S(2)}, u32[]{:S(2)}) collective-permute-start(f32[25,16,256]{2,1,0:T(8,128)} %get-tuple-element.26), channel_id=1, source_target_pairs={{1,2},{3,4},{5,6},{7,8},{9,10},{11,12},{13,14},{2,1},{4,3},{6,5},{... | collective-permute-start | bytes 1228808 | tf_op jit(solution)/shard_map/ppermute | solution.py:30
  4.5 1.9 %copy-start = (f32[2,6,16,4096]{3,2,1,0:T(8,128)S(1)}, f32[2,6,16,4096]{3,2,1,0:T(8,128)}, u32[]{:S(2)}) copy-start(f32[2,6,16,4096]{3,2,1,0:T(8,128)} %refs_0_.2) | copy-start | bytes 9437188
  6.4 1.9 %copy-start.2 = (f32[2,6,16,4096]{3,2,1,0:T(8,128)S(1)}, f32[2,6,16,4096]{3,2,1,0:T(8,128)}, u32[]{:S(2)}) copy-start(f32[2,6,16,4096]{3,2,1,0:T(8,128)} %refs_0_.3) | copy-start | bytes 9437188
  8.3 5.5 %copy-start.1 = (f32[2,6,16,4096]{3,2,1,0:T(8,128)S(1)}, f32[2,6,16,4096]{3,2,1,0:T(8,128)}, u32[]{:S(2)}) copy-start(f32[2,6,16,4096]{3,2,1,0:T(8,128)} %refs_0_.2) | copy-start | bytes 9437188
  14.3 15.2 %collective-permute-start.2 = (f32[1872,128]{1,0:T(8,128)S(1)}, f32[1872,128]{1,0:T(8,128)S(1)}, u32[]{:S(2)}, u32[]{:S(2)}) collective-permute-start(f32[1872,128]{1,0:T(8,128)S(1)} %get-tuple-element.39), channel_id=1, source_target_pairs={{16,32},{48,64},{80,96},{32,16},{64,48},{96,80},{17,33},{49,65},{8... | collective-permute-start | bytes 2875400 | tf_op jit(solution)/shard_map/ppermute | solution.py:30
  16.2 13.2 %copy-start.6 = (s32[2,3]{1,0:T(2,128)S(1)}, s32[2,3]{1,0:T(2,128)}, u32[]{:S(2)}) copy-start(s32[2,3]{1,0:T(2,128)} %cells.1) | copy-start | bytes 76
  16.3 13.2 %copy-start.7 = (f32[2,4]{1,0:T(2,128)S(1)}, f32[2,4]{1,0:T(2,128)}, u32[]{:S(2)}) copy-start(f32[2,4]{1,0:T(2,128)} %wave.1) | copy-start | bytes 100
  16.3 13.2 %collective-permute-start.3 = (f32[1872,128]{1,0:T(8,128)S(1)}, f32[1872,128]{1,0:T(8,128)S(1)}, u32[]{:S(2)}, u32[]{:S(2)}) collective-permute-start(f32[1872,128]{1,0:T(8,128)S(1)} %get-tuple-element.40), channel_id=1, source_target_pairs={{0,16},{32,48},{64,80},{96,112},{16,0},{48,32},{80,64},{112,96},{1... | collective-permute-start | bytes 2875400 | tf_op jit(solution)/shard_map/ppermute | solution.py:30
  18.9 22.1 %collective-permute-start.4 = (f32[1728,128]{1,0:T(8,128)S(1)}, f32[1728,128]{1,0:T(8,128)S(1)}, u32[]{:S(2)}, u32[]{:S(2)}) collective-permute-start(f32[1728,128]{1,0:T(8,128)S(1)} %get-tuple-element.43), channel_id=1, source_target_pairs={{16,32},{48,64},{80,96},{32,16},{64,48},{96,80},{17,33},{49,65},{8... | collective-permute-start | bytes 2654216 | tf_op jit(solution)/shard_map/ppermute | solution.py:30
  20.8 20.2 %copy-start.4 = (s32[4,16]{1,0:T(4,128)S(1)}, s32[4,16]{1,0:T(4,128)}, u32[]{:S(2)}) copy-start(s32[4,16]{1,0:T(4,128)} %owners.1) | copy-start | bytes 772
  20.8 20.2 %copy-start.5 = (s32[4,16]{1,0:T(4,128)S(1)}, s32[4,16]{1,0:T(4,128)}, u32[]{:S(2)}) copy-start(s32[4,16]{1,0:T(4,128)} %slots.1) | copy-start | bytes 772
  20.8 20.2 %collective-permute-start.5 = (f32[1728,128]{1,0:T(8,128)S(1)}, f32[1728,128]{1,0:T(8,128)S(1)}, u32[]{:S(2)}, u32[]{:S(2)}) collective-permute-start(f32[1728,128]{1,0:T(8,128)S(1)} %get-tuple-element.44), channel_id=1, source_target_pairs={{0,16},{32,48},{64,80},{96,112},{16,0},{48,32},{80,64},{112,96},{1... | collective-permute-start | bytes 2654216 | tf_op jit(solution)/shard_map/ppermute | solution.py:30
  41.0 44.9 %copy-start.8 = (s32[1,64]{1,0:T(1,128)S(1)}, s32[1,64]{1,0:T(1,128)}, u32[]{:S(2)}) copy-start(s32[1,64]{1,0:T(1,128)} %rows.1) | copy-start | bytes 772

commit v5 on v4

--- a/solution.py
+++ b/solution.py
@@ -373,8 +373,8 @@
         def _():
             c = pl.multiple_of(slots[i // 16, i % 16] * 4, 4)
             b = pl.multiple_of(i * 8, 8)
-            out[o, pl.ds(c, 4), :] = block[pl.ds(b, 4), :]
-            out[16 + o, pl.ds(c, 4), :] = block[pl.ds(b + 4, 4), :]
+            out[2 * o, pl.ds(c, 4), :] = block[pl.ds(b, 4), :]
+            out[2 * o + 1, pl.ds(c, 4), :] = block[pl.ds(b + 4, 4), :]
 
         return 0
 
@@ -383,9 +383,9 @@
 
 def place(rows, arrived, out, wide):
     def one(g, _):
-        v = arrived[g] + arrived[16 + g]
+        v = arrived[2 * g] + arrived[2 * g + 1]
         for c in range(4):
-            r = pl.multiple_of(rows[0, g * 4 + c] * 4, 4)
+            r = pl.multiple_of(rows[0, g * 4 + c], 4)
             wide[pl.ds(r, 4), :] = v[c * 4 : c * 4 + 4]
         return 0
 
@@ -503,8 +503,9 @@
         y_far,
         y_near,
     )
-    arrived = lax.all_to_all(outgoing, ("src", "gy"), 0, 0, tiled=True)
-    (placed,) = call(place, 1, 1, [buf(64, 512)], [(256, W)])(owner_rows, arrived)
+    outgoing, rows = lax.optimization_barrier((outgoing, owner_rows))
+    arrived = lax.all_to_all(outgoing, ("gy", "src"), 0, 0, tiled=True)
+    (placed,) = call(place, 1, 1, [buf(64, 512)], [(256, W)])(rows * 4, arrived)
     return placed
 
 

time: 87 us -> 88.8 us (1.021)
  blocking collectives: 31.4 us -> 0 us
  starting transfers between devices: 10.3 us -> 27.6 us
  waiting for transfers between devices: 10.6 us -> 25.3 us
    all_to_all x1 -> x0, blocking collectives: 31.4 us -> none  [per_device(): arrived = lax.all_to_all(outgoing, ('src', 'gy'), 0, 0, tiled=True)]
    all_to_all x0 -> x1, starting transfers between devices: none -> 17.3 us  [per_device(): arrived = lax.all_to_all(outgoing, ('gy', 'src'), 0, 0, tiled=True)]
    all_to_all x0 -> x1, waiting for transfers between devices: none -> 14.7 us  [per_device(): arrived = lax.all_to_all(outgoing, ('gy', 'src'), 0, 0, tiled=True)]
  transfers between devices with their start and end apart: 6 -> 7, of which waited for: 2 -> 3; matrix products, arithmetic and copies ran while one was open for 0% -> 0% of each run, Pallas kernels for 17% -> 17%
where the time goes in v5:
time: 88.8 us; the launch traced here: 88.5 us
  Pallas kernels  33.1 us (37%)
  starting transfers between devices  27.6 us (31%)
  waiting for transfers between devices  25.3 us (28%)
  local copies, waits for them, and re-layouts  2.27 us (3%)
    all_to_all x1, starting transfers between devices, per_device(): arrived = lax.all_to_all(outgoing, ('gy', 'src'), 0, 0, tiled=True)  17.3 us
    all_to_all x1, waiting for transfers between devices, per_device(): arrived = lax.all_to_all(outgoing, ('gy', 'src'), 0, 0, tiled=True)  14.7 us
    pallas_call x1, Pallas kernels, per_device(): call_adjoint()  14.1 us
    pallas_call x1, Pallas kernels, per_device(): call_forward()  11.5 us
    ppermute x6, waiting for transfers between devices, swapped(): out.append(lax.ppermute(shard, axis, pairs + [(j, i) for i, j in pairs]))  10.6 us
    ppermute x6, starting transfers between devices, swapped(): out.append(lax.ppermute(shard, axis, pairs + [(j, i) for i, j in pairs]))  10.3 us
    unnamed x18, local copies, waits for them, and re-layouts  2.27 us
    pallas_call x1, Pallas kernels, per_device(): call_pack_y()(forward_state, adjoint_state, permittivity)  2.25 us
  transfers between devices with their start and end apart: 7, of which 3 were waited for; matrix products, arithmetic and copies ran while one was open for 0% of the time, Pallas kernels for 17%

profile of v5, /device:TPU:32, one launch (start us, length us, event | category | flops | bytes accessed | tf_op | source)
XLA Modules:
  0.0 88.5 jit_solution(2552828433699606001)
XLA Ops:
  0.0 0.0 copy-start.3
  0.0 2.2 %pack_y.1 = (f32[25,16,256]{2,1,0:T(8,128)}, f32[25,16,256]{2,1,0:T(8,128)}) custom-call(f32[2,6,16,4096]{3,2,1,0:T(8,128)} %refs_0_.2, f32[2,6,16,4096]{3,2,1,0:T(8,128)} %refs_0_.3, f32[16,4096]{1,0:T(8,128)} %refs_1_.1), custom_call_target="tpu_custom_call" | custom-call | tf_op jit(solution)/shard_map/pack_y/pallas_call | solution.py:480
  2.3 1.6 %collective-permute-start = (f32[25,16,256]{2,1,0:T(8,128)}, f32[25,16,256]{2,1,0:T(8,128)S(1)}, u32[]{:S(2)}, u32[]{:S(2)}) collective-permute-start(f32[25,16,256]{2,1,0:T(8,128)} %get-tuple-element.27), channel_id=1, source_target_pairs={{0,1},{2,3},{4,5},{6,7},{8,9},{10,11},{12,13},{14,15},{1,0},{3,2},... | collective-permute-start | bytes 1228808 | tf_op jit(solution)/shard_map/ppermute | solution.py:30
  3.8 0.7 collective-permute-start.1
  4.5 0.0 copy-done.3
  4.5 0.0 copy-start
  4.5 1.9 %copy-done = f32[2,6,16,4096]{3,2,1,0:T(8,128)S(1)} copy-done((f32[2,6,16,4096]{3,2,1,0:T(8,128)S(1)}, f32[2,6,16,4096]{3,2,1,0:T(8,128)}, u32[]{:S(2)}) %copy-start) | copy-done | bytes 3145752
  6.4 0.0 copy-start.2
  6.4 1.5 %convert.2 = (f32[6,640,128]{2,1,0:T(8,128)S(1)}, f32[6,640,128]{2,1,0:T(8,128)S(1)}, f32[640,128]{1,0:T(8,128)S(1)}) custom-call(f32[2,6,16,4096]{3,2,1,0:T(8,128)S(1)} %copy-done, f32[16,4096]{1,0:T(8,128)S(1)} %copy-done.3), custom_call_target="tpu_custom_call" | custom-call | flops 2000000 | bytes 6000000 | tf_op jit(solution)/shard_map/convert/pallas_call | solution.py:483
  8.0 0.3 copy-done.2
  8.3 0.0 copy-start.1
  8.3 1.4 %convert.3 = (f32[6,640,128]{2,1,0:T(8,128)S(1)}, f32[6,640,128]{2,1,0:T(8,128)S(1)}) custom-call(f32[2,6,16,4096]{3,2,1,0:T(8,128)S(1)} %copy-done.2), custom_call_target="tpu_custom_call" | custom-call | flops 2000000 | bytes 6000000 | tf_op jit(solution)/shard_map/convert/pallas_call | solution.py:484
  9.7 4.0 %collective-permute-done.refs_3_.y_near.refs_2_ = f32[25,16,256]{2,1,0:T(8,128)S(1)} collective-permute-done((f32[25,16,256]{2,1,0:T(8,128)}, f32[25,16,256]{2,1,0:T(8,128)S(1)}, u32[]{:S(2)}, u32[]{:S(2)}) %collective-permute-start) | collective-permute-done | bytes 409632 | tf_op jit(solution)/shard_map/ppermute | solution.py:30
  13.8 0.0 collective-permute-done.1.refs_2_.y_far.refs_1_
  13.8 0.0 copy-done.1
  13.8 0.5 pack_x.2
  14.3 1.9 %collective-permute-start.2 = (f32[1872,128]{1,0:T(8,128)S(1)}, f32[1872,128]{1,0:T(8,128)S(1)}, u32[]{:S(2)}, u32[]{:S(2)}) collective-permute-start(f32[1872,128]{1,0:T(8,128)S(1)} %get-tuple-element.41), channel_id=1, source_target_pairs={{16,32},{48,64},{80,96},{32,16},{64,48},{96,80},{17,33},{49,65},{8... | collective-permute-start | bytes 2875400 | tf_op jit(solution)/shard_map/ppermute | solution.py:30
  16.2 0.0 copy-start.6
  16.2 0.0 copy-start.7
  16.3 2.1 %collective-permute-start.3 = (f32[1872,128]{1,0:T(8,128)S(1)}, f32[1872,128]{1,0:T(8,128)S(1)}, u32[]{:S(2)}, u32[]{:S(2)}) collective-permute-start(f32[1872,128]{1,0:T(8,128)S(1)} %get-tuple-element.42), channel_id=1, source_target_pairs={{0,16},{32,48},{64,80},{96,112},{16,0},{48,32},{80,64},{112,96},{1... | collective-permute-start | bytes 2875400 | tf_op jit(solution)/shard_map/ppermute | solution.py:30
  18.4 0.5 pack_x.3
  18.9 1.9 %collective-permute-start.4 = (f32[1728,128]{1,0:T(8,128)S(1)}, f32[1728,128]{1,0:T(8,128)S(1)}, u32[]{:S(2)}, u32[]{:S(2)}) collective-permute-start(f32[1728,128]{1,0:T(8,128)S(1)} %get-tuple-element.45), channel_id=1, source_target_pairs={{16,32},{48,64},{80,96},{32,16},{64,48},{96,80},{17,33},{49,65},{8... | collective-permute-start | bytes 2654216 | tf_op jit(solution)/shard_map/ppermute | solution.py:30
  20.8 0.0 copy-start.4
  20.8 0.0 copy-start.5
  20.8 2.1 %collective-permute-start.5 = (f32[1728,128]{1,0:T(8,128)S(1)}, f32[1728,128]{1,0:T(8,128)S(1)}, u32[]{:S(2)}, u32[]{:S(2)}) collective-permute-start(f32[1728,128]{1,0:T(8,128)S(1)} %get-tuple-element.46), channel_id=1, source_target_pairs={{0,16},{32,48},{64,80},{96,112},{16,0},{48,32},{80,64},{112,96},{1... | collective-permute-start | bytes 2654216 | tf_op jit(solution)/shard_map/ppermute | solution.py:30
  22.9 6.5 %collective-permute-done.2.x_far = f32[1872,128]{1,0:T(8,128)S(1)} collective-permute-done((f32[1872,128]{1,0:T(8,128)S(1)}, f32[1872,128]{1,0:T(8,128)S(1)}, u32[]{:S(2)}, u32[]{:S(2)}) %collective-permute-start.2) | collective-permute-done | bytes 958496 | tf_op jit(solution)/shard_map/ppermute | solution.py:30
  29.5 0.0 collective-permute-done.3.x_near
  29.5 0.0 copy-done.6
  29.5 0.0 copy-done.7
  29.5 11.5 %forward.1 = (f32[4,6,960,128]{3,2,1,0:T(8,128)S(1)}, f32[960,128]{1,0:T(8,128)S(1)}) custom-call(s32[2,3]{1,0:T(2,128)S(1)} %copy-done.6, f32[2,4]{1,0:T(2,128)S(1)} %copy-done.7, f32[6,640,128]{2,1,0:T(8,128)S(1)} %get-tuple-element.36.own_e, f32[6,640,128]{2,1,0:T(8,128)S(1)} %get-tuple-element.37.own_h, f32[640,128]{1,0:T(8,128)S(1)} %get-tuple-element.38.own_f, ...), custom_call_target="tpu_custom_call" | custom-call | flops 15000000 | bytes 45000000 | tf_op jit(solution)/shard_map/forward/pallas_call | solution.py:492
  41.0 0.0 collective-permute-done.4.x_far
  41.0 0.0 collective-permute-done.5.x_near
  41.0 0.0 copy-done.4
  41.0 0.0 copy-done.5
  41.0 0.0 copy-start.8
  41.0 14.1 %adjoint.1 = f32[32,16,128]{2,1,0:T(8,128)} custom-call(s32[4,16]{1,0:T(4,128)S(1)} %copy-done.4, s32[4,16]{1,0:T(4,128)S(1)} %copy-done.5, f32[6,640,128]{2,1,0:T(8,128)S(1)} %get-tuple-element.34.own_e, f32[6,640,128]{2,1,0:T(8,128)S(1)} %get-tuple-element.35.own_h, f32[960,128]{1,0:T(8,128)S(1)} %get-tuple-element.43.factor, ...), custom_call_target="tpu_custom_call" | custom-call | flops 15000000 | bytes 45000000 | tf_op jit(solution)/shard_map/adjoint/pallas_call | solution.py:495
  55.1 17.3 %all-to-all-start = ((f32[32,16,128]{2,1,0:T(8,128)}), f32[32,16,128]{2,1,0:T(8,128)S(1)}, u32[]{:S(2)}, u32[]{:S(2)}) async-start(f32[32,16,128]{2,1,0:T(8,128)} %adjoint.1), calls=%async_computation | async-start | bytes 524288 | tf_op jit(solution)/shard_map/all_to_all | solution.py:507
  72.4 0.0 copy-done.8
  72.5 14.7 %all-to-all-done.arrived = f32[32,16,128]{2,1,0:T(8,128)S(1)} async-done(((f32[32,16,128]{2,1,0:T(8,128)}), f32[32,16,128]{2,1,0:T(8,128)S(1)}, u32[]{:S(2)}, u32[]{:S(2)}) %all-to-all-start) | async-done | bytes 262176 | tf_op jit(solution)/shard_map/all_to_all | solution.py:507
  87.2 1.3 %place.1 = f32[64,512]{1,0:T(8,128)} custom-call(s32[1,64]{1,0:T(1,128)S(1)} %broadcast_multiply_fusion.rows, f32[32,16,128]{2,1,0:T(8,128)S(1)} %all-to-all-done.arrived), custom_call_target="tpu_custom_call" | custom-call | flops 2000000 | bytes 6000000 | tf_op jit(solution)/shard_map/place/pallas_call | solution.py:508
  (1 shorter events, 0.0 us)
Async XLA Ops:
  0.0 4.5 %copy-start.3 = (f32[16,4096]{1,0:T(8,128)S(1)}, f32[16,4096]{1,0:T(8,128)}, u32[]{:S(2)}) copy-start(f32[16,4096]{1,0:T(8,128)} %refs_1_.1) | copy-start | bytes 786436
  2.3 11.5 %collective-permute-start = (f32[25,16,256]{2,1,0:T(8,128)}, f32[25,16,256]{2,1,0:T(8,128)S(1)}, u32[]{:S(2)}, u32[]{:S(2)}) collective-permute-start(f32[25,16,256]{2,1,0:T(8,128)} %get-tuple-element.27), channel_id=1, source_target_pairs={{0,1},{2,3},{4,5},{6,7},{8,9},{10,11},{12,13},{14,15},{1,0},{3,2},... | collective-permute-start | bytes 1228808 | tf_op jit(solution)/shard_map/ppermute | solution.py:30
  3.8 9.9 %collective-permute-start.1 = (f32[25,16,256]{2,1,0:T(8,128)}, f32[25,16,256]{2,1,0:T(8,128)S(1)}, u32[]{:S(2)}, u32[]{:S(2)}) collective-permute-start(f32[25,16,256]{2,1,0:T(8,128)} %get-tuple-element.28), channel_id=1, source_target_pairs={{1,2},{3,4},{5,6},{7,8},{9,10},{11,12},{13,14},{2,1},{4,3},{6,5},{... | collective-permute-start | bytes 1228808 | tf_op jit(solution)/shard_map/ppermute | solution.py:30
  4.5 1.9 %copy-start = (f32[2,6,16,4096]{3,2,1,0:T(8,128)S(1)}, f32[2,6,16,4096]{3,2,1,0:T(8,128)}, u32[]{:S(2)}) copy-start(f32[2,6,16,4096]{3,2,1,0:T(8,128)} %refs_0_.2) | copy-start | bytes 9437188
  6.4 1.9 %copy-start.2 = (f32[2,6,16,4096]{3,2,1,0:T(8,128)S(1)}, f32[2,6,16,4096]{3,2,1,0:T(8,128)}, u32[]{:S(2)}) copy-start(f32[2,6,16,4096]{3,2,1,0:T(8,128)} %refs_0_.3) | copy-start | bytes 9437188
  8.3 5.5 %copy-start.1 = (f32[2,6,16,4096]{3,2,1,0:T(8,128)S(1)}, f32[2,6,16,4096]{3,2,1,0:T(8,128)}, u32[]{:S(2)}) copy-start(f32[2,6,16,4096]{3,2,1,0:T(8,128)} %refs_0_.2) | copy-start | bytes 9437188
  14.3 15.2 %collective-permute-start.2 = (f32[1872,128]{1,0:T(8,128)S(1)}, f32[1872,128]{1,0:T(8,128)S(1)}, u32[]{:S(2)}, u32[]{:S(2)}) collective-permute-start(f32[1872,128]{1,0:T(8,128)S(1)} %get-tuple-element.41), channel_id=1, source_target_pairs={{16,32},{48,64},{80,96},{32,16},{64,48},{96,80},{17,33},{49,65},{8... | collective-permute-start | bytes 2875400 | tf_op jit(solution)/shard_map/ppermute | solution.py:30
  16.2 13.2 %copy-start.6 = (s32[2,3]{1,0:T(2,128)S(1)}, s32[2,3]{1,0:T(2,128)}, u32[]{:S(2)}) copy-start(s32[2,3]{1,0:T(2,128)} %cells.1) | copy-start | bytes 76
  16.2 13.2 %copy-start.7 = (f32[2,4]{1,0:T(2,128)S(1)}, f32[2,4]{1,0:T(2,128)}, u32[]{:S(2)}) copy-start(f32[2,4]{1,0:T(2,128)} %wave.1) | copy-start | bytes 100
  16.3 13.2 %collective-permute-start.3 = (f32[1872,128]{1,0:T(8,128)S(1)}, f32[1872,128]{1,0:T(8,128)S(1)}, u32[]{:S(2)}, u32[]{:S(2)}) collective-permute-start(f32[1872,128]{1,0:T(8,128)S(1)} %get-tuple-element.42), channel_id=1, source_target_pairs={{0,16},{32,48},{64,80},{96,112},{16,0},{48,32},{80,64},{112,96},{1... | collective-permute-start | bytes 2875400 | tf_op jit(solution)/shard_map/ppermute | solution.py:30
  18.9 22.1 %collective-permute-start.4 = (f32[1728,128]{1,0:T(8,128)S(1)}, f32[1728,128]{1,0:T(8,128)S(1)}, u32[]{:S(2)}, u32[]{:S(2)}) collective-permute-start(f32[1728,128]{1,0:T(8,128)S(1)} %get-tuple-element.45), channel_id=1, source_target_pairs={{16,32},{48,64},{80,96},{32,16},{64,48},{96,80},{17,33},{49,65},{8... | collective-permute-start | bytes 2654216 | tf_op jit(solution)/shard_map/ppermute | solution.py:30
  20.8 20.2 %copy-start.4 = (s32[4,16]{1,0:T(4,128)S(1)}, s32[4,16]{1,0:T(4,128)}, u32[]{:S(2)}) copy-start(s32[4,16]{1,0:T(4,128)} %owners.1) | copy-start | bytes 772
  20.8 20.2 %copy-start.5 = (s32[4,16]{1,0:T(4,128)S(1)}, s32[4,16]{1,0:T(4,128)}, u32[]{:S(2)}) copy-start(s32[4,16]{1,0:T(4,128)} %slots.1) | copy-start | bytes 772
  20.8 20.2 %collective-permute-start.5 = (f32[1728,128]{1,0:T(8,128)S(1)}, f32[1728,128]{1,0:T(8,128)S(1)}, u32[]{:S(2)}, u32[]{:S(2)}) collective-permute-start(f32[1728,128]{1,0:T(8,128)S(1)} %get-tuple-element.46), channel_id=1, source_target_pairs={{0,16},{32,48},{64,80},{96,112},{16,0},{48,32},{80,64},{112,96},{1... | collective-permute-start | bytes 2654216 | tf_op jit(solution)/shard_map/ppermute | solution.py:30
  41.0 31.4 %copy-start.8 = (s32[1,64]{1,0:T(1,128)S(1)}, s32[1,64]{1,0:T(1,128)}, u32[]{:S(2)}) copy-start(s32[1,64]{1,0:T(1,128)} %param.15) | copy-start | bytes 772
  55.1 32.1 %all-to-all-start = ((f32[32,16,128]{2,1,0:T(8,128)}), f32[32,16,128]{2,1,0:T(8,128)S(1)}, u32[]{:S(2)}, u32[]{:S(2)}) async-start(f32[32,16,128]{2,1,0:T(8,128)} %adjoint.1), calls=%async_computation | async-start | bytes 524288 | tf_op jit(solution)/shard_map/all_to_all | solution.py:507

commit v6 on v5

--- a/solution.py
+++ b/solution.py
@@ -43,24 +43,24 @@
     return lax.axis_index(axis) & 1
 
 
-def pack_y(fwd, adj, eps, far, near, rim, sems):
+def pack_y(fwd, adj, eps, f_far, f_near, a_far, a_near, rim, sems):
     at = (1 - odd("gy")) * (TJ - 2)
     copies = []
-    for i, (out, tile) in enumerate(((far, TJ - 2 - at), (near, at))):
+    for i, (out_f, out_a, tile) in enumerate(((f_far, a_far, TJ - 2 - at), (f_near, a_near, at))):
         where = pl.ds(pl.multiple_of(tile * W, W), 2 * W)
         copies.append(pltpu.make_async_copy(eps.at[:, where], rim.at[i], sems.at[i, 4]))
         for n in range(4):
-            state, src = (fwd, adj)[n // 2], n % 2
+            state, out, src = (fwd, adj)[n // 2], (out_f, out_a)[n // 2], n % 2
             copies.append(
                 pltpu.make_async_copy(
-                    state.at[src, :, :, where], out.at[pl.ds(6 * n, 6)], sems.at[i, n]
+                    state.at[src, :, :, where], out.at[pl.ds(6 * src, 6)], sems.at[i, n]
                 )
             )
     for copy in copies:
         copy.start()
-    for i, out in enumerate((far, near)):
+    for i, out in enumerate((f_far, f_near)):
         copies[5 * i].wait()
-        out[24] = COURANT / rim[i]
+        out[12] = COURANT / rim[i]
     for copy in copies[1:5] + copies[6:]:
         copy.wait()
 
@@ -96,29 +96,29 @@
         to_halves(lambda x, j: COURANT / eps[x : x + 8, lanes(j)], put, low)
 
 
-def pack_x(first, state, *rest):
+def pack_x(state, *rest):
     eps, y_far, y_near, far, near = rest if len(rest) == 5 else (None, *rest)
 
     def fill(lo, hi, dn, up):
-        def put(k, q, get):
+        def put(k, get):
             for j in range(TE):
                 row = aligned((k * TE + j) * 4, 4)
                 for out, x in ((dn, 0), (up, CX - 4)):
                     if j < 2:
-                        v = lo[q, x : x + 4, lanes(j)]
+                        v = lo[k, x : x + 4, lanes(j)]
                     elif j >= TE - 2:
-                        v = hi[q, x : x + 4, lanes(j - TE + 2)]
+                        v = hi[k, x : x + 4, lanes(j - TE + 2)]
                     else:
                         v = get(x, lanes(j - 2))
                     out[pl.ds(row, 4), :] = v
 
         def one(k, _):
-            put(k, first + k, lambda x, j: state[k // 6, k % 6, x : x + 4, j])
+            put(k, lambda x, j: state[k // 6, k % 6, x : x + 4, j])
             return 0
 
         lax.fori_loop(0, 12, one, 0)
         if eps is not None:
-            put(12, 24, lambda x, j: COURANT / eps[x : x + 4, j])
+            put(12, lambda x, j: COURANT / eps[x : x + 4, j])
 
     for px in range(2):
         for py in range(2):
@@ -151,15 +151,12 @@
                 put(r * XR + HALO + x, v)
 
 
-def order_ghosts(x_near, x_far, y_near, y_far, first, count, xg, yg):
+def order_ghosts(x_near, x_far, y_near, y_far, xg, yg):
     px, py = odd("gx"), odd("gy")
     xg[1 - px] = x_near[...]
     xg[px] = x_far[...]
-    yg[1 - py, 0:12] = y_near[first : first + 12]
-    yg[py, 0:12] = y_far[first : first + 12]
-    if count == 13:
-        yg[1 - py, 12] = y_near[24]
-        yg[py, 12] = y_far[24]
+    yg[1 - py] = y_near[...]
+    yg[py] = y_far[...]
 
 
 def masks():
@@ -265,7 +262,7 @@
     yg,
 ):
     low = masks()[0]
-    order_ghosts(x_near, x_far, y_near, y_far, 0, 13, xg, yg)
+    order_ghosts(x_near, x_far, y_near, y_far, xg, yg)
 
     def load(k, _):
         for ref, own, c in ((fe, own_e, 0), (fh, own_h, 3)):
@@ -326,7 +323,7 @@
     block,
 ):
     low = masks()[0]
-    order_ghosts(x_near, x_far, y_near, y_far, 12, 12, xg, yg)
+    order_ghosts(x_near, x_far, y_near, y_far, xg, yg)
 
     def load(k, _):
         for ref, own, c in ((fe, own_e, 0), (fh, own_h, 3)):
@@ -418,7 +415,7 @@
     )
 
 
-RIM = (25, CX, 2 * W)
+RIM = (CX, 2 * W)
 
 
 def call_pack_y():
@@ -426,20 +423,16 @@
     return pl.pallas_call(
         pack_y,
         in_specs=[hbm] * 3,
-        out_specs=[FULL] * 2,
-        out_shape=[buf(*RIM)] * 2,
-        scratch_shapes=[pltpu.VMEM((2, CX, 2 * W), F32), pltpu.SemaphoreType.DMA((2, 5))],
+        out_specs=[FULL] * 4,
+        out_shape=[buf(13, *RIM)] * 2 + [buf(12, *RIM)] * 2,
+        scratch_shapes=[pltpu.VMEM((2, *RIM), F32), pltpu.SemaphoreType.DMA((2, 5))],
         compiler_params=pltpu.CompilerParams(vmem_limit_bytes=62 << 20),
         name="pack_y",
     )
 
 
-def call_pack_x(first, count):
-    def kernel(*refs):
-        pack_x(first, *refs)
-
-    kernel.__name__ = "pack_x"
-    return call(kernel, 0, 3 + (count == 13), [buf(count * TE * 4, W)] * 2, us=1)
+def call_pack_x(count):
+    return call(pack_x, 0, 3 + (count == 13), [buf(count * TE * 4, W)] * 2, us=1)
 
 
 FIELD = (6, ROWS, W)
@@ -447,14 +440,14 @@
 
 
 def call_forward():
-    ghosts = [(2, 13 * TE * 4, W), (2, 13, CX, 2 * W)]
+    ghosts = [(2, 13 * TE * 4, W), (2, 13, *RIM)]
     return call(
         forward, 2, 7, [buf(STEPS, *FIELD), buf(ROWS, W)], [FIELD, FIELD, *ghosts], 12, 15
     )
 
 
 def call_adjoint():
-    ghosts = [(2, 12 * TE * 4, W), (2, 12, CX, 2 * W)]
+    ghosts = [(2, 12 * TE * 4, W), (2, 12, *RIM)]
     return call(
         adjoint,
         2,
@@ -476,21 +469,20 @@
     block_slot,
     owner_rows,
 ):
-    y_near, y_far = swapped(
-        *call_pack_y()(forward_state, adjoint_state, permittivity), "gy"
-    )
+    rows_y = call_pack_y()(forward_state, adjoint_state, permittivity)
+    fy_near, fy_far = swapped(*rows_y[:2], "gy")
+    ay_near, ay_far = swapped(*rows_y[2:], "gy")
     own = [buf(6, TR * CX, W)] * 2
     forward_own = call(convert, 0, 2, [*own, buf(TR * CX, W)])(forward_state, permittivity)
+    fy_near, fy_far, forward_own = lax.optimization_barrier((fy_near, fy_far, forward_own))
+    fx_near, fx_far = swapped(
+        *call_pack_x(13)(forward_state, permittivity, fy_far, fy_near), "gx"
+    )
+    ax_near, ax_far = swapped(*call_pack_x(12)(adjoint_state, ay_far, ay_near), "gx")
     adjoint_own = call(convert, 0, 1, own)(adjoint_state)
-    y_near, y_far, forward_own, adjoint_own = lax.optimization_barrier(
-        (y_near, y_far, forward_own, adjoint_own)
-    )
-    fx_near, fx_far = swapped(
-        *call_pack_x(0, 13)(forward_state, permittivity, y_far, y_near), "gx"
-    )
-    ax_near, ax_far = swapped(*call_pack_x(12, 12)(adjoint_state, y_far, y_near), "gx")
+    fx_near, fx_far, adjoint_own = lax.optimization_barrier((fx_near, fx_far, adjoint_own))
     inc, factor = call_forward()(
-        source_cell, waveform, *forward_own, fx_far, fx_near, y_far, y_near
+        source_cell, waveform, *forward_own, fx_far, fx_near, fy_far, fy_near
     )
     (outgoing,) = call_adjoint()(
         block_owner,
@@ -500,8 +492,8 @@
         inc,
         ax_far,
         ax_near,
-        y_far,
-        y_near,
+        ay_far,
+        ay_near,
     )
     outgoing, rows = lax.optimization_barrier((outgoing, owner_rows))
     arrived = lax.all_to_all(outgoing, ("gy", "src"), 0, 0, tiled=True)

time: 88.8 us -> 87.9 us (0.990)
  waiting for transfers between devices: 25.3 us -> 22.7 us
  starting transfers between devices: 27.6 us -> 29.4 us
    ppermute x6 -> x8, starting transfers between devices: 10.3 us -> 14.4 us  [swapped(): out.append(lax.ppermute(shard, axis, pairs + [(j, i) for i, j in pairs]))]
    ppermute x6 -> x8, waiting for transfers between devices: 10.6 us -> 7.15 us  [swapped(): out.append(lax.ppermute(shard, axis, pairs + [(j, i) for i, j in pairs]))]
    all_to_all x1, starting transfers between devices: 17.3 us -> 15 us  [per_device(): arrived = lax.all_to_all(outgoing, ('gy', 'src'), 0, 0, tiled=True)]
    unnamed x18 -> x16, local copies, waits for them, and re-layouts: 2.27 us -> 1.93 us
  transfers between devices with their start and end apart: 7 -> 9, of which waited for: 3 -> 2; matrix products, arithmetic and copies ran while one was open for 0% -> 0% of each run, Pallas kernels for 17% -> 18%
where the time goes in v6:
time: 87.9 us; the launch traced here: 87.6 us
  Pallas kernels  33.3 us (38%)
  starting transfers between devices  29.4 us (33%)
  waiting for transfers between devices  22.7 us (26%)
  local copies, waits for them, and re-layouts  1.93 us (2%)
    all_to_all x1, waiting for transfers between devices, per_device(): arrived = lax.all_to_all(outgoing, ('gy', 'src'), 0, 0, tiled=True)  15.5 us
    all_to_all x1, starting transfers between devices, per_device(): arrived = lax.all_to_all(outgoing, ('gy', 'src'), 0, 0, tiled=True)  15 us
    ppermute x8, starting transfers between devices, swapped(): out.append(lax.ppermute(shard, axis, pairs + [(j, i) for i, j in pairs]))  14.4 us
    pallas_call x1, Pallas kernels, per_device(): call_adjoint()  14.1 us
    pallas_call x1, Pallas kernels, per_device(): call_forward()  11.6 us
    ppermute x8, waiting for transfers between devices, swapped(): out.append(lax.ppermute(shard, axis, pairs + [(j, i) for i, j in pairs]))  7.15 us
    pallas_call x1, Pallas kernels, per_device(): rows_y = call_pack_y()(forward_state, adjoint_state, permittivity)  2.26 us
    unnamed x16, local copies, waits for them, and re-layouts  1.93 us
  transfers between devices with their start and end apart: 9, of which 2 were waited for; matrix products, arithmetic and copies ran while one was open for 0% of the time, Pallas kernels for 18%

profile of v6, /device:TPU:32, one launch (start us, length us, event | category | flops | bytes accessed | tf_op | source)
XLA Modules:
  0.0 87.6 jit_solution(9288675434524969721)
XLA Ops:
  0.0 0.0 copy-start.2
  0.0 2.3 %pack_y.1 = (f32[13,16,256]{2,1,0:T(8,128)}, f32[13,16,256]{2,1,0:T(8,128)}, f32[12,16,256]{2,1,0:T(8,128)}, f32[12,16,256]{2,1,0:T(8,128)}) custom-call(f32[2,6,16,4096]{3,2,1,0:T(8,128)} %state.5, f32[2,6,16,4096]{3,2,1,0:T(8,128)} %state.7, f32[16,4096]{1,0:T(8,128)} %rest_0_.3), custom_call_target="tpu_custom_call" | custom-call | tf_op jit(solution)/shard_map/pack_y/pallas_call | solution.py:472
  2.3 1.6 %collective-permute-start = (f32[13,16,256]{2,1,0:T(8,128)}, f32[13,16,256]{2,1,0:T(8,128)S(1)}, u32[]{:S(2)}, u32[]{:S(2)}) collective-permute-start(f32[13,16,256]{2,1,0:T(8,128)} %get-tuple-element.31), channel_id=1, source_target_pairs={{0,1},{2,3},{4,5},{6,7},{8,9},{10,11},{12,13},{14,15},{1,0},{3,2},... | collective-permute-start | bytes 638984 | tf_op jit(solution)/shard_map/ppermute | solution.py:30
  3.8 0.7 collective-permute-start.1
  4.5 0.7 collective-permute-start.4
  5.2 5.3 %collective-permute-start.5 = (f32[12,16,256]{2,1,0:T(8,128)}, f32[12,16,256]{2,1,0:T(8,128)S(1)}, u32[]{:S(2)}, u32[]{:S(2)}) collective-permute-start(f32[12,16,256]{2,1,0:T(8,128)} %get-tuple-element.52), channel_id=1, source_target_pairs={{0,1},{2,3},{4,5},{6,7},{8,9},{10,11},{12,13},{14,15},{1,0},{3,2},... | collective-permute-start | bytes 589832 | tf_op jit(solution)/shard_map/ppermute | solution.py:30
  10.5 0.0 copy-done.2
  10.5 0.0 copy-start.1
  10.5 1.9 %copy-done.1 = f32[2,6,16,4096]{3,2,1,0:T(8,128)S(1)} copy-done((f32[2,6,16,4096]{3,2,1,0:T(8,128)S(1)}, f32[2,6,16,4096]{3,2,1,0:T(8,128)}, u32[]{:S(2)}) %copy-start.1) | copy-done | bytes 3145752
  12.3 1.5 %convert.2 = (f32[6,640,128]{2,1,0:T(8,128)S(1)}, f32[6,640,128]{2,1,0:T(8,128)S(1)}, f32[640,128]{1,0:T(8,128)S(1)}) custom-call(f32[2,6,16,4096]{3,2,1,0:T(8,128)S(1)} %copy-done.1, f32[16,4096]{1,0:T(8,128)S(1)} %copy-done.2), custom_call_target="tpu_custom_call" | custom-call | flops 2000000 | bytes 6000000 | tf_op jit(solution)/shard_map/convert/pallas_call | solution.py:476
  13.9 0.0 copy-start
  13.9 0.0 collective-permute-done.rest_2_.y_near
  13.9 0.0 collective-permute-done.1.rest_1_.y_far
  13.9 0.6 pack_x.2
  14.5 0.1 collective-permute-start.2
  14.6 3.7 %collective-permute-start.3 = (f32[1872,128]{1,0:T(8,128)S(1)}, f32[1872,128]{1,0:T(8,128)S(1)}, u32[]{:S(2)}, u32[]{:S(2)}) collective-permute-start(f32[1872,128]{1,0:T(8,128)S(1)} %get-tuple-element.39), channel_id=1, source_target_pairs={{16,32},{48,64},{80,96},{32,16},{64,48},{96,80},{17,33},{49,65},{8... | collective-permute-start | bytes 2875400 | tf_op jit(solution)/shard_map/ppermute | solution.py:30
  18.3 0.0 collective-permute-done.4.rest_0_.y_far
  18.3 0.0 collective-permute-done.5.rest_1_.y_near
  18.3 0.0 copy-done
  18.3 0.5 pack_x.3
  18.8 0.0 copy-start.5
  18.8 0.0 copy-start.6
  18.9 2.0 %collective-permute-start.6 = (f32[1728,128]{1,0:T(8,128)S(1)}, f32[1728,128]{1,0:T(8,128)S(1)}, u32[]{:S(2)}, u32[]{:S(2)}) collective-permute-start(f32[1728,128]{1,0:T(8,128)S(1)} %get-tuple-element.53), channel_id=1, source_target_pairs={{16,32},{48,64},{80,96},{32,16},{64,48},{96,80},{17,33},{49,65},{8... | collective-permute-start | bytes 2654216 | tf_op jit(solution)/shard_map/ppermute | solution.py:30
  20.9 0.4 collective-permute-start.7
  21.3 1.4 %convert.3 = (f32[6,640,128]{2,1,0:T(8,128)S(1)}, f32[6,640,128]{2,1,0:T(8,128)S(1)}) custom-call(f32[2,6,16,4096]{3,2,1,0:T(8,128)S(1)} %copy-done), custom_call_target="tpu_custom_call" | custom-call | flops 2000000 | bytes 6000000 | tf_op jit(solution)/shard_map/convert/pallas_call | solution.py:482
  22.7 0.0 collective-permute-done.2.x_near
  22.7 7.1 %collective-permute-done.3.x_far = f32[1872,128]{1,0:T(8,128)S(1)} collective-permute-done((f32[1872,128]{1,0:T(8,128)S(1)}, f32[1872,128]{1,0:T(8,128)S(1)}, u32[]{:S(2)}, u32[]{:S(2)}) %collective-permute-start.3) | collective-permute-done | bytes 958496 | tf_op jit(solution)/shard_map/ppermute | solution.py:30
  29.9 0.0 copy-done.5
  29.9 0.0 copy-done.6
  29.9 0.0 copy-start.3
  29.9 0.0 copy-start.4
  29.9 11.6 %forward.1 = (f32[4,6,960,128]{3,2,1,0:T(8,128)S(1)}, f32[960,128]{1,0:T(8,128)S(1)}) custom-call(s32[2,3]{1,0:T(2,128)S(1)} %copy-done.5, f32[2,4]{1,0:T(2,128)S(1)} %copy-done.6, f32[6,640,128]{2,1,0:T(8,128)S(1)} %get-tuple-element.44.own_e, f32[6,640,128]{2,1,0:T(8,128)S(1)} %get-tuple-element.45.own_h, f32[640,128]{1,0:T(8,128)S(1)} %get-tuple-element.46.own_f, ...), custom_call_target="tpu_custom_call" | custom-call | flops 15000000 | bytes 45000000 | tf_op jit(solution)/shard_map/forward/pallas_call | solution.py:484
  41.5 0.0 collective-permute-done.6.x_far
  41.5 0.0 collective-permute-done.7.x_near
  41.5 0.0 copy-done.3
  41.5 0.0 copy-done.4
  41.5 0.0 copy-start.7
  41.5 14.1 %adjoint.1 = f32[32,16,128]{2,1,0:T(8,128)} custom-call(s32[4,16]{1,0:T(4,128)S(1)} %copy-done.3, s32[4,16]{1,0:T(4,128)S(1)} %copy-done.4, f32[6,640,128]{2,1,0:T(8,128)S(1)} %get-tuple-element.42.own_e, f32[6,640,128]{2,1,0:T(8,128)S(1)} %get-tuple-element.43.own_h, f32[960,128]{1,0:T(8,128)S(1)} %get-tuple-element.49.factor, ...), custom_call_target="tpu_custom_call" | custom-call | flops 15000000 | bytes 45000000 | tf_op jit(solution)/shard_map/adjoint/pallas_call | solution.py:487
  55.7 15.0 %all-to-all-start = ((f32[32,16,128]{2,1,0:T(8,128)}), f32[32,16,128]{2,1,0:T(8,128)S(1)}, u32[]{:S(2)}, u32[]{:S(2)}) async-start(f32[32,16,128]{2,1,0:T(8,128)} %adjoint.1), calls=%async_computation | async-start | bytes 524288 | tf_op jit(solution)/shard_map/all_to_all | solution.py:499
  70.7 0.0 copy-done.7
  70.7 15.5 %all-to-all-done.arrived = f32[32,16,128]{2,1,0:T(8,128)S(1)} async-done(((f32[32,16,128]{2,1,0:T(8,128)}), f32[32,16,128]{2,1,0:T(8,128)S(1)}, u32[]{:S(2)}, u32[]{:S(2)}) %all-to-all-start) | async-done | bytes 262176 | tf_op jit(solution)/shard_map/all_to_all | solution.py:499
  86.2 1.3 %place.1 = f32[64,512]{1,0:T(8,128)} custom-call(s32[1,64]{1,0:T(1,128)S(1)} %broadcast_multiply_fusion.rows, f32[32,16,128]{2,1,0:T(8,128)S(1)} %all-to-all-done.arrived), custom_call_target="tpu_custom_call" | custom-call | flops 2000000 | bytes 6000000 | tf_op jit(solution)/shard_map/place/pallas_call | solution.py:500
  (1 shorter events, 0.0 us)
Async XLA Ops:
  0.0 10.5 %copy-start.2 = (f32[16,4096]{1,0:T(8,128)S(1)}, f32[16,4096]{1,0:T(8,128)}, u32[]{:S(2)}) copy-start(f32[16,4096]{1,0:T(8,128)} %rest_0_.3) | copy-start | bytes 786436
  2.3 11.6 %collective-permute-start = (f32[13,16,256]{2,1,0:T(8,128)}, f32[13,16,256]{2,1,0:T(8,128)S(1)}, u32[]{:S(2)}, u32[]{:S(2)}) collective-permute-start(f32[13,16,256]{2,1,0:T(8,128)} %get-tuple-element.31), channel_id=1, source_target_pairs={{0,1},{2,3},{4,5},{6,7},{8,9},{10,11},{12,13},{14,15},{1,0},{3,2},... | collective-permute-start | bytes 638984 | tf_op jit(solution)/shard_map/ppermute | solution.py:30
  3.8 10.1 %collective-permute-start.1 = (f32[13,16,256]{2,1,0:T(8,128)}, f32[13,16,256]{2,1,0:T(8,128)S(1)}, u32[]{:S(2)}, u32[]{:S(2)}) collective-permute-start(f32[13,16,256]{2,1,0:T(8,128)} %get-tuple-element.32), channel_id=1, source_target_pairs={{1,2},{3,4},{5,6},{7,8},{9,10},{11,12},{13,14},{2,1},{4,3},{6,5},{... | collective-permute-start | bytes 638984 | tf_op jit(solution)/shard_map/ppermute | solution.py:30
  4.5 13.8 %collective-permute-start.4 = (f32[12,16,256]{2,1,0:T(8,128)}, f32[12,16,256]{2,1,0:T(8,128)S(1)}, u32[]{:S(2)}, u32[]{:S(2)}) collective-permute-start(f32[12,16,256]{2,1,0:T(8,128)} %get-tuple-element.51), channel_id=1, source_target_pairs={{1,2},{3,4},{5,6},{7,8},{9,10},{11,12},{13,14},{2,1},{4,3},{6,5},{... | collective-permute-start | bytes 589832 | tf_op jit(solution)/shard_map/ppermute | solution.py:30
  5.2 13.1 %collective-permute-start.5 = (f32[12,16,256]{2,1,0:T(8,128)}, f32[12,16,256]{2,1,0:T(8,128)S(1)}, u32[]{:S(2)}, u32[]{:S(2)}) collective-permute-start(f32[12,16,256]{2,1,0:T(8,128)} %get-tuple-element.52), channel_id=1, source_target_pairs={{0,1},{2,3},{4,5},{6,7},{8,9},{10,11},{12,13},{14,15},{1,0},{3,2},... | collective-permute-start | bytes 589832 | tf_op jit(solution)/shard_map/ppermute | solution.py:30
  10.5 1.9 %copy-start.1 = (f32[2,6,16,4096]{3,2,1,0:T(8,128)S(1)}, f32[2,6,16,4096]{3,2,1,0:T(8,128)}, u32[]{:S(2)}) copy-start(f32[2,6,16,4096]{3,2,1,0:T(8,128)} %state.5) | copy-start | bytes 9437188
  13.9 4.4 %copy-start = (f32[2,6,16,4096]{3,2,1,0:T(8,128)S(1)}, f32[2,6,16,4096]{3,2,1,0:T(8,128)}, u32[]{:S(2)}) copy-start(f32[2,6,16,4096]{3,2,1,0:T(8,128)} %state.7) | copy-start | bytes 9437188
  14.5 8.2 %collective-permute-start.2 = (f32[1872,128]{1,0:T(8,128)S(1)}, f32[1872,128]{1,0:T(8,128)S(1)}, u32[]{:S(2)}, u32[]{:S(2)}) collective-permute-start(f32[1872,128]{1,0:T(8,128)S(1)} %get-tuple-element.38), channel_id=1, source_target_pairs={{0,16},{32,48},{64,80},{96,112},{16,0},{48,32},{80,64},{112,96},{1... | collective-permute-start | bytes 2875400 | tf_op jit(solution)/shard_map/ppermute | solution.py:30
  14.6 15.3 %collective-permute-start.3 = (f32[1872,128]{1,0:T(8,128)S(1)}, f32[1872,128]{1,0:T(8,128)S(1)}, u32[]{:S(2)}, u32[]{:S(2)}) collective-permute-start(f32[1872,128]{1,0:T(8,128)S(1)} %get-tuple-element.39), channel_id=1, source_target_pairs={{16,32},{48,64},{80,96},{32,16},{64,48},{96,80},{17,33},{49,65},{8... | collective-permute-start | bytes 2875400 | tf_op jit(solution)/shard_map/ppermute | solution.py:30
  18.8 11.0 %copy-start.5 = (s32[2,3]{1,0:T(2,128)S(1)}, s32[2,3]{1,0:T(2,128)}, u32[]{:S(2)}) copy-start(s32[2,3]{1,0:T(2,128)} %cells.1) | copy-start | bytes 76
  18.8 11.0 %copy-start.6 = (f32[2,4]{1,0:T(2,128)S(1)}, f32[2,4]{1,0:T(2,128)}, u32[]{:S(2)}) copy-start(f32[2,4]{1,0:T(2,128)} %wave.1) | copy-start | bytes 100
  18.9 22.6 %collective-permute-start.6 = (f32[1728,128]{1,0:T(8,128)S(1)}, f32[1728,128]{1,0:T(8,128)S(1)}, u32[]{:S(2)}, u32[]{:S(2)}) collective-permute-start(f32[1728,128]{1,0:T(8,128)S(1)} %get-tuple-element.53), channel_id=1, source_target_pairs={{16,32},{48,64},{80,96},{32,16},{64,48},{96,80},{17,33},{49,65},{8... | collective-permute-start | bytes 2654216 | tf_op jit(solution)/shard_map/ppermute | solution.py:30
  20.9 20.6 %collective-permute-start.7 = (f32[1728,128]{1,0:T(8,128)S(1)}, f32[1728,128]{1,0:T(8,128)S(1)}, u32[]{:S(2)}, u32[]{:S(2)}) collective-permute-start(f32[1728,128]{1,0:T(8,128)S(1)} %get-tuple-element.54), channel_id=1, source_target_pairs={{0,16},{32,48},{64,80},{96,112},{16,0},{48,32},{80,64},{112,96},{1... | collective-permute-start | bytes 2654216 | tf_op jit(solution)/shard_map/ppermute | solution.py:30
  29.9 11.6 %copy-start.3 = (s32[4,16]{1,0:T(4,128)S(1)}, s32[4,16]{1,0:T(4,128)}, u32[]{:S(2)}) copy-start(s32[4,16]{1,0:T(4,128)} %owners.1) | copy-start | bytes 772
  29.9 11.6 %copy-start.4 = (s32[4,16]{1,0:T(4,128)S(1)}, s32[4,16]{1,0:T(4,128)}, u32[]{:S(2)}) copy-start(s32[4,16]{1,0:T(4,128)} %slots.1) | copy-start | bytes 772
  41.5 29.2 %copy-start.7 = (s32[1,64]{1,0:T(1,128)S(1)}, s32[1,64]{1,0:T(1,128)}, u32[]{:S(2)}) copy-start(s32[1,64]{1,0:T(1,128)} %param.15) | copy-start | bytes 772
  55.7 30.6 %all-to-all-start = ((f32[32,16,128]{2,1,0:T(8,128)}), f32[32,16,128]{2,1,0:T(8,128)S(1)}, u32[]{:S(2)}, u32[]{:S(2)}) async-start(f32[32,16,128]{2,1,0:T(8,128)} %adjoint.1), calls=%async_computation | async-start | bytes 524288 | tf_op jit(solution)/shard_map/all_to_all | solution.py:499

commit v7 on v6

--- a/solution.py
+++ b/solution.py
@@ -314,7 +314,8 @@
     x_near,
     y_far,
     y_near,
-    out,
+    keep,
+    give,
     fe,
     fh,
     xg,
@@ -361,7 +362,9 @@
                 for h in range(2):
                     b = ((2 * t + h) * (TJ // 2) + tile // 2) * 8 + tile % 2
                     block[pl.ds(b, 4, stride=2), :] = v[4 * h : 4 * h + 4]
-    out[...] = jnp.zeros_like(out)
+    keep[...] = jnp.zeros_like(keep)
+    give[...] = jnp.zeros_like(give)
+    mine = pl.multiple_of(lax.axis_index("src") * 4, 4)
 
     def send(i, _):
         o = owners[i // 16, i % 16]
@@ -370,8 +373,8 @@
         def _():
             c = pl.multiple_of(slots[i // 16, i % 16] * 4, 4)
             b = pl.multiple_of(i * 8, 8)
-            out[2 * o, pl.ds(c, 4), :] = block[pl.ds(b, 4), :]
-            out[2 * o + 1, pl.ds(c, 4), :] = block[pl.ds(b + 4, 4), :]
+            keep[o, pl.ds(c, 4), :] = block[pl.ds(b + mine, 4), :]
+            give[o, pl.ds(c, 4), :] = block[pl.ds(b + 4 - mine, 4), :]
 
         return 0
 
@@ -380,7 +383,7 @@
 
 def place(rows, arrived, out, wide):
     def one(g, _):
-        v = arrived[2 * g] + arrived[2 * g + 1]
+        v = arrived[g]
         for c in range(4):
             r = pl.multiple_of(rows[0, g * 4 + c], 4)
             wide[pl.ds(r, 4), :] = v[c * 4 : c * 4 + 4]
@@ -436,7 +439,7 @@
 
 
 FIELD = (6, ROWS, W)
-SENT = (32, 16, W)
+SENT = (16, 16, W)
 
 
 def call_forward():
@@ -452,7 +455,7 @@
         adjoint,
         2,
         8,
-        [buf(*SENT)],
+        [buf(*SENT)] * 2,
         [FIELD, FIELD, *ghosts, (ROWS, W), (64 * 8, W)],
         12,
         15,
@@ -484,7 +487,7 @@
     inc, factor = call_forward()(
         source_cell, waveform, *forward_own, fx_far, fx_near, fy_far, fy_near
     )
-    (outgoing,) = call_adjoint()(
+    keep, give = call_adjoint()(
         block_owner,
         block_slot,
         *adjoint_own,
@@ -495,8 +498,9 @@
         ay_far,
         ay_near,
     )
+    outgoing = keep + lax.ppermute(give, "src", [(0, 1), (1, 0)])
     outgoing, rows = lax.optimization_barrier((outgoing, owner_rows))
-    arrived = lax.all_to_all(outgoing, ("gy", "src"), 0, 0, tiled=True)
+    arrived = lax.all_to_all(outgoing, "gy", 0, 0, tiled=True)
     (placed,) = call(place, 1, 1, [buf(64, 512)], [(256, W)])(rows * 4, arrived)
     return placed
 

time: 87.9 us -> 86.4 us (0.983)
  waiting for transfers between devices: 22.7 us -> 20.9 us
    all_to_all x1, waiting for transfers between devices: 15.5 us -> 7.97 us  [per_device(): arrived = lax.all_to_all(outgoing, 'gy', 0, 0, tiled=True)]
    ppermute x0 -> x1, starting transfers between devices: none -> 6.38 us  [per_device(): outgoing = keep + lax.ppermute(give, 'src', [(0, 1), (1, 0)])]
    all_to_all x1, starting transfers between devices: 15 us -> 9.01 us  [per_device(): arrived = lax.all_to_all(outgoing, 'gy', 0, 0, tiled=True)]
    ppermute x0 -> x1, waiting for transfers between devices: none -> 5.78 us  [per_device(): outgoing = keep + lax.ppermute(give, 'src', [(0, 1), (1, 0)])]
  transfers between devices with their start and end apart: 9 -> 10, of which waited for: 2 -> 3; matrix products, arithmetic and copies ran while one was open for 0% -> 0% of each run, Pallas kernels for 18% -> 18%
where the time goes in v7:
time: 86.4 us; the launch traced here: 86.1 us
  Pallas kernels  32.6 us (38%)
  starting transfers between devices  29.8 us (34%)
  waiting for transfers between devices  20.9 us (24%)
  local copies, waits for them, and re-layouts  1.93 us (2%)
    ppermute x8, starting transfers between devices, swapped(): out.append(lax.ppermute(shard, axis, pairs + [(j, i) for i, j in pairs]))  14.4 us
    pallas_call x1, Pallas kernels, per_device(): call_adjoint()  13.4 us
    pallas_call x1, Pallas kernels, per_device(): call_forward()  11.6 us
    all_to_all x1, starting transfers between devices, per_device(): arrived = lax.all_to_all(outgoing, 'gy', 0, 0, tiled=True)  9.01 us
    all_to_all x1, waiting for transfers between devices, per_device(): arrived = lax.all_to_all(outgoing, 'gy', 0, 0, tiled=True)  7.97 us
    ppermute x8, waiting for transfers between devices, swapped(): out.append(lax.ppermute(shard, axis, pairs + [(j, i) for i, j in pairs]))  7.15 us
    ppermute x1, starting transfers between devices, per_device(): outgoing = keep + lax.ppermute(give, 'src', [(0, 1), (1, 0)])  6.38 us
    ppermute x1, waiting for transfers between devices, per_device(): outgoing = keep + lax.ppermute(give, 'src', [(0, 1), (1, 0)])  5.78 us
  transfers between devices with their start and end apart: 10, of which 3 were waited for; matrix products, arithmetic and copies ran while one was open for 0% of the time, Pallas kernels for 18%

profile of v7, /device:TPU:32, one launch (start us, length us, event | category | flops | bytes accessed | tf_op | source)
XLA Modules:
  0.0 86.1 jit_solution(8953527579807396197)
XLA Ops:
  0.0 0.0 copy-start.2
  0.0 2.2 %pack_y.1 = (f32[13,16,256]{2,1,0:T(8,128)}, f32[13,16,256]{2,1,0:T(8,128)}, f32[12,16,256]{2,1,0:T(8,128)}, f32[12,16,256]{2,1,0:T(8,128)}) custom-call(f32[2,6,16,4096]{3,2,1,0:T(8,128)} %state.5, f32[2,6,16,4096]{3,2,1,0:T(8,128)} %state.7, f32[16,4096]{1,0:T(8,128)} %rest_0_.3), custom_call_target="tpu_custom_call" | custom-call | tf_op jit(solution)/shard_map/pack_y/pallas_call | solution.py:475
  2.3 1.6 %collective-permute-start = (f32[13,16,256]{2,1,0:T(8,128)}, f32[13,16,256]{2,1,0:T(8,128)S(1)}, u32[]{:S(2)}, u32[]{:S(2)}) collective-permute-start(f32[13,16,256]{2,1,0:T(8,128)} %get-tuple-element.33), channel_id=1, source_target_pairs={{0,1},{2,3},{4,5},{6,7},{8,9},{10,11},{12,13},{14,15},{1,0},{3,2},... | collective-permute-start | bytes 638984 | tf_op jit(solution)/shard_map/ppermute | solution.py:30
  3.8 0.7 collective-permute-start.1
  4.5 0.7 collective-permute-start.4
  5.2 5.3 %collective-permute-start.5 = (f32[12,16,256]{2,1,0:T(8,128)}, f32[12,16,256]{2,1,0:T(8,128)S(1)}, u32[]{:S(2)}, u32[]{:S(2)}) collective-permute-start(f32[12,16,256]{2,1,0:T(8,128)} %get-tuple-element.54), channel_id=1, source_target_pairs={{0,1},{2,3},{4,5},{6,7},{8,9},{10,11},{12,13},{14,15},{1,0},{3,2},... | collective-permute-start | bytes 589832 | tf_op jit(solution)/shard_map/ppermute | solution.py:30
  10.4 0.0 copy-done.2
  10.4 0.0 copy-start.1
  10.4 1.9 %copy-done.1 = f32[2,6,16,4096]{3,2,1,0:T(8,128)S(1)} copy-done((f32[2,6,16,4096]{3,2,1,0:T(8,128)S(1)}, f32[2,6,16,4096]{3,2,1,0:T(8,128)}, u32[]{:S(2)}) %copy-start.1) | copy-done | bytes 3145752
  12.3 1.5 %convert.2 = (f32[6,640,128]{2,1,0:T(8,128)S(1)}, f32[6,640,128]{2,1,0:T(8,128)S(1)}, f32[640,128]{1,0:T(8,128)S(1)}) custom-call(f32[2,6,16,4096]{3,2,1,0:T(8,128)S(1)} %copy-done.1, f32[16,4096]{1,0:T(8,128)S(1)} %copy-done.2), custom_call_target="tpu_custom_call" | custom-call | flops 2000000 | bytes 6000000 | tf_op jit(solution)/shard_map/convert/pallas_call | solution.py:479
  13.9 0.0 copy-start
  13.9 0.0 collective-permute-done.rest_2_.y_near
  13.9 0.0 collective-permute-done.1.rest_1_.y_far
  13.9 0.6 pack_x.2
  14.5 0.1 collective-permute-start.2
  14.6 3.7 %collective-permute-start.3 = (f32[1872,128]{1,0:T(8,128)S(1)}, f32[1872,128]{1,0:T(8,128)S(1)}, u32[]{:S(2)}, u32[]{:S(2)}) collective-permute-start(f32[1872,128]{1,0:T(8,128)S(1)} %get-tuple-element.41), channel_id=1, source_target_pairs={{16,32},{48,64},{80,96},{32,16},{64,48},{96,80},{17,33},{49,65},{8... | collective-permute-start | bytes 2875400 | tf_op jit(solution)/shard_map/ppermute | solution.py:30
  18.3 0.0 collective-permute-done.4.rest_0_.y_far
  18.3 0.0 collective-permute-done.5.rest_1_.y_near
  18.3 0.0 copy-done
  18.3 0.5 pack_x.3
  18.8 0.0 copy-start.5
  18.8 0.0 copy-start.6
  18.9 2.0 %collective-permute-start.6 = (f32[1728,128]{1,0:T(8,128)S(1)}, f32[1728,128]{1,0:T(8,128)S(1)}, u32[]{:S(2)}, u32[]{:S(2)}) collective-permute-start(f32[1728,128]{1,0:T(8,128)S(1)} %get-tuple-element.55), channel_id=1, source_target_pairs={{16,32},{48,64},{80,96},{32,16},{64,48},{96,80},{17,33},{49,65},{8... | collective-permute-start | bytes 2654216 | tf_op jit(solution)/shard_map/ppermute | solution.py:30
  20.9 0.4 collective-permute-start.7
  21.3 1.4 %convert.3 = (f32[6,640,128]{2,1,0:T(8,128)S(1)}, f32[6,640,128]{2,1,0:T(8,128)S(1)}) custom-call(f32[2,6,16,4096]{3,2,1,0:T(8,128)S(1)} %copy-done), custom_call_target="tpu_custom_call" | custom-call | flops 2000000 | bytes 6000000 | tf_op jit(solution)/shard_map/convert/pallas_call | solution.py:485
  22.7 0.0 collective-permute-done.2.x_near
  22.7 7.1 %collective-permute-done.3.x_far = f32[1872,128]{1,0:T(8,128)S(1)} collective-permute-done((f32[1872,128]{1,0:T(8,128)S(1)}, f32[1872,128]{1,0:T(8,128)S(1)}, u32[]{:S(2)}, u32[]{:S(2)}) %collective-permute-start.3) | collective-permute-done | bytes 958496 | tf_op jit(solution)/shard_map/ppermute | solution.py:30
  29.9 0.0 copy-done.5
  29.9 0.0 copy-done.6
  29.9 0.0 copy-start.3
  29.9 0.0 copy-start.4
  29.9 11.6 %forward.1 = (f32[4,6,960,128]{3,2,1,0:T(8,128)S(1)}, f32[960,128]{1,0:T(8,128)S(1)}) custom-call(s32[2,3]{1,0:T(2,128)S(1)} %copy-done.5, f32[2,4]{1,0:T(2,128)S(1)} %copy-done.6, f32[6,640,128]{2,1,0:T(8,128)S(1)} %get-tuple-element.46.own_e, f32[6,640,128]{2,1,0:T(8,128)S(1)} %get-tuple-element.47.own_h, f32[640,128]{1,0:T(8,128)S(1)} %get-tuple-element.48.own_f, ...), custom_call_target="tpu_custom_call" | custom-call | flops 15000000 | bytes 45000000 | tf_op jit(solution)/shard_map/forward/pallas_call | solution.py:487
  41.5 0.0 collective-permute-done.6.x_far
  41.5 0.0 collective-permute-done.7.x_near
  41.5 0.0 copy-done.3
  41.5 0.0 copy-done.4
  41.5 0.0 copy-start.7
  41.5 13.4 %adjoint.1 = (f32[16,16,128]{2,1,0:T(8,128)S(1)}, f32[16,16,128]{2,1,0:T(8,128)S(1)}) custom-call(s32[4,16]{1,0:T(4,128)S(1)} %copy-done.3, s32[4,16]{1,0:T(4,128)S(1)} %copy-done.4, f32[6,640,128]{2,1,0:T(8,128)S(1)} %get-tuple-element.44.own_e, f32[6,640,128]{2,1,0:T(8,128)S(1)} %get-tuple-element.45.own_h, f32[960,128]{1,0:T(8,128)S(1)} %get-tuple-element.51.factor, ...), custom_call_target="tpu_custom_call" | custom-call | flops 15000000 | bytes 45000000 | tf_op jit(solution)/shard_map/adjoint/pallas_call | solution.py:490
  54.9 6.4 %collective-permute-start.8 = (f32[16,16,128]{2,1,0:T(8,128)S(1)}, f32[16,16,128]{2,1,0:T(8,128)S(1)}, u32[]{:S(2)}, u32[]{:S(2)}) collective-permute-start(f32[16,16,128]{2,1,0:T(8,128)S(1)} %get-tuple-element.58), channel_id=1, source_target_pairs={{0,128},{128,0},{1,129},{129,1},{2,130},{130,2},{3,131},{131,3},{4... | collective-permute-start | bytes 393224 | tf_op jit(solution)/shard_map/ppermute | solution.py:501
  61.3 5.8 %collective-permute-done.8 = f32[16,16,128]{2,1,0:T(8,128)S(1)} collective-permute-done((f32[16,16,128]{2,1,0:T(8,128)S(1)}, f32[16,16,128]{2,1,0:T(8,128)S(1)}, u32[]{:S(2)}, u32[]{:S(2)}) %collective-permute-start.8) | collective-permute-done | bytes 131104 | tf_op jit(solution)/shard_map/ppermute | solution.py:501
  67.1 0.7 add.3
  67.8 9.0 %all-to-all-start = ((f32[16,16,128]{2,1,0:T(8,128)}), f32[16,16,128]{2,1,0:T(8,128)S(1)}, u32[]{:S(2)}, u32[]{:S(2)}) async-start(f32[16,16,128]{2,1,0:T(8,128)} %add.3), calls=%async_computation | async-start | bytes 262144 | tf_op jit(solution)/shard_map/all_to_all | solution.py:503
  76.8 0.0 copy-done.7
  76.8 8.0 %all-to-all-done.arrived = f32[16,16,128]{2,1,0:T(8,128)S(1)} async-done(((f32[16,16,128]{2,1,0:T(8,128)}), f32[16,16,128]{2,1,0:T(8,128)S(1)}, u32[]{:S(2)}, u32[]{:S(2)}) %all-to-all-start) | async-done | bytes 131104 | tf_op jit(solution)/shard_map/all_to_all | solution.py:503
  84.8 1.3 %place.1 = f32[64,512]{1,0:T(8,128)} custom-call(s32[1,64]{1,0:T(1,128)S(1)} %broadcast_multiply_fusion.rows, f32[16,16,128]{2,1,0:T(8,128)S(1)} %all-to-all-done.arrived), custom_call_target="tpu_custom_call" | custom-call | flops 2000000 | bytes 6000000 | tf_op jit(solution)/shard_map/place/pallas_call | solution.py:504
  (1 shorter events, 0.0 us)
Async XLA Ops:
  0.0 10.4 %copy-start.2 = (f32[16,4096]{1,0:T(8,128)S(1)}, f32[16,4096]{1,0:T(8,128)}, u32[]{:S(2)}) copy-start(f32[16,4096]{1,0:T(8,128)} %rest_0_.3) | copy-start | bytes 786436
  2.3 11.6 %collective-permute-start = (f32[13,16,256]{2,1,0:T(8,128)}, f32[13,16,256]{2,1,0:T(8,128)S(1)}, u32[]{:S(2)}, u32[]{:S(2)}) collective-permute-start(f32[13,16,256]{2,1,0:T(8,128)} %get-tuple-element.33), channel_id=1, source_target_pairs={{0,1},{2,3},{4,5},{6,7},{8,9},{10,11},{12,13},{14,15},{1,0},{3,2},... | collective-permute-start | bytes 638984 | tf_op jit(solution)/shard_map/ppermute | solution.py:30
  3.8 10.1 %collective-permute-start.1 = (f32[13,16,256]{2,1,0:T(8,128)}, f32[13,16,256]{2,1,0:T(8,128)S(1)}, u32[]{:S(2)}, u32[]{:S(2)}) collective-permute-start(f32[13,16,256]{2,1,0:T(8,128)} %get-tuple-element.34), channel_id=1, source_target_pairs={{1,2},{3,4},{5,6},{7,8},{9,10},{11,12},{13,14},{2,1},{4,3},{6,5},{... | collective-permute-start | bytes 638984 | tf_op jit(solution)/shard_map/ppermute | solution.py:30
  4.5 13.8 %collective-permute-start.4 = (f32[12,16,256]{2,1,0:T(8,128)}, f32[12,16,256]{2,1,0:T(8,128)S(1)}, u32[]{:S(2)}, u32[]{:S(2)}) collective-permute-start(f32[12,16,256]{2,1,0:T(8,128)} %get-tuple-element.53), channel_id=1, source_target_pairs={{1,2},{3,4},{5,6},{7,8},{9,10},{11,12},{13,14},{2,1},{4,3},{6,5},{... | collective-permute-start | bytes 589832 | tf_op jit(solution)/shard_map/ppermute | solution.py:30
  5.2 13.1 %collective-permute-start.5 = (f32[12,16,256]{2,1,0:T(8,128)}, f32[12,16,256]{2,1,0:T(8,128)S(1)}, u32[]{:S(2)}, u32[]{:S(2)}) collective-permute-start(f32[12,16,256]{2,1,0:T(8,128)} %get-tuple-element.54), channel_id=1, source_target_pairs={{0,1},{2,3},{4,5},{6,7},{8,9},{10,11},{12,13},{14,15},{1,0},{3,2},... | collective-permute-start | bytes 589832 | tf_op jit(solution)/shard_map/ppermute | solution.py:30
  10.4 1.9 %copy-start.1 = (f32[2,6,16,4096]{3,2,1,0:T(8,128)S(1)}, f32[2,6,16,4096]{3,2,1,0:T(8,128)}, u32[]{:S(2)}) copy-start(f32[2,6,16,4096]{3,2,1,0:T(8,128)} %state.5) | copy-start | bytes 9437188
  13.9 4.4 %copy-start = (f32[2,6,16,4096]{3,2,1,0:T(8,128)S(1)}, f32[2,6,16,4096]{3,2,1,0:T(8,128)}, u32[]{:S(2)}) copy-start(f32[2,6,16,4096]{3,2,1,0:T(8,128)} %state.7) | copy-start | bytes 9437188
  14.5 8.2 %collective-permute-start.2 = (f32[1872,128]{1,0:T(8,128)S(1)}, f32[1872,128]{1,0:T(8,128)S(1)}, u32[]{:S(2)}, u32[]{:S(2)}) collective-permute-start(f32[1872,128]{1,0:T(8,128)S(1)} %get-tuple-element.40), channel_id=1, source_target_pairs={{0,16},{32,48},{64,80},{96,112},{16,0},{48,32},{80,64},{112,96},{1... | collective-permute-start | bytes 2875400 | tf_op jit(solution)/shard_map/ppermute | solution.py:30
  14.6 15.3 %collective-permute-start.3 = (f32[1872,128]{1,0:T(8,128)S(1)}, f32[1872,128]{1,0:T(8,128)S(1)}, u32[]{:S(2)}, u32[]{:S(2)}) collective-permute-start(f32[1872,128]{1,0:T(8,128)S(1)} %get-tuple-element.41), channel_id=1, source_target_pairs={{16,32},{48,64},{80,96},{32,16},{64,48},{96,80},{17,33},{49,65},{8... | collective-permute-start | bytes 2875400 | tf_op jit(solution)/shard_map/ppermute | solution.py:30
  18.8 11.0 %copy-start.5 = (s32[2,3]{1,0:T(2,128)S(1)}, s32[2,3]{1,0:T(2,128)}, u32[]{:S(2)}) copy-start(s32[2,3]{1,0:T(2,128)} %cells.1) | copy-start | bytes 76
  18.8 11.0 %copy-start.6 = (f32[2,4]{1,0:T(2,128)S(1)}, f32[2,4]{1,0:T(2,128)}, u32[]{:S(2)}) copy-start(f32[2,4]{1,0:T(2,128)} %wave.1) | copy-start | bytes 100
  18.9 22.6 %collective-permute-start.6 = (f32[1728,128]{1,0:T(8,128)S(1)}, f32[1728,128]{1,0:T(8,128)S(1)}, u32[]{:S(2)}, u32[]{:S(2)}) collective-permute-start(f32[1728,128]{1,0:T(8,128)S(1)} %get-tuple-element.55), channel_id=1, source_target_pairs={{16,32},{48,64},{80,96},{32,16},{64,48},{96,80},{17,33},{49,65},{8... | collective-permute-start | bytes 2654216 | tf_op jit(solution)/shard_map/ppermute | solution.py:30
  20.9 20.6 %collective-permute-start.7 = (f32[1728,128]{1,0:T(8,128)S(1)}, f32[1728,128]{1,0:T(8,128)S(1)}, u32[]{:S(2)}, u32[]{:S(2)}) collective-permute-start(f32[1728,128]{1,0:T(8,128)S(1)} %get-tuple-element.56), channel_id=1, source_target_pairs={{0,16},{32,48},{64,80},{96,112},{16,0},{48,32},{80,64},{112,96},{1... | collective-permute-start | bytes 2654216 | tf_op jit(solution)/shard_map/ppermute | solution.py:30
  29.9 11.6 %copy-start.3 = (s32[4,16]{1,0:T(4,128)S(1)}, s32[4,16]{1,0:T(4,128)}, u32[]{:S(2)}) copy-start(s32[4,16]{1,0:T(4,128)} %owners.1) | copy-start | bytes 772
  29.9 11.6 %copy-start.4 = (s32[4,16]{1,0:T(4,128)S(1)}, s32[4,16]{1,0:T(4,128)}, u32[]{:S(2)}) copy-start(s32[4,16]{1,0:T(4,128)} %slots.1) | copy-start | bytes 772
  41.5 35.3 %copy-start.7 = (s32[1,64]{1,0:T(1,128)S(1)}, s32[1,64]{1,0:T(1,128)}, u32[]{:S(2)}) copy-start(s32[1,64]{1,0:T(1,128)} %param.15) | copy-start | bytes 772
  54.9 12.2 %collective-permute-start.8 = (f32[16,16,128]{2,1,0:T(8,128)S(1)}, f32[16,16,128]{2,1,0:T(8,128)S(1)}, u32[]{:S(2)}, u32[]{:S(2)}) collective-permute-start(f32[16,16,128]{2,1,0:T(8,128)S(1)} %get-tuple-element.58), channel_id=1, source_target_pairs={{0,128},{128,0},{1,129},{129,1},{2,130},{130,2},{3,131},{131,3},{4... | collective-permute-start | bytes 393224 | tf_op jit(solution)/shard_map/ppermute | solution.py:501
  67.8 17.0 %all-to-all-start = ((f32[16,16,128]{2,1,0:T(8,128)}), f32[16,16,128]{2,1,0:T(8,128)S(1)}, u32[]{:S(2)}, u32[]{:S(2)}) async-start(f32[16,16,128]{2,1,0:T(8,128)} %add.3), calls=%async_computation | async-start | bytes 262144 | tf_op jit(solution)/shard_map/all_to_all | solution.py:503

commit v8 on v6

--- a/solution.py
+++ b/solution.py
@@ -16,19 +16,17 @@
 TR = HY + 2 * HALO
 TE = TJ + 4
 ROWS = TR * XR
-UNROLL = 6
+LBY = CY // 4
+LB = LBY * CX // 4
+UNROLL = 8
 W = 128
 COURANT = 0.55
 F32 = jnp.float32
 
 
-def swapped(far, near, axis):
-    count = lax.axis_size(axis)
-    out = []
-    for shard, first in ((near, 0), (far, 1)):
-        pairs = [(i, i + 1) for i in range(first, count - 1, 2)]
-        out.append(lax.ppermute(shard, axis, pairs + [(j, i) for i, j in pairs]))
-    return out[0], out[1]
+def swapped(shard, axis, first):
+    pairs = [(i, i + 1) for i in range(first, lax.axis_size(axis) - 1, 2)]
+    return lax.ppermute(shard, axis, pairs + [(j, i) for i, j in pairs])
 
 
 def lanes(tile):
@@ -321,6 +319,7 @@
     yg,
     density,
     block,
+    sent,
 ):
     low = masks()[0]
     order_ghosts(x_near, x_far, y_near, y_far, xg, yg)
@@ -361,28 +360,22 @@
                 for h in range(2):
                     b = ((2 * t + h) * (TJ // 2) + tile // 2) * 8 + tile % 2
                     block[pl.ds(b, 4, stride=2), :] = v[4 * h : 4 * h + 4]
-    out[...] = jnp.zeros_like(out)
-
-    def send(i, _):
-        o = owners[i // 16, i % 16]
-
-        @pl.when(o >= 0)
-        def _():
-            c = pl.multiple_of(slots[i // 16, i % 16] * 4, 4)
-            b = pl.multiple_of(i * 8, 8)
-            out[2 * o, pl.ds(c, 4), :] = block[pl.ds(b, 4), :]
-            out[2 * o + 1, pl.ds(c, 4), :] = block[pl.ds(b + 4, 4), :]
-
-        return 0
-
-    lax.fori_loop(0, 64, send, 0)
+    sent[...] = jnp.zeros_like(sent)
+    for i in range(LB):
+        o = owners[i // LBY, i % LBY]
+        o0 = jnp.where(o < 0, 32, o)
+        o1 = jnp.where(o < 0, 32, 16 + o)
+        c = pl.multiple_of(jnp.maximum(slots[i // LBY, i % LBY], 0) * 4, 4)
+        sent[o0, pl.ds(c, 4), :] = block[8 * i : 8 * i + 4, :]
+        sent[o1, pl.ds(c, 4), :] = block[8 * i + 4 : 8 * i + 8, :]
+    out[...] = sent[0:32]
 
 
 def place(rows, arrived, out, wide):
     def one(g, _):
-        v = arrived[2 * g] + arrived[2 * g + 1]
+        v = arrived[g] + arrived[16 + g]
         for c in range(4):
-            r = pl.multiple_of(rows[0, g * 4 + c], 4)
+            r = pl.multiple_of(rows[0, g * 4 + c] * 4, 4)
             wide[pl.ds(r, 4), :] = v[c * 4 : c * 4 + 4]
         return 0
 
@@ -453,7 +446,7 @@
         2,
         8,
         [buf(*SENT)],
-        [FIELD, FIELD, *ghosts, (ROWS, W), (64 * 8, W)],
+        [FIELD, FIELD, *ghosts, (ROWS, W), (LB * 8, W), (33, 16, W)],
         12,
         15,
     )
@@ -470,17 +463,18 @@
     owner_rows,
 ):
     rows_y = call_pack_y()(forward_state, adjoint_state, permittivity)
-    fy_near, fy_far = swapped(*rows_y[:2], "gy")
-    ay_near, ay_far = swapped(*rows_y[2:], "gy")
+    fy_far, fy_near = (swapped(rows_y[i], "gy", 1 - i) for i in range(2))
+    ay_far, ay_near = (swapped(rows_y[2 + i], "gy", 1 - i) for i in range(2))
     own = [buf(6, TR * CX, W)] * 2
+    adjoint_own = call(convert, 0, 1, own)(adjoint_state)
+    fy_far, fy_near, adjoint_own = lax.optimization_barrier((fy_far, fy_near, adjoint_own))
+    fx = call_pack_x(13)(forward_state, permittivity, fy_far, fy_near)
+    fx_far, fx_near = (swapped(fx[i], "gx", 1 - i) for i in range(2))
+    ax = call_pack_x(12)(adjoint_state, ay_far, ay_near)
+    ax_near = swapped(ax[1], "gx", 0)
     forward_own = call(convert, 0, 2, [*own, buf(TR * CX, W)])(forward_state, permittivity)
-    fy_near, fy_far, forward_own = lax.optimization_barrier((fy_near, fy_far, forward_own))
-    fx_near, fx_far = swapped(
-        *call_pack_x(13)(forward_state, permittivity, fy_far, fy_near), "gx"
-    )
-    ax_near, ax_far = swapped(*call_pack_x(12)(adjoint_state, ay_far, ay_near), "gx")
-    adjoint_own = call(convert, 0, 1, own)(adjoint_state)
-    fx_near, fx_far, adjoint_own = lax.optimization_barrier((fx_near, fx_far, adjoint_own))
+    fx_far, ax_far, forward_own = lax.optimization_barrier((fx_far, ax[0], forward_own))
+    ax_far = swapped(ax_far, "gx", 1)
     inc, factor = call_forward()(
         source_cell, waveform, *forward_own, fx_far, fx_near, fy_far, fy_near
     )
@@ -495,9 +489,8 @@
         ay_far,
         ay_near,
     )
-    outgoing, rows = lax.optimization_barrier((outgoing, owner_rows))
-    arrived = lax.all_to_all(outgoing, ("gy", "src"), 0, 0, tiled=True)
-    (placed,) = call(place, 1, 1, [buf(64, 512)], [(256, W)])(rows * 4, arrived)
+    arrived = lax.all_to_all(outgoing, ("src", "gy"), 0, 0, tiled=True)
+    (placed,) = call(place, 1, 1, [buf(64, 512)], [(256, W)])(owner_rows, arrived)
     return placed
 
 

time: 87.9 us -> 84.9 us (0.966)
  blocking collectives: 0 us -> 28.2 us
  waiting for transfers between devices: 22.7 us -> 6.74 us
  starting transfers between devices: 29.4 us -> 16.6 us
  Pallas kernels: 33.3 us -> 31 us
    all_to_all x0 -> x1, blocking collectives: none -> 28.2 us  [per_device(): arrived = lax.all_to_all(outgoing, ('src', 'gy'), 0, 0, tiled=True)]
    all_to_all x1 -> x0, waiting for transfers between devices: 15.5 us -> none  [per_device(): arrived = lax.all_to_all(outgoing, ('gy', 'src'), 0, 0, tiled=True)]
    all_to_all x1 -> x0, starting transfers between devices: 15 us -> none  [per_device(): arrived = lax.all_to_all(outgoing, ('gy', 'src'), 0, 0, tiled=True)]
    ppermute x8, starting transfers between devices: 14.4 us -> 16.6 us  [swapped(): return lax.ppermute(shard, axis, pairs + [(j, i) for i, j in pairs])]
    pallas_call x1, Pallas kernels: 14.1 us -> 12.2 us  [per_device(): call_adjoint()]
    unnamed x16 -> x22, local copies, waits for them, and re-layouts: 1.93 us -> 1.93 us
  transfers between devices with their start and end apart: 9 -> 8, of which waited for: 2 -> 4; matrix products, arithmetic and copies ran while one was open for 0% -> 0% of each run, Pallas kernels for 18% -> 17%
where the time goes in v8:
time: 84.9 us; the launch traced here: 84.7 us
  Pallas kernels  31 us (37%)
  blocking collectives  28.2 us (33%)
  starting transfers between devices  16.6 us (20%)
  waiting for transfers between devices  6.74 us (8%)
  local copies, waits for them, and re-layouts  1.93 us (2%)
    all_to_all x1, blocking collectives, per_device(): arrived = lax.all_to_all(outgoing, ('src', 'gy'), 0, 0, tiled=True)  28.2 us
    ppermute x8, starting transfers between devices, swapped(): return lax.ppermute(shard, axis, pairs + [(j, i) for i, j in pairs])  16.6 us
    pallas_call x1, Pallas kernels, per_device(): call_adjoint()  12.2 us
    pallas_call x1, Pallas kernels, per_device(): call_forward()  11.2 us
    ppermute x8, waiting for transfers between devices, swapped(): return lax.ppermute(shard, axis, pairs + [(j, i) for i, j in pairs])  6.74 us
    pallas_call x1, Pallas kernels, per_device(): rows_y = call_pack_y()(forward_state, adjoint_state, permittivity)  2.27 us
    unnamed x22, local copies, waits for them, and re-layouts  1.93 us
  transfers between devices with their start and end apart: 8, of which 4 were waited for; matrix products, arithmetic and copies ran while one was open for 0% of the time, Pallas kernels for 17%

profile of v8, /device:TPU:32, one launch (start us, length us, event | category | flops | bytes accessed | tf_op | source)
XLA Modules:
  0.0 84.7 jit_solution(9131751887370315541)
XLA Ops:
  0.0 0.0 copy-start.3
  0.0 2.3 %pack_y.1 = (f32[13,16,256]{2,1,0:T(8,128)}, f32[13,16,256]{2,1,0:T(8,128)}, f32[12,16,256]{2,1,0:T(8,128)}, f32[12,16,256]{2,1,0:T(8,128)}) custom-call(f32[2,6,16,4096]{3,2,1,0:T(8,128)} %state.7, f32[2,6,16,4096]{3,2,1,0:T(8,128)} %state.6, f32[16,4096]{1,0:T(8,128)} %rest_0_.3), custom_call_target="tpu_custom_call" | custom-call | tf_op jit(solution)/shard_map/pack_y/pallas_call | solution.py:465
  2.3 0.7 collective-permute-start
  3.0 4.3 %collective-permute-start.1 = (f32[13,16,256]{2,1,0:T(8,128)}, f32[13,16,256]{2,1,0:T(8,128)S(1)}, u32[]{:S(2)}, u32[]{:S(2)}) collective-permute-start(f32[13,16,256]{2,1,0:T(8,128)} %get-tuple-element.30), channel_id=1, source_target_pairs={{0,1},{2,3},{4,5},{6,7},{8,9},{10,11},{12,13},{14,15},{1,0},{3,2},... | collective-permute-start | bytes 638984 | tf_op jit(solution)/shard_map/ppermute | solution.py:29
  7.3 0.0 copy-start
  7.3 1.9 %copy-done = f32[2,6,16,4096]{3,2,1,0:T(8,128)S(1)} copy-done((f32[2,6,16,4096]{3,2,1,0:T(8,128)S(1)}, f32[2,6,16,4096]{3,2,1,0:T(8,128)}, u32[]{:S(2)}) %copy-start) | copy-done | bytes 3145752
  9.2 0.0 copy-start.2
  9.2 1.4 %convert.2 = (f32[6,640,128]{2,1,0:T(8,128)S(1)}, f32[6,640,128]{2,1,0:T(8,128)S(1)}) custom-call(f32[2,6,16,4096]{3,2,1,0:T(8,128)S(1)} %copy-done), custom_call_target="tpu_custom_call" | custom-call | flops 2000000 | bytes 6000000 | tf_op jit(solution)/shard_map/convert/pallas_call | solution.py:469
  10.6 0.0 copy-start.10
  10.6 0.0 copy-start.9
  10.6 0.0 collective-permute-done.rest_1_.y_far
  10.6 1.8 %collective-permute-done.1.rest_2_.y_near = f32[13,16,256]{2,1,0:T(8,128)S(1)} collective-permute-done((f32[13,16,256]{2,1,0:T(8,128)}, f32[13,16,256]{2,1,0:T(8,128)S(1)}, u32[]{:S(2)}, u32[]{:S(2)}) %collective-permute-start.1) | collective-permute-done | bytes 213024 | tf_op jit(solution)/shard_map/ppermute | solution.py:29
  12.4 0.0 copy-done.3
  12.4 0.0 copy-done.2
  12.5 0.5 pack_x.2
  13.0 0.0 copy-start.1
  13.0 2.2 %collective-permute-start.2 = (f32[1872,128]{1,0:T(8,128)S(1)}, f32[1872,128]{1,0:T(8,128)S(1)}, u32[]{:S(2)}, u32[]{:S(2)}) collective-permute-start(f32[1872,128]{1,0:T(8,128)S(1)} %get-tuple-element.37), channel_id=1, source_target_pairs={{16,32},{48,64},{80,96},{32,16},{64,48},{96,80},{17,33},{49,65},{8... | collective-permute-start | bytes 2875400 | tf_op jit(solution)/shard_map/ppermute | solution.py:29
  15.2 0.0 copy-done.10
  15.2 0.7 collective-permute-start.3
  15.9 0.0 copy-done.9
  15.9 4.0 %collective-permute-start.4 = (f32[12,16,256]{2,1,0:T(8,128)S(1)}, f32[12,16,256]{2,1,0:T(8,128)S(1)}, u32[]{:S(2)}, u32[]{:S(2)}) collective-permute-start(f32[12,16,256]{2,1,0:T(8,128)S(1)} %copy-done.9), channel_id=1, source_target_pairs={{0,1},{2,3},{4,5},{6,7},{8,9},{10,11},{12,13},{14,15},{1,0},{3,2},... | collective-permute-start | bytes 589832 | tf_op jit(solution)/shard_map/ppermute | solution.py:29
  19.9 1.5 %collective-permute-start.5 = (f32[1872,128]{1,0:T(8,128)S(1)}, f32[1872,128]{1,0:T(8,128)S(1)}, u32[]{:S(2)}, u32[]{:S(2)}) collective-permute-start(f32[1872,128]{1,0:T(8,128)S(1)} %get-tuple-element.48), channel_id=1, source_target_pairs={{0,16},{32,48},{64,80},{96,112},{16,0},{48,32},{80,64},{112,96},{1... | collective-permute-start | bytes 2875400 | tf_op jit(solution)/shard_map/ppermute | solution.py:29
  21.4 1.5 %convert.3 = (f32[6,640,128]{2,1,0:T(8,128)S(1)}, f32[6,640,128]{2,1,0:T(8,128)S(1)}, f32[640,128]{1,0:T(8,128)S(1)}) custom-call(f32[2,6,16,4096]{3,2,1,0:T(8,128)S(1)} %copy-done.2, f32[16,4096]{1,0:T(8,128)S(1)} %copy-done.3), custom_call_target="tpu_custom_call" | custom-call | flops 2000000 | bytes 6000000 | tf_op jit(solution)/shard_map/convert/pallas_call | solution.py:475
  22.9 0.0 copy-start.6
  22.9 0.0 copy-start.7
  22.9 0.0 collective-permute-done.3.rest_0_.y_far
  22.9 1.7 %collective-permute-done.4.rest_1_.y_near = f32[12,16,256]{2,1,0:T(8,128)S(1)} collective-permute-done((f32[12,16,256]{2,1,0:T(8,128)S(1)}, f32[12,16,256]{2,1,0:T(8,128)S(1)}, u32[]{:S(2)}, u32[]{:S(2)}) %collective-permute-start.4) | collective-permute-done | bytes 196640 | tf_op jit(solution)/shard_map/ppermute | solution.py:29
  24.6 0.0 copy-done.1
  24.6 0.5 pack_x.3
  25.1 1.2 %collective-permute-start.7 = (f32[1728,128]{1,0:T(8,128)S(1)}, f32[1728,128]{1,0:T(8,128)S(1)}, u32[]{:S(2)}, u32[]{:S(2)}) collective-permute-start(f32[1728,128]{1,0:T(8,128)S(1)} %get-tuple-element.52), channel_id=1, source_target_pairs={{0,16},{32,48},{64,80},{96,112},{16,0},{48,32},{80,64},{112,96},{1... | collective-permute-start | bytes 2654216 | tf_op jit(solution)/shard_map/ppermute | solution.py:29
  26.3 2.1 %collective-permute-done.2.x_far = f32[1872,128]{1,0:T(8,128)S(1)} collective-permute-done((f32[1872,128]{1,0:T(8,128)S(1)}, f32[1872,128]{1,0:T(8,128)S(1)}, u32[]{:S(2)}, u32[]{:S(2)}) %collective-permute-start.2) | collective-permute-done | bytes 958496 | tf_op jit(solution)/shard_map/ppermute | solution.py:29
  28.4 0.0 copy-start.4
  28.4 0.0 copy-start.5
  28.4 2.0 %collective-permute-start.6 = (f32[1728,128]{1,0:T(8,128)S(1)}, f32[1728,128]{1,0:T(8,128)S(1)}, u32[]{:S(2)}, u32[]{:S(2)}) collective-permute-start(f32[1728,128]{1,0:T(8,128)S(1)} %get-tuple-element.51), channel_id=1, source_target_pairs={{16,32},{48,64},{80,96},{32,16},{64,48},{96,80},{17,33},{49,65},{8... | collective-permute-start | bytes 2654216 | tf_op jit(solution)/shard_map/ppermute | solution.py:29
  30.5 0.0 collective-permute-done.5.x_near
  30.5 0.0 copy-done.6
  30.5 0.0 copy-done.7
  30.5 11.2 %forward.1 = (f32[4,6,960,128]{3,2,1,0:T(8,128)S(1)}, f32[960,128]{1,0:T(8,128)S(1)}) custom-call(s32[2,3]{1,0:T(2,128)S(1)} %copy-done.6, f32[2,4]{1,0:T(2,128)S(1)} %copy-done.7, f32[6,640,128]{2,1,0:T(8,128)S(1)} %get-tuple-element.44.own_e, f32[6,640,128]{2,1,0:T(8,128)S(1)} %get-tuple-element.45.own_h, f32[640,128]{1,0:T(8,128)S(1)} %get-tuple-element.46.own_f, ...), custom_call_target="tpu_custom_call" | custom-call | flops 15000000 | bytes 45000000 | tf_op jit(solution)/shard_map/forward/pallas_call | solution.py:478
  41.7 0.0 collective-permute-done.7.x_near
  41.8 1.2 %collective-permute-done.6.x_far = f32[1728,128]{1,0:T(8,128)S(1)} collective-permute-done((f32[1728,128]{1,0:T(8,128)S(1)}, f32[1728,128]{1,0:T(8,128)S(1)}, u32[]{:S(2)}, u32[]{:S(2)}) %collective-permute-start.6) | collective-permute-done | bytes 884768 | tf_op jit(solution)/shard_map/ppermute | solution.py:29
  42.9 0.0 copy-done.4
  42.9 0.0 copy-done.5
  42.9 0.0 copy-start.8
  42.9 12.2 %adjoint.1 = f32[32,16,128]{2,1,0:T(8,128)S(1)} custom-call(s32[4,16]{1,0:T(4,128)S(1)} %copy-done.4, s32[4,16]{1,0:T(4,128)S(1)} %copy-done.5, f32[6,640,128]{2,1,0:T(8,128)S(1)} %get-tuple-element.33.own_e, f32[6,640,128]{2,1,0:T(8,128)S(1)} %get-tuple-element.34.own_h, f32[960,128]{1,0:T(8,128)S(1)} %get-tuple-element.49.factor, ...), custom_call_target="tpu_custom_call" | custom-call | flops 15000000 | bytes 45000000 | tf_op jit(solution)/shard_map/adjoint/pallas_call | solution.py:481
  55.1 28.2 %all_to_all.5.arrived = f32[32,16,128]{2,1,0:T(8,128)S(1)} all-to-all(f32[32,16,128]{2,1,0:T(8,128)S(1)} %adjoint.1), channel_id=1, replica_groups=mesh['src'=2,'gx'=8,'gy'=16] {'src','gy'}, dimensions={0} | all-to-all | bytes 524288 | tf_op jit(solution)/shard_map/all_to_all | solution.py:492
  83.3 0.0 copy-done.8
  83.3 1.3 %place.1 = f32[64,512]{1,0:T(8,128)} custom-call(s32[1,64]{1,0:T(1,128)S(1)} %copy-done.8, f32[32,16,128]{2,1,0:T(8,128)S(1)} %all_to_all.5.arrived), custom_call_target="tpu_custom_call" | custom-call | flops 2000000 | bytes 6000000 | tf_op jit(solution)/shard_map/place/pallas_call | solution.py:493
Async XLA Ops:
  0.0 12.4 %copy-start.3 = (f32[16,4096]{1,0:T(8,128)S(1)}, f32[16,4096]{1,0:T(8,128)}, u32[]{:S(2)}) copy-start(f32[16,4096]{1,0:T(8,128)} %rest_0_.3) | copy-start | bytes 786436
  2.3 8.3 %collective-permute-start = (f32[13,16,256]{2,1,0:T(8,128)}, f32[13,16,256]{2,1,0:T(8,128)S(1)}, u32[]{:S(2)}, u32[]{:S(2)}) collective-permute-start(f32[13,16,256]{2,1,0:T(8,128)} %get-tuple-element.29), channel_id=1, source_target_pairs={{1,2},{3,4},{5,6},{7,8},{9,10},{11,12},{13,14},{2,1},{4,3},{6,5},{... | collective-permute-start | bytes 638984 | tf_op jit(solution)/shard_map/ppermute | solution.py:29
  3.0 9.5 %collective-permute-start.1 = (f32[13,16,256]{2,1,0:T(8,128)}, f32[13,16,256]{2,1,0:T(8,128)S(1)}, u32[]{:S(2)}, u32[]{:S(2)}) collective-permute-start(f32[13,16,256]{2,1,0:T(8,128)} %get-tuple-element.30), channel_id=1, source_target_pairs={{0,1},{2,3},{4,5},{6,7},{8,9},{10,11},{12,13},{14,15},{1,0},{3,2},... | collective-permute-start | bytes 638984 | tf_op jit(solution)/shard_map/ppermute | solution.py:29
  7.3 1.9 %copy-start = (f32[2,6,16,4096]{3,2,1,0:T(8,128)S(1)}, f32[2,6,16,4096]{3,2,1,0:T(8,128)}, u32[]{:S(2)}) copy-start(f32[2,6,16,4096]{3,2,1,0:T(8,128)} %state.6) | copy-start | bytes 9437188
  9.2 3.3 %copy-start.2 = (f32[2,6,16,4096]{3,2,1,0:T(8,128)S(1)}, f32[2,6,16,4096]{3,2,1,0:T(8,128)}, u32[]{:S(2)}) copy-start(f32[2,6,16,4096]{3,2,1,0:T(8,128)} %state.7) | copy-start | bytes 9437188
  10.6 4.6 %copy-start.10 = (f32[12,16,256]{2,1,0:T(8,128)S(1)}, f32[12,16,256]{2,1,0:T(8,128)}, u32[]{:S(2)}) copy-start(f32[12,16,256]{2,1,0:T(8,128)} %get-tuple-element.38) | copy-start | bytes 589828
  10.6 5.3 %copy-start.9 = (f32[12,16,256]{2,1,0:T(8,128)S(1)}, f32[12,16,256]{2,1,0:T(8,128)}, u32[]{:S(2)}) copy-start(f32[12,16,256]{2,1,0:T(8,128)} %get-tuple-element.39) | copy-start | bytes 589828
  13.0 11.6 %copy-start.1 = (f32[2,6,16,4096]{3,2,1,0:T(8,128)S(1)}, f32[2,6,16,4096]{3,2,1,0:T(8,128)}, u32[]{:S(2)}) copy-start(f32[2,6,16,4096]{3,2,1,0:T(8,128)} %state.6) | copy-start | bytes 9437188
  13.0 15.4 %collective-permute-start.2 = (f32[1872,128]{1,0:T(8,128)S(1)}, f32[1872,128]{1,0:T(8,128)S(1)}, u32[]{:S(2)}, u32[]{:S(2)}) collective-permute-start(f32[1872,128]{1,0:T(8,128)S(1)} %get-tuple-element.37), channel_id=1, source_target_pairs={{16,32},{48,64},{80,96},{32,16},{64,48},{96,80},{17,33},{49,65},{8... | collective-permute-start | bytes 2875400 | tf_op jit(solution)/shard_map/ppermute | solution.py:29
  15.2 7.7 %collective-permute-start.3 = (f32[12,16,256]{2,1,0:T(8,128)S(1)}, f32[12,16,256]{2,1,0:T(8,128)S(1)}, u32[]{:S(2)}, u32[]{:S(2)}) collective-permute-start(f32[12,16,256]{2,1,0:T(8,128)S(1)} %copy-done.10), channel_id=1, source_target_pairs={{1,2},{3,4},{5,6},{7,8},{9,10},{11,12},{13,14},{2,1},{4,3},{6,5},{... | collective-permute-start | bytes 589832 | tf_op jit(solution)/shard_map/ppermute | solution.py:29
  15.9 8.7 %collective-permute-start.4 = (f32[12,16,256]{2,1,0:T(8,128)S(1)}, f32[12,16,256]{2,1,0:T(8,128)S(1)}, u32[]{:S(2)}, u32[]{:S(2)}) collective-permute-start(f32[12,16,256]{2,1,0:T(8,128)S(1)} %copy-done.9), channel_id=1, source_target_pairs={{0,1},{2,3},{4,5},{6,7},{8,9},{10,11},{12,13},{14,15},{1,0},{3,2},... | collective-permute-start | bytes 589832 | tf_op jit(solution)/shard_map/ppermute | solution.py:29
  19.9 10.6 %collective-permute-start.5 = (f32[1872,128]{1,0:T(8,128)S(1)}, f32[1872,128]{1,0:T(8,128)S(1)}, u32[]{:S(2)}, u32[]{:S(2)}) collective-permute-start(f32[1872,128]{1,0:T(8,128)S(1)} %get-tuple-element.48), channel_id=1, source_target_pairs={{0,16},{32,48},{64,80},{96,112},{16,0},{48,32},{80,64},{112,96},{1... | collective-permute-start | bytes 2875400 | tf_op jit(solution)/shard_map/ppermute | solution.py:29
  22.9 7.6 %copy-start.6 = (s32[2,3]{1,0:T(2,128)S(1)}, s32[2,3]{1,0:T(2,128)}, u32[]{:S(2)}) copy-start(s32[2,3]{1,0:T(2,128)} %cells.1) | copy-start | bytes 76
  22.9 7.6 %copy-start.7 = (f32[2,4]{1,0:T(2,128)S(1)}, f32[2,4]{1,0:T(2,128)}, u32[]{:S(2)}) copy-start(f32[2,4]{1,0:T(2,128)} %wave.1) | copy-start | bytes 100
  25.1 16.6 %collective-permute-start.7 = (f32[1728,128]{1,0:T(8,128)S(1)}, f32[1728,128]{1,0:T(8,128)S(1)}, u32[]{:S(2)}, u32[]{:S(2)}) collective-permute-start(f32[1728,128]{1,0:T(8,128)S(1)} %get-tuple-element.52), channel_id=1, source_target_pairs={{0,16},{32,48},{64,80},{96,112},{16,0},{48,32},{80,64},{112,96},{1... | collective-permute-start | bytes 2654216 | tf_op jit(solution)/shard_map/ppermute | solution.py:29
  28.4 14.5 %copy-start.4 = (s32[4,16]{1,0:T(4,128)S(1)}, s32[4,16]{1,0:T(4,128)}, u32[]{:S(2)}) copy-start(s32[4,16]{1,0:T(4,128)} %owners.1) | copy-start | bytes 772
  28.4 14.5 %copy-start.5 = (s32[4,16]{1,0:T(4,128)S(1)}, s32[4,16]{1,0:T(4,128)}, u32[]{:S(2)}) copy-start(s32[4,16]{1,0:T(4,128)} %slots.1) | copy-start | bytes 772
  28.4 14.5 %collective-permute-start.6 = (f32[1728,128]{1,0:T(8,128)S(1)}, f32[1728,128]{1,0:T(8,128)S(1)}, u32[]{:S(2)}, u32[]{:S(2)}) collective-permute-start(f32[1728,128]{1,0:T(8,128)S(1)} %get-tuple-element.51), channel_id=1, source_target_pairs={{16,32},{48,64},{80,96},{32,16},{64,48},{96,80},{17,33},{49,65},{8... | collective-permute-start | bytes 2654216 | tf_op jit(solution)/shard_map/ppermute | solution.py:29
  42.9 40.4 %copy-start.8 = (s32[1,64]{1,0:T(1,128)S(1)}, s32[1,64]{1,0:T(1,128)}, u32[]{:S(2)}) copy-start(s32[1,64]{1,0:T(1,128)} %rows.1) | copy-start | bytes 772

commit v9 on v8

--- a/solution.py
+++ b/solution.py
@@ -18,15 +18,19 @@
 ROWS = TR * XR
 LBY = CY // 4
 LB = LBY * CX // 4
-UNROLL = 8
+UNROLL = 16
 W = 128
 COURANT = 0.55
 F32 = jnp.float32
 
 
-def swapped(shard, axis, first):
-    pairs = [(i, i + 1) for i in range(first, lax.axis_size(axis) - 1, 2)]
-    return lax.ppermute(shard, axis, pairs + [(j, i) for i, j in pairs])
+def swapped(far, near, axis):
+    count = lax.axis_size(axis)
+    out = []
+    for shard, first in ((near, 0), (far, 1)):
+        pairs = [(i, i + 1) for i in range(first, count - 1, 2)]
+        out.append(lax.ppermute(shard, axis, pairs + [(j, i) for i, j in pairs]))
+    return out[0], out[1]
 
 
 def lanes(tile):
@@ -180,64 +184,80 @@
     def down_z(v):
         return jnp.where(z_first, 0.0, pltpu.roll(v, 1, 1))
 
-    def magnetic(r):
-        in_low = jnp.where((r < HALO) & at_y0, 0.0, 1.0).astype(F32)
-        in_high = jnp.where((r >= HALO + HY) & at_y1, 0.0, 1.0).astype(F32)
-        inside = jnp.where(low, in_low, in_high)
+    def magnetic(first, count, edge):
         for t in range(3):
-            b = pl.multiple_of(r * XR + 8 * t, 8)
-            c = coef_x[t] * inside
             for s in range(2):
                 k = 3 * s
-                ex = fe[k, pl.ds(b, 8), :]
-                ey = fe[k + 1, pl.ds(b, 8), :]
-                ez = fe[k + 2, pl.ds(b, 8), :]
-                ex_y = fe[k, pl.ds(b + XR, 8), :]
-                ez_y = fe[k + 2, pl.ds(b + XR, 8), :]
-                ey_x = fe[k + 1, pl.ds(b + 1, 8), :]
-                ez_x = fe[k + 2, pl.ds(b + 1, 8), :]
-                hx = fh[k, pl.ds(b, 8), :] - c * ((ez_y - ez) - (up_z(ey) - ey))
-                hy = fh[k + 1, pl.ds(b, 8), :] - c * ((up_z(ex) - ex) - (ez_x - ez))
-                hz = fh[k + 2, pl.ds(b, 8), :] - c * ((ey_x - ey) - (ex_y - ex))
-                fh[k, pl.ds(b, 8), :] = hx
-                fh[k + 1, pl.ds(b, 8), :] = hy
-                fh[k + 2, pl.ds(b, 8), :] = hz
-
-    def electric(r, use):
+                b = aligned(first * XR + 8 * t, 8)
+                ex, ez = fe[k, pl.ds(b, 8), :], fe[k + 2, pl.ds(b, 8), :]
+                for i in range(count):
+                    b = aligned((first + i) * XR + 8 * t, 8)
+                    c = coef_x[t]
+                    if edge:
+                        r = first + i
+                        out = (low & at_y0) if r < HALO else (~low & at_y1)
+                        c = jnp.where(out, 0.0, c)
+                    ex_y, ez_y = fe[k, pl.ds(b + XR, 8), :], fe[k + 2, pl.ds(b + XR, 8), :]
+                    ey = fe[k + 1, pl.ds(b, 8), :]
+                    ey_x = fe[k + 1, pl.ds(b + 1, 8), :]
+                    ez_x = fe[k + 2, pl.ds(b + 1, 8), :]
+                    hx = fh[k, pl.ds(b, 8), :] - c * ((ez_y - ez) - (up_z(ey) - ey))
+                    hy = fh[k + 1, pl.ds(b, 8), :] - c * ((up_z(ex) - ex) - (ez_x - ez))
+                    hz = fh[k + 2, pl.ds(b, 8), :] - c * ((ey_x - ey) - (ex_y - ex))
+                    fh[k, pl.ds(b, 8), :] = hx
+                    fh[k + 1, pl.ds(b, 8), :] = hy
+                    fh[k + 2, pl.ds(b, 8), :] = hz
+                    ex, ez = ex_y, ez_y
+
+    def electric(first, count, use):
         for t in range(3):
-            b = pl.multiple_of(r * XR + 8 * t, 8)
-            f = factor[pl.ds(b, 8), :]
-            olds, news = [], []
             for s in range(2):
                 k = 3 * s
-                hx = fh[k, pl.ds(b, 8), :]
-                hy = fh[k + 1, pl.ds(b, 8), :]
-                hz = fh[k + 2, pl.ds(b, 8), :]
-                hx_y = fh[k, pl.ds(b - XR, 8), :]
-                hz_y = fh[k + 2, pl.ds(b - XR, 8), :]
-                hy_x = fh[k + 1, pl.ds(b - 1, 8), :]
-                hz_x = fh[k + 2, pl.ds(b - 1, 8), :]
-                ex, ey, ez = (fe[k + c, pl.ds(b, 8), :] for c in range(3))
-                nx = ex + f * ((hz - hz_y) - (hy - down_z(hy)))
-                ny = ey + f * ((hx - down_z(hx)) - (hz - hz_x))
-                nz = ez + f * ((hy - hy_x) - (hx - hx_y))
-                fe[k, pl.ds(b, 8), :] = nx
-                fe[k + 1, pl.ds(b, 8), :] = ny
-                fe[k + 2, pl.ds(b, 8), :] = nz
-                olds += [ex, ey, ez]
-                news += [nx, ny, nz]
-            use(b, olds, news)
-
-    def over(first, last, one):
-        def body(r, _):
-            one(r)
+                b = aligned((first - 1) * XR + 8 * t, 8)
+                hx_y, hz_y = fh[k, pl.ds(b, 8), :], fh[k + 2, pl.ds(b, 8), :]
+                for i in range(count):
+                    b = aligned((first + i) * XR + 8 * t, 8)
+                    f = factor[pl.ds(b, 8), :]
+                    hx, hy, hz = (fh[k + c, pl.ds(b, 8), :] for c in range(3))
+                    hy_x = fh[k + 1, pl.ds(b - 1, 8), :]
+                    hz_x = fh[k + 2, pl.ds(b - 1, 8), :]
+                    ex, ey, ez = (fe[k + c, pl.ds(b, 8), :] for c in range(3))
+                    nx = ex + f * ((hz - hz_y) - (hy - down_z(hy)))
+                    ny = ey + f * ((hx - down_z(hx)) - (hz - hz_x))
+                    nz = ez + f * ((hy - hy_x) - (hx - hx_y))
+                    fe[k, pl.ds(b, 8), :] = nx
+                    fe[k + 1, pl.ds(b, 8), :] = ny
+                    fe[k + 2, pl.ds(b, 8), :] = nz
+                    if use is not None:
+                        use(s, b, (ex, ey, ez), (nx, ny, nz))
+                    hx_y, hz_y = hx, hz
+
+    def over(first, last, edge, inner):
+        own = HALO + HY
+        if first < HALO:
+            edge(first, HALO - first)
+
+        def body(i, _):
+            inner(HALO + i * UNROLL, UNROLL)
             return 0
 
-        lax.fori_loop(first, last, body, 0, unroll=UNROLL)
+        lax.fori_loop(0, HY // UNROLL, body, 0)
+        if last > own:
+            edge(own, last - own)
 
     def step(n, use):
-        over(n, TR - 1 - n, magnetic)
-        over(n + 1, TR - 1 - n, lambda r: electric(r, use))
+        over(
+            n,
+            TR - 1 - n,
+            lambda r, m: magnetic(r, m, True),
+            lambda r, m: magnetic(r, m, False),
+        )
+        over(
+            n + 1,
+            TR - 1 - n,
+            lambda r, m: electric(r, m, None),
+            lambda r, m: electric(r, m, use),
+        )
 
     return step
 
@@ -282,9 +302,9 @@
     lane = lax.broadcasted_iota(jnp.int32, (1, W), 1)
     for n in range(STEPS):
 
-        def use(b, olds, news):
-            for i in range(6):
-                inc[n, i, pl.ds(b, 8), :] = news[i] - olds[i]
+        def use(s, b, olds, news):
+            for c in range(3):
+                inc[n, 3 * s + c, pl.ds(b, 8), :] = news[c] - olds[c]
 
         step(n, use)
         for s in range(2):
@@ -338,12 +358,14 @@
     step = half_steps(fe, fh, factor)
     for n in range(STEPS):
 
-        def use(b, olds, news):
-            terms = [news[i] * inc[STEPS - 1 - n, i, pl.ds(b, 8), :] for i in range(6)]
-            total = ((terms[0] + terms[1]) + terms[2]) + ((terms[3] + terms[4]) + terms[5])
+        def use(s, b, olds, news):
+            x, y, z = (
+                news[c] * inc[STEPS - 1 - n, 3 * s + c, pl.ds(b, 8), :] for c in range(3)
+            )
+            total = (x + y) + z
             if n > 0:
-                total = total + density[pl.ds(b, 8), :]
-            density[pl.ds(b, 8), :] = total
+                total = total + density[s, pl.ds(b, 8), :]
+            density[s, pl.ds(b, 8), :] = total
 
         step(n, use)
 
@@ -352,7 +374,8 @@
             g = []
             for r in (2 * j + HALO, 2 * j + HALO + 1):
                 at = pl.ds(r * XR + HALO + 8 * t, 8)
-                g.append(density[at, :] * (factor[at, :] * (-1.0 / COURANT)))
+                both = density[0, at, :] + density[1, at, :]
+                g.append(both * (factor[at, :] * (-1.0 / COURANT)))
             for tile, v in (
                 (j, jnp.where(low, g[0], pltpu.roll(g[1], NZ, 1))),
                 (j + TJ // 2, jnp.where(low, pltpu.roll(g[0], NZ, 1), g[1])),
@@ -446,7 +469,7 @@
         2,
         8,
         [buf(*SENT)],
-        [FIELD, FIELD, *ghosts, (ROWS, W), (LB * 8, W), (33, 16, W)],
+        [FIELD, FIELD, *ghosts, (2, ROWS, W), (LB * 8, W), (33, 16, W)],
         12,
         15,
     )
@@ -463,18 +486,17 @@
     owner_rows,
 ):
     rows_y = call_pack_y()(forward_state, adjoint_state, permittivity)
-    fy_far, fy_near = (swapped(rows_y[i], "gy", 1 - i) for i in range(2))
-    ay_far, ay_near = (swapped(rows_y[2 + i], "gy", 1 - i) for i in range(2))
+    fy_near, fy_far = swapped(*rows_y[:2], "gy")
+    ay_near, ay_far = swapped(*rows_y[2:], "gy")
     own = [buf(6, TR * CX, W)] * 2
+    forward_own = call(convert, 0, 2, [*own, buf(TR * CX, W)])(forward_state, permittivity)
+    fy_near, fy_far, forward_own = lax.optimization_barrier((fy_near, fy_far, forward_own))
+    fx_near, fx_far = swapped(
+        *call_pack_x(13)(forward_state, permittivity, fy_far, fy_near), "gx"
+    )
+    ax_near, ax_far = swapped(*call_pack_x(12)(adjoint_state, ay_far, ay_near), "gx")
     adjoint_own = call(convert, 0, 1, own)(adjoint_state)
-    fy_far, fy_near, adjoint_own = lax.optimization_barrier((fy_far, fy_near, adjoint_own))
-    fx = call_pack_x(13)(forward_state, permittivity, fy_far, fy_near)
-    fx_far, fx_near = (swapped(fx[i], "gx", 1 - i) for i in range(2))
-    ax = call_pack_x(12)(adjoint_state, ay_far, ay_near)
-    ax_near = swapped(ax[1], "gx", 0)
-    forward_own = call(convert, 0, 2, [*own, buf(TR * CX, W)])(forward_state, permittivity)
-    fx_far, ax_far, forward_own = lax.optimization_barrier((fx_far, ax[0], forward_own))
-    ax_far = swapped(ax_far, "gx", 1)
+    fx_near, fx_far, adjoint_own = lax.optimization_barrier((fx_near, fx_far, adjoint_own))
     inc, factor = call_forward()(
         source_cell, waveform, *forward_own, fx_far, fx_near, fy_far, fy_near
     )

time: 84.9 us -> 80.6 us (0.949)
  Pallas kernels: 31 us -> 26.6 us
  starting transfers between devices: 16.6 us -> 14.4 us
  blocking collectives: 28.2 us -> 29.9 us
    pallas_call x1, Pallas kernels: 12.2 us -> 9.71 us  [per_device(): call_adjoint()]
    ppermute x8, starting transfers between devices: 16.6 us -> 14.4 us  [swapped(): out.append(lax.ppermute(shard, axis, pairs + [(j, i) for i, j in pairs]))]
    pallas_call x1, Pallas kernels: 11.2 us -> 9.3 us  [per_device(): call_forward()]
    all_to_all x1, blocking collectives: 28.2 us -> 29.9 us  [per_device(): arrived = lax.all_to_all(outgoing, ('src', 'gy'), 0, 0, tiled=True)]
    unnamed x22 -> x16, local copies, waits for them, and re-layouts: 1.93 us -> 1.93 us
  transfers between devices with their start and end apart: 8 -> 8, of which waited for: 4 -> 2; matrix products, arithmetic and copies ran while one was open for 0% -> 0% of each run, Pallas kernels for 17% -> 17%
where the time goes in v9:
time: 80.6 us; the launch traced here: 80.3 us
  blocking collectives  29.9 us (37%)
  Pallas kernels  26.6 us (33%)
  starting transfers between devices  14.4 us (18%)
  waiting for transfers between devices  7.3 us (9%)
  local copies, waits for them, and re-layouts  1.93 us (2%)
    all_to_all x1, blocking collectives, per_device(): arrived = lax.all_to_all(outgoing, ('src', 'gy'), 0, 0, tiled=True)  29.9 us
    ppermute x8, starting transfers between devices, swapped(): out.append(lax.ppermute(shard, axis, pairs + [(j, i) for i, j in pairs]))  14.4 us
    pallas_call x1, Pallas kernels, per_device(): call_adjoint()  9.71 us
    pallas_call x1, Pallas kernels, per_device(): call_forward()  9.3 us
    ppermute x8, waiting for transfers between devices, swapped(): out.append(lax.ppermute(shard, axis, pairs + [(j, i) for i, j in pairs]))  7.3 us
    pallas_call x1, Pallas kernels, per_device(): rows_y = call_pack_y()(forward_state, adjoint_state, permittivity)  2.25 us
    unnamed x16, local copies, waits for them, and re-layouts  1.93 us
  transfers between devices with their start and end apart: 8, of which 2 were waited for; matrix products, arithmetic and copies ran while one was open for 0% of the time, Pallas kernels for 17%

profile of v9, /device:TPU:32, one launch (start us, length us, event | category | flops | bytes accessed | tf_op | source)
XLA Modules:
  0.0 80.3 jit_solution(5667218812960524531)
XLA Ops:
  0.0 0.0 copy-start.2
  0.0 2.2 %pack_y.1 = (f32[13,16,256]{2,1,0:T(8,128)}, f32[13,16,256]{2,1,0:T(8,128)}, f32[12,16,256]{2,1,0:T(8,128)}, f32[12,16,256]{2,1,0:T(8,128)}) custom-call(f32[2,6,16,4096]{3,2,1,0:T(8,128)} %state.5, f32[2,6,16,4096]{3,2,1,0:T(8,128)} %state.7, f32[16,4096]{1,0:T(8,128)} %rest_0_.3), custom_call_target="tpu_custom_call" | custom-call | tf_op jit(solution)/shard_map/pack_y/pallas_call | solution.py:488
  2.3 1.6 %collective-permute-start = (f32[13,16,256]{2,1,0:T(8,128)}, f32[13,16,256]{2,1,0:T(8,128)S(1)}, u32[]{:S(2)}, u32[]{:S(2)}) collective-permute-start(f32[13,16,256]{2,1,0:T(8,128)} %get-tuple-element.29), channel_id=1, source_target_pairs={{0,1},{2,3},{4,5},{6,7},{8,9},{10,11},{12,13},{14,15},{1,0},{3,2},... | collective-permute-start | bytes 638984 | tf_op jit(solution)/shard_map/ppermute | solution.py:32
  3.8 0.7 collective-permute-start.1
  4.5 0.7 collective-permute-start.4
  5.2 5.3 %collective-permute-start.5 = (f32[12,16,256]{2,1,0:T(8,128)}, f32[12,16,256]{2,1,0:T(8,128)S(1)}, u32[]{:S(2)}, u32[]{:S(2)}) collective-permute-start(f32[12,16,256]{2,1,0:T(8,128)} %get-tuple-element.50), channel_id=1, source_target_pairs={{0,1},{2,3},{4,5},{6,7},{8,9},{10,11},{12,13},{14,15},{1,0},{3,2},... | collective-permute-start | bytes 589832 | tf_op jit(solution)/shard_map/ppermute | solution.py:32
  10.4 0.0 copy-done.2
  10.4 0.0 copy-start.1
  10.4 1.9 %copy-done.1 = f32[2,6,16,4096]{3,2,1,0:T(8,128)S(1)} copy-done((f32[2,6,16,4096]{3,2,1,0:T(8,128)S(1)}, f32[2,6,16,4096]{3,2,1,0:T(8,128)}, u32[]{:S(2)}) %copy-start.1) | copy-done | bytes 3145752
  12.3 1.5 %convert.2 = (f32[6,640,128]{2,1,0:T(8,128)S(1)}, f32[6,640,128]{2,1,0:T(8,128)S(1)}, f32[640,128]{1,0:T(8,128)S(1)}) custom-call(f32[2,6,16,4096]{3,2,1,0:T(8,128)S(1)} %copy-done.1, f32[16,4096]{1,0:T(8,128)S(1)} %copy-done.2), custom_call_target="tpu_custom_call" | custom-call | flops 2000000 | bytes 6000000 | tf_op jit(solution)/shard_map/convert/pallas_call | solution.py:492
  13.9 0.0 copy-start
  13.9 0.0 collective-permute-done.rest_2_.y_near
  13.9 0.0 collective-permute-done.1.rest_1_.y_far
  13.9 0.6 pack_x.2
  14.5 0.1 collective-permute-start.2
  14.6 3.7 %collective-permute-start.3 = (f32[1872,128]{1,0:T(8,128)S(1)}, f32[1872,128]{1,0:T(8,128)S(1)}, u32[]{:S(2)}, u32[]{:S(2)}) collective-permute-start(f32[1872,128]{1,0:T(8,128)S(1)} %get-tuple-element.37), channel_id=1, source_target_pairs={{16,32},{48,64},{80,96},{32,16},{64,48},{96,80},{17,33},{49,65},{8... | collective-permute-start | bytes 2875400 | tf_op jit(solution)/shard_map/ppermute | solution.py:32
  18.3 0.0 collective-permute-done.4.rest_0_.y_far
  18.3 0.0 collective-permute-done.5.rest_1_.y_near
  18.3 0.0 copy-done
  18.3 0.5 pack_x.3
  18.8 0.0 copy-start.5
  18.8 0.0 copy-start.6
  18.9 2.0 %collective-permute-start.6 = (f32[1728,128]{1,0:T(8,128)S(1)}, f32[1728,128]{1,0:T(8,128)S(1)}, u32[]{:S(2)}, u32[]{:S(2)}) collective-permute-start(f32[1728,128]{1,0:T(8,128)S(1)} %get-tuple-element.51), channel_id=1, source_target_pairs={{16,32},{48,64},{80,96},{32,16},{64,48},{96,80},{17,33},{49,65},{8... | collective-permute-start | bytes 2654216 | tf_op jit(solution)/shard_map/ppermute | solution.py:32
  20.9 0.4 collective-permute-start.7
  21.3 1.4 %convert.3 = (f32[6,640,128]{2,1,0:T(8,128)S(1)}, f32[6,640,128]{2,1,0:T(8,128)S(1)}) custom-call(f32[2,6,16,4096]{3,2,1,0:T(8,128)S(1)} %copy-done), custom_call_target="tpu_custom_call" | custom-call | flops 2000000 | bytes 6000000 | tf_op jit(solution)/shard_map/convert/pallas_call | solution.py:498
  22.7 0.0 collective-permute-done.2.x_near
  22.7 7.1 %collective-permute-done.3.x_far = f32[1872,128]{1,0:T(8,128)S(1)} collective-permute-done((f32[1872,128]{1,0:T(8,128)S(1)}, f32[1872,128]{1,0:T(8,128)S(1)}, u32[]{:S(2)}, u32[]{:S(2)}) %collective-permute-start.3) | collective-permute-done | bytes 958496 | tf_op jit(solution)/shard_map/ppermute | solution.py:32
  29.9 0.0 copy-done.5
  29.9 0.0 copy-done.6
  29.9 0.0 copy-start.3
  29.9 0.0 copy-start.4
  29.9 9.3 %forward.1 = (f32[4,6,960,128]{3,2,1,0:T(8,128)S(1)}, f32[960,128]{1,0:T(8,128)S(1)}) custom-call(s32[2,3]{1,0:T(2,128)S(1)} %copy-done.5, f32[2,4]{1,0:T(2,128)S(1)} %copy-done.6, f32[6,640,128]{2,1,0:T(8,128)S(1)} %get-tuple-element.42.own_e, f32[6,640,128]{2,1,0:T(8,128)S(1)} %get-tuple-element.43.own_h, f32[640,128]{1,0:T(8,128)S(1)} %get-tuple-element.44.own_f, ...), custom_call_target="tpu_custom_call" | custom-call | flops 15000000 | bytes 45000000 | tf_op jit(solution)/shard_map/forward/pallas_call | solution.py:500
  39.2 0.2 collective-permute-done.6.x_far
  39.3 0.0 collective-permute-done.7.x_near
  39.3 0.0 copy-done.3
  39.3 0.0 copy-done.4
  39.3 0.0 copy-start.7
  39.4 9.7 %adjoint.1 = f32[32,16,128]{2,1,0:T(8,128)S(1)} custom-call(s32[4,16]{1,0:T(4,128)S(1)} %copy-done.3, s32[4,16]{1,0:T(4,128)S(1)} %copy-done.4, f32[6,640,128]{2,1,0:T(8,128)S(1)} %get-tuple-element.40.own_e, f32[6,640,128]{2,1,0:T(8,128)S(1)} %get-tuple-element.41.own_h, f32[960,128]{1,0:T(8,128)S(1)} %get-tuple-element.47.factor, ...), custom_call_target="tpu_custom_call" | custom-call | flops 15000000 | bytes 45000000 | tf_op jit(solution)/shard_map/adjoint/pallas_call | solution.py:503
  49.1 29.9 %all_to_all.5.arrived = f32[32,16,128]{2,1,0:T(8,128)S(1)} all-to-all(f32[32,16,128]{2,1,0:T(8,128)S(1)} %adjoint.1), channel_id=1, replica_groups=mesh['src'=2,'gx'=8,'gy'=16] {'src','gy'}, dimensions={0} | all-to-all | bytes 524288 | tf_op jit(solution)/shard_map/all_to_all | solution.py:514
  78.9 0.0 copy-done.7
  78.9 1.3 %place.1 = f32[64,512]{1,0:T(8,128)} custom-call(s32[1,64]{1,0:T(1,128)S(1)} %copy-done.7, f32[32,16,128]{2,1,0:T(8,128)S(1)} %all_to_all.5.arrived), custom_call_target="tpu_custom_call" | custom-call | flops 2000000 | bytes 6000000 | tf_op jit(solution)/shard_map/place/pallas_call | solution.py:515
Async XLA Ops:
  0.0 10.4 %copy-start.2 = (f32[16,4096]{1,0:T(8,128)S(1)}, f32[16,4096]{1,0:T(8,128)}, u32[]{:S(2)}) copy-start(f32[16,4096]{1,0:T(8,128)} %rest_0_.3) | copy-start | bytes 786436
  2.3 11.6 %collective-permute-start = (f32[13,16,256]{2,1,0:T(8,128)}, f32[13,16,256]{2,1,0:T(8,128)S(1)}, u32[]{:S(2)}, u32[]{:S(2)}) collective-permute-start(f32[13,16,256]{2,1,0:T(8,128)} %get-tuple-element.29), channel_id=1, source_target_pairs={{0,1},{2,3},{4,5},{6,7},{8,9},{10,11},{12,13},{14,15},{1,0},{3,2},... | collective-permute-start | bytes 638984 | tf_op jit(solution)/shard_map/ppermute | solution.py:32
  3.8 10.1 %collective-permute-start.1 = (f32[13,16,256]{2,1,0:T(8,128)}, f32[13,16,256]{2,1,0:T(8,128)S(1)}, u32[]{:S(2)}, u32[]{:S(2)}) collective-permute-start(f32[13,16,256]{2,1,0:T(8,128)} %get-tuple-element.30), channel_id=1, source_target_pairs={{1,2},{3,4},{5,6},{7,8},{9,10},{11,12},{13,14},{2,1},{4,3},{6,5},{... | collective-permute-start | bytes 638984 | tf_op jit(solution)/shard_map/ppermute | solution.py:32
  4.5 13.8 %collective-permute-start.4 = (f32[12,16,256]{2,1,0:T(8,128)}, f32[12,16,256]{2,1,0:T(8,128)S(1)}, u32[]{:S(2)}, u32[]{:S(2)}) collective-permute-start(f32[12,16,256]{2,1,0:T(8,128)} %get-tuple-element.49), channel_id=1, source_target_pairs={{1,2},{3,4},{5,6},{7,8},{9,10},{11,12},{13,14},{2,1},{4,3},{6,5},{... | collective-permute-start | bytes 589832 | tf_op jit(solution)/shard_map/ppermute | solution.py:32
  5.2 13.1 %collective-permute-start.5 = (f32[12,16,256]{2,1,0:T(8,128)}, f32[12,16,256]{2,1,0:T(8,128)S(1)}, u32[]{:S(2)}, u32[]{:S(2)}) collective-permute-start(f32[12,16,256]{2,1,0:T(8,128)} %get-tuple-element.50), channel_id=1, source_target_pairs={{0,1},{2,3},{4,5},{6,7},{8,9},{10,11},{12,13},{14,15},{1,0},{3,2},... | collective-permute-start | bytes 589832 | tf_op jit(solution)/shard_map/ppermute | solution.py:32
  10.4 1.9 %copy-start.1 = (f32[2,6,16,4096]{3,2,1,0:T(8,128)S(1)}, f32[2,6,16,4096]{3,2,1,0:T(8,128)}, u32[]{:S(2)}) copy-start(f32[2,6,16,4096]{3,2,1,0:T(8,128)} %state.5) | copy-start | bytes 9437188
  13.9 4.4 %copy-start = (f32[2,6,16,4096]{3,2,1,0:T(8,128)S(1)}, f32[2,6,16,4096]{3,2,1,0:T(8,128)}, u32[]{:S(2)}) copy-start(f32[2,6,16,4096]{3,2,1,0:T(8,128)} %state.7) | copy-start | bytes 9437188
  14.5 8.2 %collective-permute-start.2 = (f32[1872,128]{1,0:T(8,128)S(1)}, f32[1872,128]{1,0:T(8,128)S(1)}, u32[]{:S(2)}, u32[]{:S(2)}) collective-permute-start(f32[1872,128]{1,0:T(8,128)S(1)} %get-tuple-element.36), channel_id=1, source_target_pairs={{0,16},{32,48},{64,80},{96,112},{16,0},{48,32},{80,64},{112,96},{1... | collective-permute-start | bytes 2875400 | tf_op jit(solution)/shard_map/ppermute | solution.py:32
  14.6 15.3 %collective-permute-start.3 = (f32[1872,128]{1,0:T(8,128)S(1)}, f32[1872,128]{1,0:T(8,128)S(1)}, u32[]{:S(2)}, u32[]{:S(2)}) collective-permute-start(f32[1872,128]{1,0:T(8,128)S(1)} %get-tuple-element.37), channel_id=1, source_target_pairs={{16,32},{48,64},{80,96},{32,16},{64,48},{96,80},{17,33},{49,65},{8... | collective-permute-start | bytes 2875400 | tf_op jit(solution)/shard_map/ppermute | solution.py:32
  18.8 11.0 %copy-start.5 = (s32[2,3]{1,0:T(2,128)S(1)}, s32[2,3]{1,0:T(2,128)}, u32[]{:S(2)}) copy-start(s32[2,3]{1,0:T(2,128)} %cells.1) | copy-start | bytes 76
  18.8 11.0 %copy-start.6 = (f32[2,4]{1,0:T(2,128)S(1)}, f32[2,4]{1,0:T(2,128)}, u32[]{:S(2)}) copy-start(f32[2,4]{1,0:T(2,128)} %wave.1) | copy-start | bytes 100
  18.9 20.5 %collective-permute-start.6 = (f32[1728,128]{1,0:T(8,128)S(1)}, f32[1728,128]{1,0:T(8,128)S(1)}, u32[]{:S(2)}, u32[]{:S(2)}) collective-permute-start(f32[1728,128]{1,0:T(8,128)S(1)} %get-tuple-element.51), channel_id=1, source_target_pairs={{16,32},{48,64},{80,96},{32,16},{64,48},{96,80},{17,33},{49,65},{8... | collective-permute-start | bytes 2654216 | tf_op jit(solution)/shard_map/ppermute | solution.py:32
  20.9 18.5 %collective-permute-start.7 = (f32[1728,128]{1,0:T(8,128)S(1)}, f32[1728,128]{1,0:T(8,128)S(1)}, u32[]{:S(2)}, u32[]{:S(2)}) collective-permute-start(f32[1728,128]{1,0:T(8,128)S(1)} %get-tuple-element.52), channel_id=1, source_target_pairs={{0,16},{32,48},{64,80},{96,112},{16,0},{48,32},{80,64},{112,96},{1... | collective-permute-start | bytes 2654216 | tf_op jit(solution)/shard_map/ppermute | solution.py:32
  29.9 9.5 %copy-start.3 = (s32[4,16]{1,0:T(4,128)S(1)}, s32[4,16]{1,0:T(4,128)}, u32[]{:S(2)}) copy-start(s32[4,16]{1,0:T(4,128)} %owners.1) | copy-start | bytes 772
  29.9 9.5 %copy-start.4 = (s32[4,16]{1,0:T(4,128)S(1)}, s32[4,16]{1,0:T(4,128)}, u32[]{:S(2)}) copy-start(s32[4,16]{1,0:T(4,128)} %slots.1) | copy-start | bytes 772
  39.3 39.6 %copy-start.7 = (s32[1,64]{1,0:T(1,128)S(1)}, s32[1,64]{1,0:T(1,128)}, u32[]{:S(2)}) copy-start(s32[1,64]{1,0:T(1,128)} %rows.1) | copy-start | bytes 772

commit v10 on v9

--- a/solution.py
+++ b/solution.py
@@ -496,10 +496,11 @@
     )
     ax_near, ax_far = swapped(*call_pack_x(12)(adjoint_state, ay_far, ay_near), "gx")
     adjoint_own = call(convert, 0, 1, own)(adjoint_state)
-    fx_near, fx_far, adjoint_own = lax.optimization_barrier((fx_near, fx_far, adjoint_own))
+    fx_far, fx_near, adjoint_own = lax.optimization_barrier((fx_far, fx_near, adjoint_own))
     inc, factor = call_forward()(
         source_cell, waveform, *forward_own, fx_far, fx_near, fy_far, fy_near
     )
+    ax_near, ax_far, inc = lax.optimization_barrier((ax_near, ax_far, inc))
     (outgoing,) = call_adjoint()(
         block_owner,
         block_slot,

time: 80.6 us -> 78.8 us (0.978)
  blocking collectives: 29.9 us -> 28 us
    all_to_all x1, blocking collectives: 29.9 us -> 28 us  [per_device(): arrived = lax.all_to_all(outgoing, ('src', 'gy'), 0, 0, tiled=True)]
where the time goes in v10:
time: 78.8 us; the launch traced here: 78.3 us
  blocking collectives  28 us (36%)
  Pallas kernels  26.6 us (34%)
  starting transfers between devices  14.5 us (18%)
  waiting for transfers between devices  7.07 us (9%)
  local copies, waits for them, and re-layouts  1.93 us (2%)
    all_to_all x1, blocking collectives, per_device(): arrived = lax.all_to_all(outgoing, ('src', 'gy'), 0, 0, tiled=True)  28 us
    ppermute x8, starting transfers between devices, swapped(): out.append(lax.ppermute(shard, axis, pairs + [(j, i) for i, j in pairs]))  14.5 us
    pallas_call x1, Pallas kernels, per_device(): call_adjoint()  9.71 us
    pallas_call x1, Pallas kernels, per_device(): call_forward()  9.3 us
    ppermute x8, waiting for transfers between devices, swapped(): out.append(lax.ppermute(shard, axis, pairs + [(j, i) for i, j in pairs]))  7.07 us
    pallas_call x1, Pallas kernels, per_device(): rows_y = call_pack_y()(forward_state, adjoint_state, permittivity)  2.25 us
    unnamed x16, local copies, waits for them, and re-layouts  1.93 us
  transfers between devices with their start and end apart: 8, of which 2 were waited for; matrix products, arithmetic and copies ran while one was open for 0% of the time, Pallas kernels for 17%

profile of v10, /device:TPU:32, one launch (start us, length us, event | category | flops | bytes accessed | tf_op | source)
XLA Modules:
  0.0 78.3 jit_solution(12702175075655719699)
XLA Ops:
  0.0 0.0 copy-start.2
  0.0 2.2 %pack_y.1 = (f32[13,16,256]{2,1,0:T(8,128)}, f32[13,16,256]{2,1,0:T(8,128)}, f32[12,16,256]{2,1,0:T(8,128)}, f32[12,16,256]{2,1,0:T(8,128)}) custom-call(f32[2,6,16,4096]{3,2,1,0:T(8,128)} %state.5, f32[2,6,16,4096]{3,2,1,0:T(8,128)} %state.7, f32[16,4096]{1,0:T(8,128)} %rest_0_.3), custom_call_target="tpu_custom_call" | custom-call | tf_op jit(solution)/shard_map/pack_y/pallas_call | solution.py:488
  2.3 1.6 %collective-permute-start = (f32[13,16,256]{2,1,0:T(8,128)}, f32[13,16,256]{2,1,0:T(8,128)S(1)}, u32[]{:S(2)}, u32[]{:S(2)}) collective-permute-start(f32[13,16,256]{2,1,0:T(8,128)} %get-tuple-element.32), channel_id=1, source_target_pairs={{0,1},{2,3},{4,5},{6,7},{8,9},{10,11},{12,13},{14,15},{1,0},{3,2},... | collective-permute-start | bytes 638984 | tf_op jit(solution)/shard_map/ppermute | solution.py:32
  3.8 0.7 collective-permute-start.1
  4.5 0.7 collective-permute-start.4
  5.2 5.3 %collective-permute-start.5 = (f32[12,16,256]{2,1,0:T(8,128)}, f32[12,16,256]{2,1,0:T(8,128)S(1)}, u32[]{:S(2)}, u32[]{:S(2)}) collective-permute-start(f32[12,16,256]{2,1,0:T(8,128)} %get-tuple-element.52), channel_id=1, source_target_pairs={{0,1},{2,3},{4,5},{6,7},{8,9},{10,11},{12,13},{14,15},{1,0},{3,2},... | collective-permute-start | bytes 589832 | tf_op jit(solution)/shard_map/ppermute | solution.py:32
  10.4 0.0 copy-done.2
  10.4 0.0 copy-start.1
  10.4 1.9 %copy-done.1 = f32[2,6,16,4096]{3,2,1,0:T(8,128)S(1)} copy-done((f32[2,6,16,4096]{3,2,1,0:T(8,128)S(1)}, f32[2,6,16,4096]{3,2,1,0:T(8,128)}, u32[]{:S(2)}) %copy-start.1) | copy-done | bytes 3145752
  12.3 1.5 %convert.2 = (f32[6,640,128]{2,1,0:T(8,128)S(1)}, f32[6,640,128]{2,1,0:T(8,128)S(1)}, f32[640,128]{1,0:T(8,128)S(1)}) custom-call(f32[2,6,16,4096]{3,2,1,0:T(8,128)S(1)} %copy-done.1, f32[16,4096]{1,0:T(8,128)S(1)} %copy-done.2), custom_call_target="tpu_custom_call" | custom-call | flops 2000000 | bytes 6000000 | tf_op jit(solution)/shard_map/convert/pallas_call | solution.py:492
  13.9 0.0 copy-start
  13.9 0.0 collective-permute-done.rest_2_.y_near
  13.9 0.0 collective-permute-done.1.rest_1_.y_far
  13.9 0.6 pack_x.2
  14.5 2.1 %collective-permute-start.2 = (f32[1872,128]{1,0:T(8,128)S(1)}, f32[1872,128]{1,0:T(8,128)S(1)}, u32[]{:S(2)}, u32[]{:S(2)}) collective-permute-start(f32[1872,128]{1,0:T(8,128)S(1)} %get-tuple-element.39), channel_id=1, source_target_pairs={{16,32},{48,64},{80,96},{32,16},{64,48},{96,80},{17,33},{49,65},{8... | collective-permute-start | bytes 2875400 | tf_op jit(solution)/shard_map/ppermute | solution.py:32
  16.5 2.1 %collective-permute-start.3 = (f32[1872,128]{1,0:T(8,128)S(1)}, f32[1872,128]{1,0:T(8,128)S(1)}, u32[]{:S(2)}, u32[]{:S(2)}) collective-permute-start(f32[1872,128]{1,0:T(8,128)S(1)} %get-tuple-element.40), channel_id=1, source_target_pairs={{0,16},{32,48},{64,80},{96,112},{16,0},{48,32},{80,64},{112,96},{1... | collective-permute-start | bytes 2875400 | tf_op jit(solution)/shard_map/ppermute | solution.py:32
  18.6 0.0 collective-permute-done.4.rest_0_.y_far
  18.6 0.0 collective-permute-done.5.rest_1_.y_near
  18.6 0.0 copy-done
  18.6 0.5 pack_x.3
  19.2 0.0 copy-start.5
  19.2 0.0 copy-start.6
  19.2 0.1 collective-permute-start.6
  19.3 2.1 %collective-permute-start.7 = (f32[1728,128]{1,0:T(8,128)S(1)}, f32[1728,128]{1,0:T(8,128)S(1)}, u32[]{:S(2)}, u32[]{:S(2)}) collective-permute-start(f32[1728,128]{1,0:T(8,128)S(1)} %get-tuple-element.54), channel_id=1, source_target_pairs={{16,32},{48,64},{80,96},{32,16},{64,48},{96,80},{17,33},{49,65},{8... | collective-permute-start | bytes 2654216 | tf_op jit(solution)/shard_map/ppermute | solution.py:32
  21.4 1.4 %convert.3 = (f32[6,640,128]{2,1,0:T(8,128)S(1)}, f32[6,640,128]{2,1,0:T(8,128)S(1)}) custom-call(f32[2,6,16,4096]{3,2,1,0:T(8,128)S(1)} %copy-done), custom_call_target="tpu_custom_call" | custom-call | flops 2000000 | bytes 6000000 | tf_op jit(solution)/shard_map/convert/pallas_call | solution.py:498
  22.8 6.9 %collective-permute-done.2.x_far = f32[1872,128]{1,0:T(8,128)S(1)} collective-permute-done((f32[1872,128]{1,0:T(8,128)S(1)}, f32[1872,128]{1,0:T(8,128)S(1)}, u32[]{:S(2)}, u32[]{:S(2)}) %collective-permute-start.2) | collective-permute-done | bytes 958496 | tf_op jit(solution)/shard_map/ppermute | solution.py:32
  29.8 0.0 collective-permute-done.3.x_near
  29.8 0.0 copy-done.5
  29.8 0.0 copy-done.6
  29.8 0.0 copy-start.3
  29.8 0.0 copy-start.4
  29.8 9.3 %forward.1 = (f32[4,6,960,128]{3,2,1,0:T(8,128)S(1)}, f32[960,128]{1,0:T(8,128)S(1)}) custom-call(s32[2,3]{1,0:T(2,128)S(1)} %copy-done.5, f32[2,4]{1,0:T(2,128)S(1)} %copy-done.6, f32[6,640,128]{2,1,0:T(8,128)S(1)} %get-tuple-element.45.own_e, f32[6,640,128]{2,1,0:T(8,128)S(1)} %get-tuple-element.46.own_h, f32[640,128]{1,0:T(8,128)S(1)} %get-tuple-element.47.own_f, ...), custom_call_target="tpu_custom_call" | custom-call | flops 15000000 | bytes 45000000 | tf_op jit(solution)/shard_map/forward/pallas_call | solution.py:500
  39.1 0.0 collective-permute-done.6.x_near
  39.1 0.1 collective-permute-done.7.x_far
  39.2 0.0 copy-done.3
  39.2 0.0 copy-done.4
  39.2 0.0 copy-start.7
  39.2 9.7 %adjoint.1 = f32[32,16,128]{2,1,0:T(8,128)S(1)} custom-call(s32[4,16]{1,0:T(4,128)S(1)} %copy-done.3, s32[4,16]{1,0:T(4,128)S(1)} %copy-done.4, f32[6,640,128]{2,1,0:T(8,128)S(1)} %get-tuple-element.43.own_e, f32[6,640,128]{2,1,0:T(8,128)S(1)} %get-tuple-element.44.own_h, f32[960,128]{1,0:T(8,128)S(1)} %get-tuple-element.50.factor, ...), custom_call_target="tpu_custom_call" | custom-call | flops 15000000 | bytes 45000000 | tf_op jit(solution)/shard_map/adjoint/pallas_call | solution.py:504
  49.0 28.0 %all_to_all.5.arrived = f32[32,16,128]{2,1,0:T(8,128)S(1)} all-to-all(f32[32,16,128]{2,1,0:T(8,128)S(1)} %adjoint.1), channel_id=1, replica_groups=mesh['src'=2,'gx'=8,'gy'=16] {'src','gy'}, dimensions={0} | all-to-all | bytes 524288 | tf_op jit(solution)/shard_map/all_to_all | solution.py:515
  76.9 0.0 copy-done.7
  76.9 1.3 %place.1 = f32[64,512]{1,0:T(8,128)} custom-call(s32[1,64]{1,0:T(1,128)S(1)} %copy-done.7, f32[32,16,128]{2,1,0:T(8,128)S(1)} %all_to_all.5.arrived), custom_call_target="tpu_custom_call" | custom-call | flops 2000000 | bytes 6000000 | tf_op jit(solution)/shard_map/place/pallas_call | solution.py:516
Async XLA Ops:
  0.0 10.4 %copy-start.2 = (f32[16,4096]{1,0:T(8,128)S(1)}, f32[16,4096]{1,0:T(8,128)}, u32[]{:S(2)}) copy-start(f32[16,4096]{1,0:T(8,128)} %rest_0_.3) | copy-start | bytes 786436
  2.3 11.6 %collective-permute-start = (f32[13,16,256]{2,1,0:T(8,128)}, f32[13,16,256]{2,1,0:T(8,128)S(1)}, u32[]{:S(2)}, u32[]{:S(2)}) collective-permute-start(f32[13,16,256]{2,1,0:T(8,128)} %get-tuple-element.32), channel_id=1, source_target_pairs={{0,1},{2,3},{4,5},{6,7},{8,9},{10,11},{12,13},{14,15},{1,0},{3,2},... | collective-permute-start | bytes 638984 | tf_op jit(solution)/shard_map/ppermute | solution.py:32
  3.8 10.1 %collective-permute-start.1 = (f32[13,16,256]{2,1,0:T(8,128)}, f32[13,16,256]{2,1,0:T(8,128)S(1)}, u32[]{:S(2)}, u32[]{:S(2)}) collective-permute-start(f32[13,16,256]{2,1,0:T(8,128)} %get-tuple-element.33), channel_id=1, source_target_pairs={{1,2},{3,4},{5,6},{7,8},{9,10},{11,12},{13,14},{2,1},{4,3},{6,5},{... | collective-permute-start | bytes 638984 | tf_op jit(solution)/shard_map/ppermute | solution.py:32
  4.5 14.1 %collective-permute-start.4 = (f32[12,16,256]{2,1,0:T(8,128)}, f32[12,16,256]{2,1,0:T(8,128)S(1)}, u32[]{:S(2)}, u32[]{:S(2)}) collective-permute-start(f32[12,16,256]{2,1,0:T(8,128)} %get-tuple-element.51), channel_id=1, source_target_pairs={{1,2},{3,4},{5,6},{7,8},{9,10},{11,12},{13,14},{2,1},{4,3},{6,5},{... | collective-permute-start | bytes 589832 | tf_op jit(solution)/shard_map/ppermute | solution.py:32
  5.2 13.5 %collective-permute-start.5 = (f32[12,16,256]{2,1,0:T(8,128)}, f32[12,16,256]{2,1,0:T(8,128)S(1)}, u32[]{:S(2)}, u32[]{:S(2)}) collective-permute-start(f32[12,16,256]{2,1,0:T(8,128)} %get-tuple-element.52), channel_id=1, source_target_pairs={{0,1},{2,3},{4,5},{6,7},{8,9},{10,11},{12,13},{14,15},{1,0},{3,2},... | collective-permute-start | bytes 589832 | tf_op jit(solution)/shard_map/ppermute | solution.py:32
  10.4 1.9 %copy-start.1 = (f32[2,6,16,4096]{3,2,1,0:T(8,128)S(1)}, f32[2,6,16,4096]{3,2,1,0:T(8,128)}, u32[]{:S(2)}) copy-start(f32[2,6,16,4096]{3,2,1,0:T(8,128)} %state.5) | copy-start | bytes 9437188
  13.9 4.8 %copy-start = (f32[2,6,16,4096]{3,2,1,0:T(8,128)S(1)}, f32[2,6,16,4096]{3,2,1,0:T(8,128)}, u32[]{:S(2)}) copy-start(f32[2,6,16,4096]{3,2,1,0:T(8,128)} %state.7) | copy-start | bytes 9437188
  14.5 15.3 %collective-permute-start.2 = (f32[1872,128]{1,0:T(8,128)S(1)}, f32[1872,128]{1,0:T(8,128)S(1)}, u32[]{:S(2)}, u32[]{:S(2)}) collective-permute-start(f32[1872,128]{1,0:T(8,128)S(1)} %get-tuple-element.39), channel_id=1, source_target_pairs={{16,32},{48,64},{80,96},{32,16},{64,48},{96,80},{17,33},{49,65},{8... | collective-permute-start | bytes 2875400 | tf_op jit(solution)/shard_map/ppermute | solution.py:32
  16.5 13.2 %collective-permute-start.3 = (f32[1872,128]{1,0:T(8,128)S(1)}, f32[1872,128]{1,0:T(8,128)S(1)}, u32[]{:S(2)}, u32[]{:S(2)}) collective-permute-start(f32[1872,128]{1,0:T(8,128)S(1)} %get-tuple-element.40), channel_id=1, source_target_pairs={{0,16},{32,48},{64,80},{96,112},{16,0},{48,32},{80,64},{112,96},{1... | collective-permute-start | bytes 2875400 | tf_op jit(solution)/shard_map/ppermute | solution.py:32
  19.2 10.6 %copy-start.5 = (s32[2,3]{1,0:T(2,128)S(1)}, s32[2,3]{1,0:T(2,128)}, u32[]{:S(2)}) copy-start(s32[2,3]{1,0:T(2,128)} %cells.1) | copy-start | bytes 76
  19.2 10.6 %copy-start.6 = (f32[2,4]{1,0:T(2,128)S(1)}, f32[2,4]{1,0:T(2,128)}, u32[]{:S(2)}) copy-start(f32[2,4]{1,0:T(2,128)} %wave.1) | copy-start | bytes 100
  19.2 19.9 %collective-permute-start.6 = (f32[1728,128]{1,0:T(8,128)S(1)}, f32[1728,128]{1,0:T(8,128)S(1)}, u32[]{:S(2)}, u32[]{:S(2)}) collective-permute-start(f32[1728,128]{1,0:T(8,128)S(1)} %get-tuple-element.53), channel_id=1, source_target_pairs={{0,16},{32,48},{64,80},{96,112},{16,0},{48,32},{80,64},{112,96},{1... | collective-permute-start | bytes 2654216 | tf_op jit(solution)/shard_map/ppermute | solution.py:32
  19.3 19.9 %collective-permute-start.7 = (f32[1728,128]{1,0:T(8,128)S(1)}, f32[1728,128]{1,0:T(8,128)S(1)}, u32[]{:S(2)}, u32[]{:S(2)}) collective-permute-start(f32[1728,128]{1,0:T(8,128)S(1)} %get-tuple-element.54), channel_id=1, source_target_pairs={{16,32},{48,64},{80,96},{32,16},{64,48},{96,80},{17,33},{49,65},{8... | collective-permute-start | bytes 2654216 | tf_op jit(solution)/shard_map/ppermute | solution.py:32
  29.8 9.5 %copy-start.3 = (s32[4,16]{1,0:T(4,128)S(1)}, s32[4,16]{1,0:T(4,128)}, u32[]{:S(2)}) copy-start(s32[4,16]{1,0:T(4,128)} %owners.1) | copy-start | bytes 772
  29.8 9.5 %copy-start.4 = (s32[4,16]{1,0:T(4,128)S(1)}, s32[4,16]{1,0:T(4,128)}, u32[]{:S(2)}) copy-start(s32[4,16]{1,0:T(4,128)} %slots.1) | copy-start | bytes 772
  39.2 37.7 %copy-start.7 = (s32[1,64]{1,0:T(1,128)S(1)}, s32[1,64]{1,0:T(1,128)}, u32[]{:S(2)}) copy-start(s32[1,64]{1,0:T(1,128)} %rows.1) | copy-start | bytes 772
